TPU v7x, 512 devices: a whole 4x8x8 slice. The times are simulated.
512 devices in a mesh: cuts: 16 (over y, z_hi), slab: 32 (over x, z_lo, core).
Axes of the slice: x: 4, y: 8, z: 8 (z_hi: 2, z_lo: 4; z = z_hi * 4 + z_lo), core: 2. Of those that a mesh axis runs over, the one named last changes fastest.
Arguments:
- states: float32 [16, 64, 256, 128], P(None, 'slab', 'cuts'), may hold values from -4 to 4
- diffusivity: float32 [64, 256, 128], P('slab'), may hold values from 0.04 to 0.08
- coarse_gain: float32 [64, 256, 128], P('slab'), may hold values from 0.2 to 0.99
- read_block: int32 [16, 16, 2], replicated, may hold values from 0 to 63
- read_count: int32 [16, 16], replicated, may hold values from 0 to 2, as said below
Outputs:
- new_states: float32 [16, 64, 256, 128], P(None, 'slab', 'cuts')
- fetched_blocks: float32 [16, 16, 2, 64, 4, 128], P('cuts', None, None, 'slab')
Inputs may be any that keep to these rules, and one draw needn't show every extreme that they name: `read_block`: block ids count in units of 4 y rows. Slots of read_block at or beyond read_count[d, s] are not read. In every draw some slice d reads 2 blocks from every slice.
All inputs are finite; a program needn't handle non-finite values.
Results may differ from a plain program's by a relative error of at most 0.00002.
Values sent between devices are 32-bit elements; how exact they have to be, the bound alone decides.
No kernel may reach another device: no remote copies, remote signals or barrier semaphores. Data moves between devices by JAX's collectives and lax.ppermute only.
A program may use at most 64 MiB of HBM per device.

v0:
```python
import jax
import jax.numpy as jnp
from jax import lax
from jax.sharding import PartitionSpec as P

FINE = 8
BY = 4


courant = 0.45


def with_halo(block, sides, width):
    for axis, dim in sides:
        count = lax.axis_size(axis)
        forward = [(i, i + 1) for i in range(count - 1)]
        backward = [(target, source) for source, target in forward]
        low = lax.ppermute(
            lax.slice_in_dim(block, block.shape[dim] - width, None, axis=dim), axis, forward
        )
        high = lax.ppermute(lax.slice_in_dim(block, 0, width, axis=dim), axis, backward)
        block = jnp.concatenate([low, block, high], axis=dim)
    return block


def entering(value, axis, join, neutral):
    count, mine = (lax.axis_size(axis), lax.axis_index(axis))
    pieces = jax.tree.map(lambda part: lax.all_gather(part, axis), value)
    subtotal = jax.tree.map(
        lambda part, zero: jnp.full_like(part, 0) + jnp.asarray(zero, part.dtype), value, neutral
    )

    def turn(position, subtotal):
        longer = join(subtotal, jax.tree.map(lambda part: part[position], pieces))
        return jax.tree.map(lambda new, old: jnp.where(position < mine, new, old), longer, subtotal)

    return lax.fori_loop(0, count - 1, turn, subtotal)


def face_values(kappa_ext):
    face_z = 0.5 * (kappa_ext[1:] + kappa_ext[:-1])
    pad_y = jnp.pad(kappa_ext, ((0, 0), (1, 1), (0, 0)))
    face_y = 0.5 * (pad_y[:, 1:] + pad_y[:, :-1])
    pad_x = jnp.pad(kappa_ext, ((0, 0), (0, 0), (1, 1)))
    face_x = 0.5 * (pad_x[:, :, 1:] + pad_x[:, :, :-1])
    return (face_z, face_y, face_x)


def fine_step(field, face_z, face_y, face_x):
    centre = field[1:-1]
    upper_z = field[2:]
    lower_z = field[:-2]
    flux_sum = face_z[1:] * (upper_z - centre) + face_z[:-1] * (lower_z - centre)
    pad_y = jnp.pad(centre, ((0, 0), (1, 1), (0, 0)))
    faces_y = face_y[1:-1]
    flux_sum = (
        flux_sum
        + faces_y[:, 1:] * (pad_y[:, 2:] - centre)
        + faces_y[:, :-1] * (pad_y[:, :-2] - centre)
    )
    pad_x = jnp.pad(centre, ((0, 0), (0, 0), (1, 1)))
    faces_x = face_x[1:-1]
    flux_sum = (
        flux_sum
        + faces_x[:, :, 1:] * (pad_x[:, :, 2:] - centre)
        + faces_x[:, :, :-1] * (pad_x[:, :, :-2] - centre)
    )
    return centre + flux_sum - courant * (centre - lower_z)


def combine(earlier, later):
    return (earlier[0] * later[0], later[0] * earlier[1] + later[1])


def body(states, diffusivity, coarse_gain, read_block, read_count):
    position = lax.axis_index("cuts")
    layers = diffusivity.shape[0]
    y_rows = diffusivity.shape[1]
    slice_start = lax.all_to_all(states, "cuts", split_axis=0, concat_axis=2, tiled=True)[0]
    halo_depth = 1
    kappa_ext = with_halo(diffusivity, (("slab", 0),), halo_depth)
    face_z, face_y, face_x = face_values(kappa_ext)

    def single_step(step_index, current):
        padded = with_halo(current, (("slab", 0),), 1)
        return fine_step(padded, face_z, face_y, face_x)

    fine_end = lax.fori_loop(0, FINE, single_step, slice_start)
    difference = fine_end - coarse_gain * slice_start
    blocks = fine_end.reshape(layers, y_rows // BY, BY, fine_end.shape[2]).transpose(1, 0, 2, 3)
    wanted_blocks = lax.dynamic_index_in_dim(read_block, position, 1, keepdims=False)
    counts = lax.dynamic_index_in_dim(read_count, position, 1, keepdims=False)
    picked = jnp.take(blocks, wanted_blocks, axis=0)
    live_slot = jnp.arange(read_block.shape[2], dtype=jnp.int32)[None, :] < counts[:, None]
    picked = jnp.where(live_slot[:, :, None, None, None], picked, 0.0)
    received = lax.all_to_all(picked, "cuts", split_axis=0, concat_axis=0, tiled=True)
    fetched_blocks = received[None]
    leading = position == 0
    factor = jnp.where(leading, 0.0, coarse_gain)
    offset = jnp.where(leading, difference + coarse_gain * slice_start, difference)
    identity = (jnp.ones_like(factor), jnp.zeros_like(offset))
    prefix_pair = entering((factor, offset), "cuts", combine, identity)
    newest = factor * prefix_pair[1] + offset
    new_states = lax.all_to_all(newest[None], "cuts", split_axis=2, concat_axis=0, tiled=True)
    return (new_states, fetched_blocks)


def solution(mesh):
    placed = (P(None, "slab", "cuts", None), P("slab", None, None), P("slab", None, None), P(), P())
    return jax.shard_map(
        body,
        mesh=mesh,
        in_specs=placed,
        out_specs=(P(None, "slab", "cuts", None), P("cuts", None, None, "slab", None, None)),
        check_vma=False,
    )
```

profile of v0, /device:TPU:1, one launch (start us, length us, event | category | flops | bytes accessed | tf_op | source)
XLA Modules:
  0.0 440.5 jit_solution(2078087062163330457)
XLA Ops:
  8.2 5.4 %collective-permute-start.3 = (f32[1,256,128]{2,1,0:T(8,128)S(1)}, f32[1,256,128]{2,1,0:T(8,128)S(1)}, u32[]{:S(2)}, u32[]{:S(2)}) collective-permute-start(f32[1,256,128]{2,1,0:T(8,128)S(1)} %get-tuple-element.209), channel_id=1, source_target_pairs={{0,1},{1,2},{2,3},{3,4},{4,5},{5,6},{6,7},{7,8},{8,9},{9,10},{10,1... | collective-permute-start | bytes 393224 | tf_op jit(solution)/shard_map/ppermute | solution.py:18
  13.6 14.5 %all-to-all-start = ((f32[16,2,16,128]{3,2,1,0:T(8,128)}), f32[16,2,16,128]{3,2,1,0:T(8,128)S(1)}, u32[]{:S(2)}, u32[]{:S(2)}) async-start(f32[16,2,16,128]{3,2,1,0:T(8,128)} %param.9), calls=%async_computation | async-start | bytes 524288 | tf_op jit(solution)/shard_map/all_to_all | solution.py:79
  28.1 1.9 collective-permute-start.2
  31.0 4.3 collective-permute-done.2
  36.9 7.1 %all-to-all-done = f32[16,2,16,128]{3,2,1,0:T(8,128)S(1)} async-done(((f32[16,2,16,128]{3,2,1,0:T(8,128)}), f32[16,2,16,128]{3,2,1,0:T(8,128)S(1)}, u32[]{:S(2)}, u32[]{:S(2)}) %all-to-all-start) | async-done | bytes 262176 | tf_op jit(solution)/shard_map/all_to_all | solution.py:79
  44.1 86.2 %while.26 = (s32[]{:T(128)}, f32[2,256,128]{2,1,0:T(8,128)S(1)}, f32[3,256,128]{2,1,0:T(8,128)S(1)}, f32[4,257,128]{2,1,0:T(8,128)S(1)}, f32[4,256,129]{2,1,0:T(8,128)S(1)}, /*index=5*/s32[]{:T(128)}) while((s32[]{:T(128)}, f32[2,256,128]{2,1,0:T(8,128)S(1)}, f32[3,256,128]{2,1,0:T(8,128)S(1)}, f32[4,257,128]{2,1,0:T(8,128)S(1)}, ...), condition=%wide.region_1.2_spmd, body=%wide.region_0.1_spmd.sunk | while | flops 1507330 | bytes 4456597 | solution.py:88
  44.2 3.1 collective-permute-start
  47.3 1.9 collective-permute-start.1
  49.2 4.9 %collective-permute-done.1 = f32[1,256,128]{2,1,0:T(8,128)S(1)} collective-permute-done((f32[1,256,128]{2,1,0:T(8,128)S(1)}, f32[1,256,128]{2,1,0:T(8,128)S(1)}, u32[]{:S(2)}, u32[]{:S(2)}) %collective-permute-start.1) | collective-permute-done | bytes 131104 | tf_op jit(solution)/shard_map/while/body/eval_jaxpr/ppermute | solution.py:21
  54.5 1.9 collective-permute-start
  56.4 2.4 collective-permute-start.1
  58.9 4.0 collective-permute-done.1
  63.2 1.9 collective-permute-start
  65.1 2.4 collective-permute-start.1
  67.5 4.4 %collective-permute-done.1 = f32[1,256,128]{2,1,0:T(8,128)S(1)} collective-permute-done((f32[1,256,128]{2,1,0:T(8,128)S(1)}, f32[1,256,128]{2,1,0:T(8,128)S(1)}, u32[]{:S(2)}, u32[]{:S(2)}) %collective-permute-start.1) | collective-permute-done | bytes 131104 | tf_op jit(solution)/shard_map/while/body/eval_jaxpr/ppermute | solution.py:21
  74.3 2.4 collective-permute-start.1
  76.7 6.4 %collective-permute-done.1 = f32[1,256,128]{2,1,0:T(8,128)S(1)} collective-permute-done((f32[1,256,128]{2,1,0:T(8,128)S(1)}, f32[1,256,128]{2,1,0:T(8,128)S(1)}, u32[]{:S(2)}, u32[]{:S(2)}) %collective-permute-start.1) | collective-permute-done | bytes 131104 | tf_op jit(solution)/shard_map/while/body/eval_jaxpr/ppermute | solution.py:21
  83.4 1.9 collective-permute-start
  85.3 2.4 collective-permute-start.1
  87.8 5.3 %collective-permute-done.1 = f32[1,256,128]{2,1,0:T(8,128)S(1)} collective-permute-done((f32[1,256,128]{2,1,0:T(8,128)S(1)}, f32[1,256,128]{2,1,0:T(8,128)S(1)}, u32[]{:S(2)}, u32[]{:S(2)}) %collective-permute-start.1) | collective-permute-done | bytes 131104 | tf_op jit(solution)/shard_map/while/body/eval_jaxpr/ppermute | solution.py:21
  95.3 2.4 collective-permute-start.1
  97.7 8.6 %collective-permute-done.1 = f32[1,256,128]{2,1,0:T(8,128)S(1)} collective-permute-done((f32[1,256,128]{2,1,0:T(8,128)S(1)}, f32[1,256,128]{2,1,0:T(8,128)S(1)}, u32[]{:S(2)}, u32[]{:S(2)}) %collective-permute-start.1) | collective-permute-done | bytes 131104 | tf_op jit(solution)/shard_map/while/body/eval_jaxpr/ppermute | solution.py:21
  108.7 2.4 collective-permute-start.1
  111.1 4.9 %collective-permute-done.1 = f32[1,256,128]{2,1,0:T(8,128)S(1)} collective-permute-done((f32[1,256,128]{2,1,0:T(8,128)S(1)}, f32[1,256,128]{2,1,0:T(8,128)S(1)}, u32[]{:S(2)}, u32[]{:S(2)}) %collective-permute-start.1) | collective-permute-done | bytes 131104 | tf_op jit(solution)/shard_map/while/body/eval_jaxpr/ppermute | solution.py:21
  118.2 2.4 collective-permute-start.1
  120.7 9.3 %collective-permute-done.1 = f32[1,256,128]{2,1,0:T(8,128)S(1)} collective-permute-done((f32[1,256,128]{2,1,0:T(8,128)S(1)}, f32[1,256,128]{2,1,0:T(8,128)S(1)}, u32[]{:S(2)}, u32[]{:S(2)}) %collective-permute-start.1) | collective-permute-done | bytes 131104 | tf_op jit(solution)/shard_map/while/body/eval_jaxpr/ppermute | solution.py:21
  134.2 5.8 %all-to-all-start.2 = ((f32[16,2,2,4,128]{4,3,2,1,0:T(4,128)}), f32[16,2,2,4,128]{4,3,2,1,0:T(4,128)S(1)}, u32[]{:S(2)}, u32[]{:S(2)}) async-start(f32[16,2,2,4,128]{4,3,2,1,0:T(4,128)} %select_select_fusion), calls=%async_computation.2 | async-start | bytes 262144 | tf_op jit(solution)/shard_map/all_to_all | solution.py:96
  140.0 123.8 %all-gather.5.cloned.1.call-done = f32[32,256,128]{2,1,0:T(8,128)} async-done(((f32[2,256,128]{2,1,0:T(8,128)}), f32[32,256,128]{2,1,0:T(8,128)}) %all-gather.5.cloned.1.call-update) | async-done | bytes 4194320 | tf_op jit(solution)/shard_map/all_gather | solution.py:28
  263.8 130.4 %all-gather.7.cloned.1.call-done = f32[32,256,128]{2,1,0:T(8,128)} async-done(((f32[2,256,128]{2,1,0:T(8,128)}), f32[32,256,128]{2,1,0:T(8,128)}) %all-gather.7.cloned.1.call-update) | async-done | bytes 4194320 | tf_op jit(solution)/shard_map/all_gather | solution.py:28
  394.1 19.1 %while.27 = (s32[]{:T(128)}, f32[2,256,128]{2,1,0:T(8,128)S(1)}, s32[]{:T(128)}, f32[16,2,256,128]{3,2,1,0:T(8,128)}, f32[16,2,256,128]{3,2,1,0:T(8,128)}, /*index=5*/s32[]{:T(128)}, s32[]{:T(128)}) while((s32[]{:T(128)}, f32[2,256,128]{2,1,0:T(8,128)S(1)}, s32[]{:T(128)}, f32[16,2,256,128]{3,2,1,0:T(8,128)}, ...), condition=%wide.region_3.4_spmd.clone, body=%wide.region_2.3_spmd.clone.sunk | while | flops 262148 | bytes 1048685 | solution.py:37
  414.2 4.4 all-to-all-start.1
  418.6 13.7 %all-to-all-done.1 = f32[1,2,256,128]{3,1,0,2:T(2,128)S(1)} async-done(((f32[1,2,256,128]{3,1,0,2:T(2,128)}), f32[1,2,256,128]{3,1,0,2:T(2,128)S(1)}, u32[]{:S(2)}, u32[]{:S(2)}) %all-to-all-start.1) | async-done | bytes 262176 | tf_op jit(solution)/shard_map/all_to_all | solution.py:104
  (95 shorter events, 38.8 us)
Async XLA Ops:
  7.2 124.8 %copy-start = (s32[16,16,2]{1,2,0:T(2,128)S(1)}, s32[16,16,2]{1,2,0:T(2,128)}, u32[]{:S(2)}) copy-start(s32[16,16,2]{1,2,0:T(2,128)} %param.12) | copy-start | bytes 6148
  8.2 21.9 %collective-permute-start.3 = (f32[1,256,128]{2,1,0:T(8,128)S(1)}, f32[1,256,128]{2,1,0:T(8,128)S(1)}, u32[]{:S(2)}, u32[]{:S(2)}) collective-permute-start(f32[1,256,128]{2,1,0:T(8,128)S(1)} %get-tuple-element.209), channel_id=1, source_target_pairs={{0,1},{1,2},{2,3},{3,4},{4,5},{5,6},{6,7},{7,8},{8,9},{9,10},{10,1... | collective-permute-start | bytes 393224 | tf_op jit(solution)/shard_map/ppermute | solution.py:18
  13.6 30.5 %all-to-all-start = ((f32[16,2,16,128]{3,2,1,0:T(8,128)}), f32[16,2,16,128]{3,2,1,0:T(8,128)S(1)}, u32[]{:S(2)}, u32[]{:S(2)}) async-start(f32[16,2,16,128]{3,2,1,0:T(8,128)} %param.9), calls=%async_computation | async-start | bytes 524288 | tf_op jit(solution)/shard_map/all_to_all | solution.py:79
  28.1 235.7 %all-gather.5.cloned.1.call-start = ((), (), s32[]{:S(2)}) async-start(), calls=%async_computation.3 | async-start | bytes 4456448 | tf_op jit(solution)/shard_map/all_gather | solution.py:28
  28.1 7.3 %collective-permute-start.2 = (f32[1,256,128]{2,1,0:T(8,128)S(1)}, f32[1,256,128]{2,1,0:T(8,128)S(1)}, u32[]{:S(2)}, u32[]{:S(2)}) collective-permute-start(f32[1,256,128]{2,1,0:T(8,128)S(1)} %get-tuple-element.210), channel_id=1, source_target_pairs={{1,0},{2,1},{3,2},{4,3},{5,4},{6,5},{7,6},{8,7},{9,8},{10,9},{11,1... | collective-permute-start | bytes 393224 | tf_op jit(solution)/shard_map/ppermute | solution.py:21
  44.1 86.2 %copy-start.3 = (f32[2,256,128]{2,1,0:T(8,128)S(1)}, f32[2,256,128]{2,1,0:T(8,128)}, u32[]{:S(2)}) copy-start(f32[2,256,128]{2,1,0:T(8,128)} %param.11) | copy-start | bytes 786436
  44.1 88.3 %copy-start.4 = (s32[16,16]{1,0:T(8,128)S(1)}, s32[16,16]{1,0:T(8,128)}, u32[]{:S(2)}) copy-start(s32[16,16]{1,0:T(8,128)} %param.13) | copy-start | bytes 3076
  44.2 5.0 %collective-permute-start = (f32[1,256,128]{2,1,0:T(8,128)S(1)}, f32[1,256,128]{2,1,0:T(8,128)S(1)}, u32[]{:S(2)}, u32[]{:S(2)}) collective-permute-start(f32[1,256,128]{2,1,0:T(8,128)S(1)} %get-tuple-element.270), channel_id=1, source_target_pairs={{0,1},{1,2},{2,3},{3,4},{4,5},{5,6},{6,7},{7,8},{8,9},{9,10},{10,1... | collective-permute-start | bytes 393224 | tf_op jit(solution)/shard_map/while/body/eval_jaxpr/ppermute | solution.py:18
  47.3 6.9 %collective-permute-start.1 = (f32[1,256,128]{2,1,0:T(8,128)S(1)}, f32[1,256,128]{2,1,0:T(8,128)S(1)}, u32[]{:S(2)}, u32[]{:S(2)}) collective-permute-start(f32[1,256,128]{2,1,0:T(8,128)S(1)} %get-tuple-element.271), channel_id=1, source_target_pairs={{1,0},{2,1},{3,2},{4,3},{5,4},{6,5},{7,6},{8,7},{9,8},{10,9},{11,1... | collective-permute-start | bytes 393224 | tf_op jit(solution)/shard_map/while/body/eval_jaxpr/ppermute | solution.py:21
  54.5 4.3 collective-permute-start
  56.4 6.4 %collective-permute-start.1 = (f32[1,256,128]{2,1,0:T(8,128)S(1)}, f32[1,256,128]{2,1,0:T(8,128)S(1)}, u32[]{:S(2)}, u32[]{:S(2)}) collective-permute-start(f32[1,256,128]{2,1,0:T(8,128)S(1)} %get-tuple-element.271), channel_id=1, source_target_pairs={{1,0},{2,1},{3,2},{4,3},{5,4},{6,5},{7,6},{8,7},{9,8},{10,9},{11,1... | collective-permute-start | bytes 393224 | tf_op jit(solution)/shard_map/while/body/eval_jaxpr/ppermute | solution.py:21
  63.2 4.3 collective-permute-start
  65.1 6.8 %collective-permute-start.1 = (f32[1,256,128]{2,1,0:T(8,128)S(1)}, f32[1,256,128]{2,1,0:T(8,128)S(1)}, u32[]{:S(2)}, u32[]{:S(2)}) collective-permute-start(f32[1,256,128]{2,1,0:T(8,128)S(1)} %get-tuple-element.271), channel_id=1, source_target_pairs={{1,0},{2,1},{3,2},{4,3},{5,4},{6,5},{7,6},{8,7},{9,8},{10,9},{11,1... | collective-permute-start | bytes 393224 | tf_op jit(solution)/shard_map/while/body/eval_jaxpr/ppermute | solution.py:21
  72.3 4.3 collective-permute-start
  74.3 8.8 %collective-permute-start.1 = (f32[1,256,128]{2,1,0:T(8,128)S(1)}, f32[1,256,128]{2,1,0:T(8,128)S(1)}, u32[]{:S(2)}, u32[]{:S(2)}) collective-permute-start(f32[1,256,128]{2,1,0:T(8,128)S(1)} %get-tuple-element.271), channel_id=1, source_target_pairs={{1,0},{2,1},{3,2},{4,3},{5,4},{6,5},{7,6},{8,7},{9,8},{10,9},{11,1... | collective-permute-start | bytes 393224 | tf_op jit(solution)/shard_map/while/body/eval_jaxpr/ppermute | solution.py:21
  83.4 4.3 collective-permute-start
  85.3 7.7 %collective-permute-start.1 = (f32[1,256,128]{2,1,0:T(8,128)S(1)}, f32[1,256,128]{2,1,0:T(8,128)S(1)}, u32[]{:S(2)}, u32[]{:S(2)}) collective-permute-start(f32[1,256,128]{2,1,0:T(8,128)S(1)} %get-tuple-element.271), channel_id=1, source_target_pairs={{1,0},{2,1},{3,2},{4,3},{5,4},{6,5},{7,6},{8,7},{9,8},{10,9},{11,1... | collective-permute-start | bytes 393224 | tf_op jit(solution)/shard_map/while/body/eval_jaxpr/ppermute | solution.py:21
  93.4 4.3 collective-permute-start
  95.3 11.1 %collective-permute-start.1 = (f32[1,256,128]{2,1,0:T(8,128)S(1)}, f32[1,256,128]{2,1,0:T(8,128)S(1)}, u32[]{:S(2)}, u32[]{:S(2)}) collective-permute-start(f32[1,256,128]{2,1,0:T(8,128)S(1)} %get-tuple-element.271), channel_id=1, source_target_pairs={{1,0},{2,1},{3,2},{4,3},{5,4},{6,5},{7,6},{8,7},{9,8},{10,9},{11,1... | collective-permute-start | bytes 393224 | tf_op jit(solution)/shard_map/while/body/eval_jaxpr/ppermute | solution.py:21
  106.7 4.3 collective-permute-start
  108.7 7.3 %collective-permute-start.1 = (f32[1,256,128]{2,1,0:T(8,128)S(1)}, f32[1,256,128]{2,1,0:T(8,128)S(1)}, u32[]{:S(2)}, u32[]{:S(2)}) collective-permute-start(f32[1,256,128]{2,1,0:T(8,128)S(1)} %get-tuple-element.271), channel_id=1, source_target_pairs={{1,0},{2,1},{3,2},{4,3},{5,4},{6,5},{7,6},{8,7},{9,8},{10,9},{11,1... | collective-permute-start | bytes 393224 | tf_op jit(solution)/shard_map/while/body/eval_jaxpr/ppermute | solution.py:21
  116.3 4.3 collective-permute-start
  118.2 11.8 %collective-permute-start.1 = (f32[1,256,128]{2,1,0:T(8,128)S(1)}, f32[1,256,128]{2,1,0:T(8,128)S(1)}, u32[]{:S(2)}, u32[]{:S(2)}) collective-permute-start(f32[1,256,128]{2,1,0:T(8,128)S(1)} %get-tuple-element.271), channel_id=1, source_target_pairs={{1,0},{2,1},{3,2},{4,3},{5,4},{6,5},{7,6},{8,7},{9,8},{10,9},{11,1... | collective-permute-start | bytes 393224 | tf_op jit(solution)/shard_map/while/body/eval_jaxpr/ppermute | solution.py:21
  131.2 282.0 %copy-start.1 = (f32[2,256,128]{2,1,0:T(8,128)S(1)}, f32[2,256,128]{2,1,0:T(8,128)}, u32[]{:S(2)}) copy-start(f32[2,256,128]{2,1,0:T(8,128)} %get-tuple-element.207) | copy-start | bytes 786436
  131.2 282.0 %copy-start.2 = (f32[2,256,128]{2,1,0:T(8,128)S(1)}, f32[2,256,128]{2,1,0:T(8,128)}, u32[]{:S(2)}) copy-start(f32[2,256,128]{2,1,0:T(8,128)} %get-tuple-element.208) | copy-start | bytes 786436
  131.2 262.9 %all-gather.7.cloned.1.call-start = ((), (), s32[]{:S(2)}) async-start(), calls=%async_computation.4 | async-start | bytes 4456448 | tf_op jit(solution)/shard_map/all_gather | solution.py:28
  134.2 280.0 %all-to-all-start.2 = ((f32[16,2,2,4,128]{4,3,2,1,0:T(4,128)}), f32[16,2,2,4,128]{4,3,2,1,0:T(4,128)S(1)}, u32[]{:S(2)}, u32[]{:S(2)}) async-start(f32[16,2,2,4,128]{4,3,2,1,0:T(4,128)} %select_select_fusion), calls=%async_computation.2 | async-start | bytes 262144 | tf_op jit(solution)/shard_map/all_to_all | solution.py:96
  414.2 18.1 %all-to-all-start.1 = ((f32[1,2,256,128]{3,1,0,2:T(2,128)}), f32[1,2,256,128]{3,1,0,2:T(2,128)S(1)}, u32[]{:S(2)}, u32[]{:S(2)}) async-start(f32[1,2,256,128]{3,1,0,2:T(2,128)} %copy.19), calls=%async_computation.1 | async-start | bytes 524288 | tf_op jit(solution)/shard_map/all_to_all | solution.py:104
Sparse Core Ops, SparseCore 0:
  131.3 132.3 all-gather.4
  267.0 127.1 all-gather.6
where the time goes:
time: 445 us; the launch traced here: 441 us
  waiting for transfers between devices  328 us (74%)
  starting transfers between devices  67.4 us (15%)
  other arithmetic  24.4 us (5%)
  between operations  14.3 us (3%)
  local copies, waits for them, and re-layouts  5.96 us (1%)
    all_gather x2, waiting for transfers between devices, entering(): pieces = jax.tree.map(lambda part: lax.all_gather(part, axis), value)  254 us
    ppermute x9, waiting for transfers between devices, with_halo(): lax.ppermute(lax.slice_in_dim(block, 0, width, axis=dim), axis, backward)  52.1 us
    ppermute x9, starting transfers between devices, with_halo(): lax.ppermute(lax.slice_in_dim(block, block.shape[dim] - width, None, axis...  21.9 us
    ppermute x9, starting transfers between devices, with_halo(): lax.ppermute(lax.slice_in_dim(block, 0, width, axis=dim), axis, backward)  20.7 us
    select_n x15, other arithmetic, turn(): jnp.where(position < mine, new, old)  18.7 us
    all_to_all x1, starting transfers between devices, body(): lax.all_to_all(states, 'cuts', split_axis=0, concat_axis=2, tiled=True)[0]  14.5 us
    all_to_all x1, waiting for transfers between devices, body(): lax.all_to_all(newest[None], 'cuts', split_axis=2, concat_axis=0, tiled=T...  13.7 us
  transfers between devices with their start and end apart: 23, of which 13 were waited for; matrix products, arithmetic and copies ran while one was open for 6% of the time, Pallas kernels for 0%

commit v1 on v0

v1 whole, which is shorter than its diff:
```python
import functools

import jax
import jax.numpy as jnp
from jax import lax
from jax.experimental import pallas as pl
from jax.experimental.pallas import tpu as pltpu
from jax.sharding import Mesh
from jax.sharding import PartitionSpec as P

FINE = 8
BY = 4
COURANT = 0.45

RING = ("zh", "zl", "c")
NEAR = ("zl", "c")
SLAB = ("x", "zl", "c")
CUTS = ("y", "zh")

VMEM = pl.BlockSpec(memory_space=pltpu.VMEM)
SMEM = pl.BlockSpec(memory_space=pltpu.SMEM)
PARAMS = pltpu.CompilerParams(vmem_limit_bytes=40 * 2**20)


def fine_kernel(
    edge, own, low, high, kappa_in, out, u, kappa, c0, zp, zm, yp, ym, xp, xm
):
    depth, rows, lanes = u.shape

    def place(layer, first, second):
        u[layer, 8:24] = first[0:16]
        u[layer, 40:48] = first[16:24]
        u[layer, 24:40] = second[0:16]
        u[layer, 0:8] = second[16:24]

    for j in range(8):
        for k in range(2):
            place(8 + 2 * j + k, own[0, j, k], own[1, j, k])
            kappa[8 + 2 * j + k] = kappa_in[j, 0, k]
            if j >= 4:
                kappa[2 * (j - 4) + k] = kappa_in[j, 1, k]
            else:
                kappa[24 + 2 * j + k] = kappa_in[j, 1, k]
    for j in range(4):
        for k in range(2):
            place(2 * j + k, low[0, j, k], low[1, j, k])
            place(24 + 2 * j + k, high[0, j, k], high[1, j, k])

    row = lax.broadcasted_iota(jnp.int32, (rows, lanes), 0)
    lane = lax.broadcasted_iota(jnp.int32, (rows, lanes), 1)
    inside_y = jnp.where(
        row < 8, edge[0], jnp.where(row >= rows - 8, edge[1], 1)
    ).astype(jnp.float32)
    not_first = jnp.where(lane == 0, 0.0, 1.0)
    not_last = jnp.where(lane == lanes - 1, 0.0, 1.0)

    def coefficients(z, _):
        inside_z = jnp.where(z < 8, edge[2], jnp.where(z >= depth - 8, edge[3], 1))
        mask = inside_y * inside_z.astype(jnp.float32)
        here = kappa[z]
        up = 0.5 * (here + kappa[z + 1])
        down = 0.5 * (here + kappa[z - 1])
        north = 0.5 * (here + pltpu.roll(here, rows - 1, 0))
        south = 0.5 * (here + pltpu.roll(here, 1, 0))
        east = 0.5 * (here + pltpu.roll(here, lanes - 1, 1) * not_last)
        west = 0.5 * (here + pltpu.roll(here, 1, 1) * not_first)
        total = ((up + down) + (north + south)) + (east + west)
        c0[z] = ((1.0 - COURANT) - total) * mask
        zp[z] = up * mask
        zm[z] = (down + COURANT) * mask
        yp[z] = north * mask
        ym[z] = south * mask
        xp[z] = east * (mask * not_last)
        xm[z] = west * (mask * not_first)
        return 0

    lax.fori_loop(1, depth - 1, coefficients, 0)

    for step in range(1, FINE + 1):
        last = step == FINE

        def layer(z, carry):
            below, here = carry
            above = u[z + 1]
            new = (
                (c0[z] * here + zp[z] * above)
                + (zm[z] * below + yp[z] * pltpu.roll(here, rows - 1, 0))
                + (
                    ym[z] * pltpu.roll(here, 1, 0)
                    + xp[z] * pltpu.roll(here, lanes - 1, 1)
                )
                + xm[z] * pltpu.roll(here, 1, 1)
            )
            if last:
                out[z - 8] = new[8 : rows - 8]
            else:
                u[z] = new
            return here, above

        lax.fori_loop(step, depth - step, layer, (u[step - 1], u[step]), unroll=2)


def pick_kernel(blocks, counts, me, tiles, out):
    slices = out.shape[0]
    upper = lax.broadcasted_iota(jnp.int32, out.shape[2:], 0) >= BY
    for d in range(slices):
        count = counts[d * slices + me[0]]
        first = blocks[(d * slices + me[0]) * 2]
        second = blocks[(d * slices + me[0]) * 2 + 1]
        for k in range(2):
            def half(block, slot):
                start = pl.multiple_of(((block >> 1) & 3) * 8, 8)
                tile = tiles[(block >> 3) & 7, k, pl.ds(start, 8), :]
                turned = pltpu.roll(tile, BY, 0)
                fits = jnp.where((block & 1) == slot, 1, 0)
                live = jnp.where(slot < count, 1, 0)
                chosen = jnp.where(jnp.full(tile.shape, fits) == 1, tile, turned)
                return jnp.where(jnp.full(tile.shape, live) == 1, chosen, 0.0)

            out[d, k] = jnp.where(upper, half(second, 1), half(first, 0))


def pack_kernel(fine, picked, out):
    for h in range(2):
        for q in range(8):
            out[h, q, :, 0:16] = fine[2 * q : 2 * q + 2, 16 * h : 16 * h + 16]
            out[h, q, :, 16:24] = picked[q, h]


def advance_kernel(received, states, gain, new_states, fetched):
    factor = gain[...]
    carried = states[0]
    for s in range(received.shape[0]):
        fine = received[s, :, 0:16]
        change = fine - factor * states[s]
        carried = factor * carried + change
        new_states[s] = carried
        tile = received[s, :, 16:24]
        fetched[s, 0] = tile[:, 0:4]
        fetched[s, 1] = tile[:, 4:8]


def exchange(value, axes):
    return lax.all_to_all(value, axes, 0, 0, tiled=True)


def body(states, diffusivity, coarse_gain, read_block, read_count):
    f32 = jnp.float32
    slices, thick, own_rows, lanes = states.shape
    y, zh, x = lax.axis_index("y"), lax.axis_index("zh"), lax.axis_index("x")
    zl = lax.axis_index("zl")
    ny, nx = lax.axis_size("y"), lax.axis_size("x")
    me = lax.axis_index(RING)
    cut = lax.axis_index(CUTS)
    tile_rows = 2 * own_rows
    wide = tile_rows + 2 * FINE
    half = slices // 2

    edge_rows = jnp.where(zh == 1, states[:, :, own_rows - FINE :], states[:, :, :FINE])
    pairs = [(i, i + 2) for i in range(1, 2 * ny - 2, 2)]
    pairs += [(i, i - 2) for i in range(2, 2 * ny, 2)]
    side_rows = lax.ppermute(edge_rows, CUTS, pairs)

    padded = jnp.pad(diffusivity, ((0, 0), (FINE, FINE), (0, 0)))
    kappa = lax.dynamic_slice_in_dim(padded, y * tile_rows, wide, 1)
    near = [((i, j), (i + 1, j)) for i in range(nx - 1) for j in (2, 3)]
    near += [((i, j), (i - 1, j)) for i in range(1, nx) for j in (0, 1)]
    flat = [(a * 4 + b, c * 4 + d) for (a, b), (c, d) in near]
    side_kappa = lax.ppermute(kappa, ("x", "zl"), flat)

    block = jnp.concatenate([states, side_rows], axis=2)
    own = exchange(block, RING).reshape(2, half, thick, own_rows + FINE, lanes)
    kappas = lax.all_gather(jnp.stack([kappa, side_kappa]), NEAR)

    up = [(i, i + 1) for i in range(nx - 1)]
    down = [(i + 1, i) for i in range(nx - 1)]
    low = lax.ppermute(own[:, half // 2 :], "x", up)
    high = lax.ppermute(own[:, : half // 2], "x", down)

    edge = jnp.stack([y > 0, y < ny - 1, x > 0, x < nx - 1]).astype(jnp.int32)
    deep = half * thick
    region = (deep + 2 * FINE, wide, lanes)
    fine = pl.pallas_call(
        fine_kernel,
        out_shape=jax.ShapeDtypeStruct((deep, tile_rows, lanes), f32),
        in_specs=[SMEM, VMEM, VMEM, VMEM, VMEM],
        out_specs=VMEM,
        scratch_shapes=[pltpu.VMEM(region, f32)] * 9,
        compiler_params=PARAMS,
        name="fine",
    )(edge, own, low, high, kappas)

    tiles = exchange(fine.reshape(ny, deep // ny, tile_rows, lanes), "y")
    picked = pl.pallas_call(
        pick_kernel,
        out_shape=jax.ShapeDtypeStruct((slices, thick, 2 * BY, lanes), f32),
        in_specs=[SMEM, SMEM, SMEM, VMEM],
        out_specs=VMEM,
        compiler_params=PARAMS,
        name="pick",
    )(read_block.reshape(-1), read_count.reshape(-1), me[None], tiles)
    picked = exchange(picked, "y").reshape(ny, 2, thick, 2 * BY, lanes)
    payload = pl.pallas_call(
        pack_kernel,
        out_shape=jax.ShapeDtypeStruct(
            (2, half, thick, own_rows + 2 * BY, lanes), f32
        ),
        in_specs=[VMEM, VMEM],
        out_specs=VMEM,
        compiler_params=PARAMS,
        name="pack",
    )(fine, picked)
    received = exchange(
        payload.reshape(slices, thick, own_rows + 2 * BY, lanes), RING
    )
    gain = lax.dynamic_slice_in_dim(coarse_gain, cut * own_rows, own_rows, 1)
    new_states, fetched = pl.pallas_call(
        advance_kernel,
        out_shape=(
            jax.ShapeDtypeStruct(states.shape, f32),
            jax.ShapeDtypeStruct((slices, 2, thick, BY, lanes), f32),
        ),
        in_specs=[VMEM, VMEM, VMEM],
        out_specs=(VMEM, VMEM),
        compiler_params=PARAMS,
        name="advance",
    )(received, states, gain)
    return new_states, fetched[None]


def solution(mesh):
    grid = Mesh(mesh.devices.reshape(8, 2, 4, 4, 2), ("y", "zh", "x", "zl", "c"))
    placed = (P(None, SLAB, CUTS, None), P(SLAB, None, None), P(SLAB, None, None), P(), P())
    return jax.shard_map(
        body,
        mesh=grid,
        in_specs=placed,
        out_specs=(P(None, SLAB, CUTS, None), P(CUTS, None, None, SLAB, None, None)),
        check_vma=False,
    )
```

time: 445 us -> 124 us (0.28)
  waiting for transfers between devices: 328 us -> 44 us
  starting transfers between devices: 67.4 us -> 33.2 us
  blocking collectives: 0 us -> 26 us
  other arithmetic: 24.4 us -> 1.91 us
  Pallas kernels: 0 us -> 15.8 us
  between operations: 14.3 us -> 0.76 us
  local copies, waits for them, and re-layouts: 5.96 us -> 1.03 us
    all_gather x2 -> x0, waiting for transfers between devices: 254 us -> none  [entering(): pieces = jax.tree.map(lambda part: lax.all_gather(part, axis), value)]
    ppermute x18 -> x4, waiting for transfers between devices: 52.1 us -> 8.83 us  [the longest x1 5.08 us: body(): side_rows = lax.ppermute(edge_rows, CUTS, pairs)]
    ppermute x18 -> x4, starting transfers between devices: 42.6 us -> 7 us  [the longest x1 3.13 us: body(): low = lax.ppermute(own[:, half // 2:], 'x', up)]
    select_n x18 -> x1, other arithmetic: 20.4 us -> 1.04 us  [body(): jnp.where(zh == 1, states[:, :, own_rows - FINE:], states[:, :, :FINE])]
    pallas_call x0 -> x4, Pallas kernels: none -> 15.8 us  [the longest x1 12.6 us: body(): pl.pallas_call(fine_kernel, out_shape=jax.ShapeDtypeStruct((deep, tile_ro...]
    all_gather x0 -> x1, blocking collectives: none -> 15.6 us  [body(): kappas = lax.all_gather(jnp.stack([kappa, side_kappa]), NEAR)]
    all_to_all x3, waiting for transfers between devices: 20.8 us -> 35.2 us  [exchange(): return lax.all_to_all(value, axes, 0, 0, tiled=True)]
    all_to_all x0 -> x1, blocking collectives: none -> 10.4 us  [exchange(): return lax.all_to_all(value, axes, 0, 0, tiled=True)]
  transfers between devices with their start and end apart: 23 -> 7, of which waited for: 13 -> 5; matrix products, arithmetic and copies ran while one was open for 6% -> 0% of each run, Pallas kernels for 0% -> 0%
where the time goes in v1:
time: 124 us; the launch traced here: 123 us
  waiting for transfers between devices  44 us (35%)
  starting transfers between devices  33.2 us (27%)
  blocking collectives  26 us (21%)
  Pallas kernels  15.8 us (13%)
  other arithmetic  1.91 us (2%)
    all_to_all x3, waiting for transfers between devices, exchange(): return lax.all_to_all(value, axes, 0, 0, tiled=True)  35.2 us
    all_to_all x3, starting transfers between devices, exchange(): return lax.all_to_all(value, axes, 0, 0, tiled=True)  26.2 us
    all_gather x1, blocking collectives, body(): kappas = lax.all_gather(jnp.stack([kappa, side_kappa]), NEAR)  15.6 us
    pallas_call x1, Pallas kernels, body(): pl.pallas_call(fine_kernel, out_shape=jax.ShapeDtypeStruct((deep, tile_ro...  12.6 us
    all_to_all x1, blocking collectives, exchange(): return lax.all_to_all(value, axes, 0, 0, tiled=True)  10.4 us
    ppermute x1, waiting for transfers between devices, body(): side_rows = lax.ppermute(edge_rows, CUTS, pairs)  5.08 us
    ppermute x1, waiting for transfers between devices, body(): side_kappa = lax.ppermute(kappa, ('x', 'zl'), flat)  3.74 us
    ppermute x1, starting transfers between devices, body(): low = lax.ppermute(own[:, half // 2:], 'x', up)  3.13 us
  transfers between devices with their start and end apart: 7, of which 5 were waited for; matrix products, arithmetic and copies ran while one was open for 0% of the time, Pallas kernels for 0%

profile of v1, /device:TPU:1, one launch (start us, length us, event | category | flops | bytes accessed | tf_op | source)
XLA Modules:
  0.0 122.8 jit_solution(13845051152281988789)
XLA Ops:
  0.6 0.0 copy-start
  0.6 0.0 copy-start.1
  0.7 1.0 slice_select_fusion
  1.7 1.3 %collective-permute-start = (f32[16,2,8,128]{3,2,1,0:T(8,128)S(1)}, f32[16,2,8,128]{3,2,1,0:T(8,128)S(1)}, u32[]{:S(2)}, u32[]{:S(2)}) collective-permute-start(f32[16,2,8,128]{3,2,1,0:T(8,128)S(1)} %slice_select_fusion), channel_id=1, source_target_pairs={{32,96},{96,160},{160,224},{224,288},{288,352},{352,416},{416,480}... | collective-permute-start | bytes 393224 | tf_op jit(solution)/shard_map/ppermute | solution.py:162
  3.0 5.1 %collective-permute-done = f32[16,2,8,128]{3,2,1,0:T(8,128)S(1)} collective-permute-done((f32[16,2,8,128]{3,2,1,0:T(8,128)S(1)}, f32[16,2,8,128]{3,2,1,0:T(8,128)S(1)}, u32[]{:S(2)}, u32[]{:S(2)}) %collective-permute-start) | collective-permute-done | bytes 131104 | tf_op jit(solution)/shard_map/ppermute | solution.py:162
  8.1 0.0 copy-done.1
  8.1 0.8 pad_maximum_fusion
  8.9 11.8 %all-to-all-start = ((f32[16,2,24,128]{3,2,1,0:T(8,128)}), f32[16,2,24,128]{3,2,1,0:T(8,128)S(1)}, u32[]{:S(2)}, u32[]{:S(2)}) async-start(f32[16,2,24,128]{3,2,1,0:T(8,128)} %pad_maximum_fusion), calls=%async_computation | async-start | bytes 786432 | tf_op jit(solution)/shard_map/all_to_all | solution.py:144
  20.7 0.0 copy-done.2
  20.7 1.3 %collective-permute-start.3 = (f32[2,48,128]{2,1,0:T(8,128)S(1)}, f32[2,48,128]{2,1,0:T(8,128)S(1)}, u32[]{:S(2)}, u32[]{:S(2)}) collective-permute-start(f32[2,48,128]{2,1,0:T(8,128)S(1)} %pad_dynamic-slice_fusion), channel_id=1, source_target_pairs={{4,12},{6,14},{12,20},{14,22},{20,28},{22,30},{8,0},{10,2},{16,8},... | collective-permute-start | bytes 147464 | tf_op jit(solution)/shard_map/ppermute | solution.py:169
  22.0 0.1 add_convert_fusion.edge
  22.1 3.7 %collective-permute-done.3 = f32[2,48,128]{2,1,0:T(8,128)S(1)} collective-permute-done((f32[2,48,128]{2,1,0:T(8,128)S(1)}, f32[2,48,128]{2,1,0:T(8,128)S(1)}, u32[]{:S(2)}, u32[]{:S(2)}) %collective-permute-start.3) | collective-permute-done | bytes 49184 | tf_op jit(solution)/shard_map/ppermute | solution.py:169
  25.9 9.4 %all-to-all-done = f32[16,2,24,128]{3,2,1,0:T(8,128)S(1)} async-done(((f32[16,2,24,128]{3,2,1,0:T(8,128)}), f32[16,2,24,128]{3,2,1,0:T(8,128)S(1)}, u32[]{:S(2)}, u32[]{:S(2)}) %all-to-all-start) | async-done | bytes 393248 | tf_op jit(solution)/shard_map/all_to_all | solution.py:144
  35.3 3.1 %collective-permute-start.1 = (f32[2,4,2,24,128]{4,3,2,1,0:T(8,128)S(1)}, f32[2,4,2,24,128]{4,3,2,1,0:T(8,128)S(1)}, u32[]{:S(2)}, u32[]{:S(2)}) collective-permute-start(f32[2,4,2,24,128]{4,3,2,1,0:T(8,128)S(1)} %get-tuple-element.7), channel_id=1, source_target_pairs={{0,8},{8,16},{16,24},{1,9},{9,17},{17,25},{2,10},{10,18},{18,26},{... | collective-permute-start | bytes 589832 | tf_op jit(solution)/shard_map/ppermute | solution.py:177
  38.4 1.3 %collective-permute-start.2 = (f32[2,4,2,24,128]{4,3,2,1,0:T(8,128)S(1)}, f32[2,4,2,24,128]{4,3,2,1,0:T(8,128)S(1)}, u32[]{:S(2)}, u32[]{:S(2)}) collective-permute-start(f32[2,4,2,24,128]{4,3,2,1,0:T(8,128)S(1)} %get-tuple-element.6), channel_id=1, source_target_pairs={{8,0},{16,8},{24,16},{9,1},{17,9},{25,17},{10,2},{18,10},{26,18},{... | collective-permute-start | bytes 589832 | tf_op jit(solution)/shard_map/ppermute | solution.py:178
  39.7 15.6 %all-gather = f32[16,2,48,128]{3,2,1,0:T(8,128)S(1)} all-gather(f32[2,2,48,128]{3,2,1,0:T(8,128)S(1)} %pad_maximum_fusion.1), channel_id=2, replica_groups=mesh['y'=8,'zh'=2,'x'=4,'zl'=4,'c'=2] {'zl','c'}, dimensions={0}, use_global_device_ids=true | all-gather | bytes 884736 | tf_op jit(solution)/shard_map/all_gather | solution.py:173
  55.3 0.0 collective-permute-done.1.low
  55.3 0.0 collective-permute-done.2.high
  55.3 12.6 %fine.1 = f32[16,32,128]{2,1,0:T(8,128)} custom-call(s32[4]{0:T(128)S(1)} %add_convert_fusion.edge, f32[2,8,2,24,128]{4,3,2,1,0:T(8,128)S(1)} %bitcast.15, f32[2,4,2,24,128]{4,3,2,1,0:T(8,128)S(1)} %collective-permute-done.1.low, f32[2,4,2,24,128]{4,3,2,1,0:T(8,128)S(1)} %collective-permute-done.2.high, f32[8,2,2,48,128]{4,3,2,1,0:T(8,128)S(1)} %bitcast.16), custom_call_target="tpu_custom_call" | custom-call | tf_op jit(solution)/shard_map/fine/pallas_call | solution.py:183
  67.9 9.1 %all-to-all-start.1 = ((f32[8,2,32,128]{3,2,1,0:T(8,128)}), f32[8,2,32,128]{3,2,1,0:T(8,128)S(1)}, u32[]{:S(2)}, u32[]{:S(2)}) async-start(f32[8,2,32,128]{3,2,1,0:T(8,128)} %bitcast.9), calls=%async_computation.1 | async-start | bytes 524288 | tf_op jit(solution)/shard_map/all_to_all | solution.py:144
  77.0 0.0 copy-done.3
  77.0 0.2 copy.8
  77.2 0.1 reshape.23.blocks
  77.3 0.6 copy-done.4
  77.8 0.1 reshape.24.counts
  77.9 11.3 %all-to-all-done.1.tiles = f32[8,2,32,128]{3,2,1,0:T(8,128)S(1)} async-done(((f32[8,2,32,128]{3,2,1,0:T(8,128)}), f32[8,2,32,128]{3,2,1,0:T(8,128)S(1)}, u32[]{:S(2)}, u32[]{:S(2)}) %all-to-all-start.1) | async-done | bytes 262176 | tf_op jit(solution)/shard_map/all_to_all | solution.py:144
  89.2 0.7 pick.1
  90.0 10.4 %all_to_all.20 = f32[16,2,8,128]{3,2,1,0:T(8,128)S(1)} all-to-all(f32[16,2,8,128]{3,2,1,0:T(8,128)S(1)} %pick.1), channel_id=1, replica_groups=mesh['y'=8,'zh'=2,'x'=4,'zl'=4,'c'=2] {'y'}, dimensions={0} | all-to-all | bytes 262144 | tf_op jit(solution)/shard_map/all_to_all | solution.py:144
  100.4 1.7 %pack.1 = f32[2,8,2,24,128]{4,3,2,1,0:T(8,128)} custom-call(f32[16,32,128]{2,1,0:T(8,128)} %fine.1, f32[8,2,2,8,128]{4,3,2,1,0:T(8,128)S(1)} %bitcast.17), custom_call_target="tpu_custom_call" | custom-call | tf_op jit(solution)/shard_map/pack/pallas_call | solution.py:203
  102.1 5.3 %all-to-all-start.3 = ((f32[16,2,24,128]{3,2,1,0:T(8,128)}), f32[16,2,24,128]{3,2,1,0:T(8,128)S(1)}, u32[]{:S(2)}, u32[]{:S(2)}) async-start(f32[16,2,24,128]{3,2,1,0:T(8,128)} %bitcast.11), calls=%async_computation.3 | async-start | bytes 786432 | tf_op jit(solution)/shard_map/all_to_all | solution.py:144
  107.5 14.5 %all-to-all-done.3.received = f32[16,2,24,128]{3,2,1,0:T(8,128)S(1)} async-done(((f32[16,2,24,128]{3,2,1,0:T(8,128)}), f32[16,2,24,128]{3,2,1,0:T(8,128)S(1)}, u32[]{:S(2)}, u32[]{:S(2)}) %all-to-all-start.3) | async-done | bytes 393248 | tf_op jit(solution)/shard_map/all_to_all | solution.py:144
  122.0 0.8 advance.1
  (9 shorter events, 0.1 us)
Async XLA Ops:
  0.6 106.8 %copy-start = (f32[2,256,128]{2,1,0:T(8,128)S(1)}, f32[2,256,128]{2,1,0:T(8,128)}, u32[]{:S(2)}) copy-start(f32[2,256,128]{2,1,0:T(8,128)} %param.7) | copy-start | bytes 786436
  0.6 7.4 %copy-start.1 = (f32[16,2,16,128]{3,2,1,0:T(8,128)S(1)}, f32[16,2,16,128]{3,2,1,0:T(8,128)}, u32[]{:S(2)}) copy-start(f32[16,2,16,128]{3,2,1,0:T(8,128)} %states.1) | copy-start | bytes 786436
  1.7 6.4 %collective-permute-start = (f32[16,2,8,128]{3,2,1,0:T(8,128)S(1)}, f32[16,2,8,128]{3,2,1,0:T(8,128)S(1)}, u32[]{:S(2)}, u32[]{:S(2)}) collective-permute-start(f32[16,2,8,128]{3,2,1,0:T(8,128)S(1)} %slice_select_fusion), channel_id=1, source_target_pairs={{32,96},{96,160},{160,224},{224,288},{288,352},{352,416},{416,480}... | collective-permute-start | bytes 393224 | tf_op jit(solution)/shard_map/ppermute | solution.py:162
  8.9 11.8 %copy-start.2 = (f32[2,256,128]{2,1,0:T(8,128)S(1)}, f32[2,256,128]{2,1,0:T(8,128)}, u32[]{:S(2)}) copy-start(f32[2,256,128]{2,1,0:T(8,128)} %param.6) | copy-start | bytes 786436
  8.9 26.4 %all-to-all-start = ((f32[16,2,24,128]{3,2,1,0:T(8,128)}), f32[16,2,24,128]{3,2,1,0:T(8,128)S(1)}, u32[]{:S(2)}, u32[]{:S(2)}) async-start(f32[16,2,24,128]{3,2,1,0:T(8,128)} %pad_maximum_fusion), calls=%async_computation | async-start | bytes 786432 | tf_op jit(solution)/shard_map/all_to_all | solution.py:144
  20.7 5.2 %collective-permute-start.3 = (f32[2,48,128]{2,1,0:T(8,128)S(1)}, f32[2,48,128]{2,1,0:T(8,128)S(1)}, u32[]{:S(2)}, u32[]{:S(2)}) collective-permute-start(f32[2,48,128]{2,1,0:T(8,128)S(1)} %pad_dynamic-slice_fusion), channel_id=1, source_target_pairs={{4,12},{6,14},{12,20},{14,22},{20,28},{22,30},{8,0},{10,2},{16,8},... | collective-permute-start | bytes 147464 | tf_op jit(solution)/shard_map/ppermute | solution.py:169
  35.3 20.0 %collective-permute-start.1 = (f32[2,4,2,24,128]{4,3,2,1,0:T(8,128)S(1)}, f32[2,4,2,24,128]{4,3,2,1,0:T(8,128)S(1)}, u32[]{:S(2)}, u32[]{:S(2)}) collective-permute-start(f32[2,4,2,24,128]{4,3,2,1,0:T(8,128)S(1)} %get-tuple-element.7), channel_id=1, source_target_pairs={{0,8},{8,16},{16,24},{1,9},{9,17},{17,25},{2,10},{10,18},{18,26},{... | collective-permute-start | bytes 589832 | tf_op jit(solution)/shard_map/ppermute | solution.py:177
  38.4 16.9 %collective-permute-start.2 = (f32[2,4,2,24,128]{4,3,2,1,0:T(8,128)S(1)}, f32[2,4,2,24,128]{4,3,2,1,0:T(8,128)S(1)}, u32[]{:S(2)}, u32[]{:S(2)}) collective-permute-start(f32[2,4,2,24,128]{4,3,2,1,0:T(8,128)S(1)} %get-tuple-element.6), channel_id=1, source_target_pairs={{8,0},{16,8},{24,16},{9,1},{17,9},{25,17},{10,2},{18,10},{26,18},{... | collective-permute-start | bytes 589832 | tf_op jit(solution)/shard_map/ppermute | solution.py:178
  67.9 9.1 %copy-start.3 = (s32[16,16,2]{1,2,0:T(2,128)S(1)}, s32[16,16,2]{1,2,0:T(2,128)}, u32[]{:S(2)}) copy-start(s32[16,16,2]{1,2,0:T(2,128)} %param.8) | copy-start | bytes 6148
  67.9 21.3 %all-to-all-start.1 = ((f32[8,2,32,128]{3,2,1,0:T(8,128)}), f32[8,2,32,128]{3,2,1,0:T(8,128)S(1)}, u32[]{:S(2)}, u32[]{:S(2)}) async-start(f32[8,2,32,128]{3,2,1,0:T(8,128)} %bitcast.9), calls=%async_computation.1 | async-start | bytes 524288 | tf_op jit(solution)/shard_map/all_to_all | solution.py:144
  77.2 0.7 copy-start.4
  102.1 19.9 %all-to-all-start.3 = ((f32[16,2,24,128]{3,2,1,0:T(8,128)}), f32[16,2,24,128]{3,2,1,0:T(8,128)S(1)}, u32[]{:S(2)}, u32[]{:S(2)}) async-start(f32[16,2,24,128]{3,2,1,0:T(8,128)} %bitcast.11), calls=%async_computation.3 | async-start | bytes 786432 | tf_op jit(solution)/shard_map/all_to_all | solution.py:144

commit v2 on v1

v2 whole, which is shorter than its diff:
```python
import jax
import jax.numpy as jnp
from jax import lax
from jax.experimental import pallas as pl
from jax.experimental.pallas import tpu as pltpu
from jax.sharding import Mesh
from jax.sharding import PartitionSpec as P

FINE = 8
BY = 4
COURANT = 0.45

RING = ("zh", "zl", "c")
SLAB = ("x", "zl", "c")
CUTS = ("y", "zh")

VMEM = pl.BlockSpec(memory_space=pltpu.VMEM)
SMEM = pl.BlockSpec(memory_space=pltpu.SMEM)
PARAMS = pltpu.CompilerParams(vmem_limit_bytes=40 * 2**20)


def join_kernel(own, south, north, first, second):
    for out, start in ((first, 0), (second, 4)):
        for j in range(4):
            for k in range(2):
                layer = 2 * j + k
                out[layer, 0:8] = south[start + j, k]
                out[layer, 8:24] = own[0, start + j, k]
                out[layer, 24:40] = own[1, start + j, k]
                out[layer, 40:48] = north[start + j, k]


def coefficient_kernel(edge, mine, other, c0, zp, zm, yp, ym, xp, xm, kappa):
    depth, rows, lanes = kappa.shape
    core = edge[4]
    for part, source in ((core, mine), (1 - core, other)):
        for j in range(4):
            side = 4 * (j - 2) if j >= 2 else 24 + 4 * j
            for k in range(2):
                kappa[8 + 4 * j + 2 * part + k] = source[j, 0, k]
                kappa[side + 2 * part + k] = source[j, 1, k]

    row = lax.broadcasted_iota(jnp.int32, (rows, lanes), 0)
    lane = lax.broadcasted_iota(jnp.int32, (rows, lanes), 1)
    inside = jnp.where(
        row < 8, edge[0], jnp.where(row >= rows - 8, edge[1], 1)
    ).astype(jnp.float32)
    below = inside * edge[2].astype(jnp.float32)
    above = inside * edge[3].astype(jnp.float32)
    not_first = jnp.where(lane == 0, 0.0, 1.0)
    not_last = jnp.where(lane == lanes - 1, 0.0, 1.0)
    for z in range(1, depth - 1):
        mask = below if z < 8 else above if z >= depth - 8 else inside
        here = kappa[z]
        up = 0.5 * (here + kappa[z + 1])
        down = 0.5 * (here + kappa[z - 1])
        north = 0.5 * (here + pltpu.roll(here, rows - 1, 0))
        south = 0.5 * (here + pltpu.roll(here, 1, 0))
        east = 0.5 * (here + pltpu.roll(here, lanes - 1, 1) * not_last)
        west = 0.5 * (here + pltpu.roll(here, 1, 1) * not_first)
        total = ((up + down) + (north + south)) + (east + west)
        c0[z] = ((1.0 - COURANT) - total) * mask
        zp[z] = up * mask
        zm[z] = (down + COURANT) * mask
        yp[z] = north * mask
        ym[z] = south * mask
        xp[z] = east * (mask * not_last)
        xm[z] = west * (mask * not_first)


def fine_kernel(low, first, second, high, c0, zp, zm, yp, ym, xp, xm, out, ends, u):
    depth, rows, lanes = u.shape
    parts = (low, first, second, high)
    for step in range(1, FINE + 1):
        at = (lambda z: parts[z // 8][z % 8]) if step == 1 else (lambda z: u[z])
        below, here = at(step - 1), at(step)
        for z in range(step, depth - step):
            above = at(z + 1)
            new = (
                (c0[z] * here + zp[z] * above)
                + (zm[z] * below + yp[z] * pltpu.roll(here, rows - 1, 0))
                + (
                    ym[z] * pltpu.roll(here, 1, 0)
                    + xp[z] * pltpu.roll(here, lanes - 1, 1)
                )
                + xm[z] * pltpu.roll(here, 1, 1)
            )
            if step < FINE:
                u[z] = new
            else:
                q, k = (z - 8) // 2, z % 2
                out[q, k] = new[8 : rows - 8]
                ends[0, q, k] = new[8:24]
                ends[1, q, k] = new[24:40]
            below, here = here, above


def pick_kernel(blocks, counts, me, tiles, out):
    slices = out.shape[0]
    upper = lax.broadcasted_iota(jnp.int32, out.shape[2:], 0) >= BY
    for d in range(slices):
        count = counts[d * slices + me[0]]
        first = blocks[(d * slices + me[0]) * 2]
        second = blocks[(d * slices + me[0]) * 2 + 1]
        for k in range(2):
            def half(block, slot):
                start = pl.multiple_of(((block >> 1) & 3) * 8, 8)
                tile = tiles[(block >> 3) & 7, k, pl.ds(start, 8), :]
                turned = pltpu.roll(tile, BY, 0)
                fits = jnp.where((block & 1) == slot, 1, 0)
                live = jnp.where(slot < count, 1, 0)
                chosen = jnp.where(jnp.full(tile.shape, fits) == 1, tile, turned)
                return jnp.where(jnp.full(tile.shape, live) == 1, chosen, 0.0)

            out[d, k] = jnp.where(upper, half(second, 1), half(first, 0))


def pack_kernel(ends, picked, out):
    for h in range(2):
        for q in range(8):
            out[h, q, :, 0:16] = ends[h, q]
            out[h, q, :, 16:24] = picked[q, h]


def advance_kernel(received, states, gain, new_states, fetched):
    factor = gain[...]
    carried = states[0]
    for s in range(received.shape[0]):
        fine = received[s, :, 0:16]
        change = fine - factor * states[s]
        carried = factor * carried + change
        new_states[s] = carried
        tile = received[s, :, 16:24]
        fetched[s, 0] = tile[:, 0:4]
        fetched[s, 1] = tile[:, 4:8]


def exchange(value, axes):
    return lax.all_to_all(value, axes, 0, 0, tiled=True)


def call(kernel, name, shapes, kinds, scratch=(), **more):
    outs = [jax.ShapeDtypeStruct(shape, jnp.float32) for shape in shapes]
    return pl.pallas_call(
        kernel,
        out_shape=outs,
        in_specs=kinds,
        out_specs=[VMEM] * len(outs),
        scratch_shapes=[pltpu.VMEM(shape, jnp.float32) for shape in scratch],
        compiler_params=PARAMS,
        name=name,
        **more,
    )


def body(states, diffusivity, coarse_gain, read_block, read_count):
    slices, thick, own_rows, lanes = states.shape
    y, x, c = lax.axis_index("y"), lax.axis_index("x"), lax.axis_index("c")
    ny, nx = lax.axis_size("y"), lax.axis_size("x")
    me = lax.axis_index(RING)
    cut = lax.axis_index(CUTS)
    tile_rows = 2 * own_rows
    wide = tile_rows + 2 * FINE
    half = slices // 2
    y_up = [(i, i + 1) for i in range(ny - 1)]
    y_down = [(i + 1, i) for i in range(ny - 1)]
    x_up = [(i, i + 1) for i in range(nx - 1)]
    x_down = [(i + 1, i) for i in range(nx - 1)]

    padded = jnp.pad(diffusivity, ((0, 0), (FINE, FINE), (0, 0)))
    kappa = lax.dynamic_slice_in_dim(padded, y * tile_rows, wide, 1)
    near = [((i, j), (i + 1, j)) for i in range(nx - 1) for j in (2, 3)]
    near += [((i, j), (i - 1, j)) for i in range(1, nx) for j in (0, 1)]
    flat = [(p * 4 + q, r * 4 + s) for (p, q), (r, s) in near]
    side_kappa = lax.ppermute(kappa, ("x", "zl"), flat)
    mine = lax.all_gather(jnp.stack([kappa, side_kappa]), "zl")

    own = exchange(states, RING).reshape(2, half, thick, own_rows, lanes)
    own, mine = lax.optimization_barrier((own, mine))
    other = lax.ppermute(mine, "c", [(0, 1), (1, 0)])
    south = lax.ppermute(own[1, :, :, own_rows - FINE :], "y", y_up)
    north = lax.ppermute(own[0, :, :, :FINE], "y", y_down)
    part = (FINE, wide, lanes)
    first, second = call(join_kernel, "join", [part] * 2, [VMEM] * 3)(own, south, north)
    low = lax.ppermute(second, "x", x_up)
    high = lax.ppermute(first, "x", x_down)

    edge = jnp.stack([y > 0, y < ny - 1, x > 0, x < nx - 1, c > 0]).astype(jnp.int32)
    deep = half * thick
    region = (deep + 2 * FINE, wide, lanes)
    coefficients = call(
        coefficient_kernel, "coefficients", [region] * 7, [SMEM, VMEM, VMEM], [region]
    )(edge, mine, other)
    fine, ends = call(
        fine_kernel,
        "fine",
        [(ny, deep // ny, tile_rows, lanes), (2, half, thick, own_rows, lanes)],
        [VMEM] * 11,
        [region],
    )(low, first, second, high, *coefficients)

    tiles = exchange(fine, "y")
    (picked,) = call(
        pick_kernel,
        "pick",
        [(slices, thick, 2 * BY, lanes)],
        [SMEM, SMEM, SMEM, VMEM],
    )(read_block.reshape(-1), read_count.reshape(-1), me[None], tiles)
    picked = exchange(picked, "y").reshape(ny, 2, thick, 2 * BY, lanes)
    (payload,) = call(
        pack_kernel, "pack", [(2, half, thick, own_rows + 2 * BY, lanes)], [VMEM] * 2
    )(ends, picked)
    received = exchange(
        payload.reshape(slices, thick, own_rows + 2 * BY, lanes), RING
    )
    gain = lax.dynamic_slice_in_dim(coarse_gain, cut * own_rows, own_rows, 1)
    new_states, fetched = call(
        advance_kernel,
        "advance",
        [states.shape, (slices, 2, thick, BY, lanes)],
        [VMEM] * 3,
    )(received, states, gain)
    return new_states, fetched[None]


def solution(mesh):
    grid = Mesh(mesh.devices.reshape(8, 2, 4, 4, 2), ("y", "zh", "x", "zl", "c"))
    placed = (P(None, SLAB, CUTS, None), P(SLAB, None, None), P(SLAB, None, None), P(), P())
    return jax.shard_map(
        body,
        mesh=grid,
        in_specs=placed,
        out_specs=(P(None, SLAB, CUTS, None), P(CUTS, None, None, SLAB, None, None)),
        check_vma=False,
    )
```

time: 124 us -> 114 us (0.919)
  starting transfers between devices: 33.2 us -> 46.8 us
  waiting for transfers between devices: 44 us -> 34.2 us
  Pallas kernels: 15.8 us -> 6.81 us
  blocking collectives: 26 us -> 23.4 us
  other arithmetic: 1.91 us -> 0.01 us
    all_to_all x3, waiting for transfers between devices: 35.2 us -> 23 us  [exchange(): return lax.all_to_all(value, axes, 0, 0, tiled=True)]
    pallas_call x4 -> x6, Pallas kernels: 15.8 us -> 6.81 us  [the longest x1 3.17 us: body(): call(fine_kernel, 'fine', [(ny, deep // ny, tile_rows, lanes), (2, half,...]
    ppermute x3 -> x5, starting transfers between devices: 5.71 us -> 13.7 us  [the longest x1 4.89 us: body(): other = lax.ppermute(mine, 'c', [(0, 1), (1, 0)])]
    all_to_all x3, starting transfers between devices: 26.2 us -> 31.8 us  [exchange(): return lax.all_to_all(value, axes, 0, 0, tiled=True)]
    all_gather x1, blocking collectives: 15.6 us -> 13.1 us  [body(): mine = lax.all_gather(jnp.stack([kappa, side_kappa]), 'zl')]
    ppermute x3 -> x5, waiting for transfers between devices: 5.09 us -> 7.35 us  [the longest x1 3.63 us: body(): high = lax.ppermute(first, 'x', x_down)]
  transfers between devices with their start and end apart: 7 -> 9, of which waited for: 5 -> 6; matrix products, arithmetic and copies ran while one was open for 0% -> 0% of each run, Pallas kernels for 0% -> 1%
where the time goes in v2:
time: 114 us; the launch traced here: 113 us
  starting transfers between devices  46.8 us (41%)
  waiting for transfers between devices  34.2 us (30%)
  blocking collectives  23.4 us (21%)
  Pallas kernels  6.81 us (6%)
    all_to_all x3, starting transfers between devices, exchange(): return lax.all_to_all(value, axes, 0, 0, tiled=True)  31.8 us
    all_to_all x3, waiting for transfers between devices, exchange(): return lax.all_to_all(value, axes, 0, 0, tiled=True)  23 us
    all_gather x1, blocking collectives, body(): mine = lax.all_gather(jnp.stack([kappa, side_kappa]), 'zl')  13.1 us
    all_to_all x1, blocking collectives, exchange(): return lax.all_to_all(value, axes, 0, 0, tiled=True)  10.3 us
    ppermute x1, starting transfers between devices, body(): other = lax.ppermute(mine, 'c', [(0, 1), (1, 0)])  4.89 us
    ppermute x1, waiting for transfers between devices, body(): side_kappa = lax.ppermute(kappa, ('x', 'zl'), flat)  3.83 us
    ppermute x1, waiting for transfers between devices, body(): high = lax.ppermute(first, 'x', x_down)  3.63 us
    ppermute x1, waiting for transfers between devices, body(): north = lax.ppermute(own[0, :, :, :FINE], 'y', y_down)  3.52 us
  transfers between devices with their start and end apart: 9, of which 6 were waited for; matrix products, arithmetic and copies ran while one was open for 0% of the time, Pallas kernels for 1%

profile of v2, /device:TPU:1, one launch (start us, length us, event | category | flops | bytes accessed | tf_op | source)
XLA Modules:
  0.0 113.1 jit_solution(11160487952935601753)
XLA Ops:
  0.6 0.0 copy-start
  0.6 0.0 copy-start.2
  0.7 12.0 %all-to-all-start = ((f32[16,2,16,128]{3,2,1,0:T(8,128)}), f32[16,2,16,128]{3,2,1,0:T(8,128)S(1)}, u32[]{:S(2)}, u32[]{:S(2)}) async-start(f32[16,2,16,128]{3,2,1,0:T(8,128)} %states.1), calls=%async_computation | async-start | bytes 524288 | tf_op jit(solution)/shard_map/all_to_all | solution.py:139
  12.7 1.3 %collective-permute-start = (f32[2,48,128]{2,1,0:T(8,128)S(1)}, f32[2,48,128]{2,1,0:T(8,128)S(1)}, u32[]{:S(2)}, u32[]{:S(2)}) collective-permute-start(f32[2,48,128]{2,1,0:T(8,128)S(1)} %pad_dynamic-slice_fusion), channel_id=1, source_target_pairs={{4,12},{6,14},{12,20},{14,22},{20,28},{22,30},{8,0},{10,2},{16,8},... | collective-permute-start | bytes 147464 | tf_op jit(solution)/shard_map/ppermute | solution.py:175
  14.0 3.8 %collective-permute-done = f32[2,48,128]{2,1,0:T(8,128)S(1)} collective-permute-done((f32[2,48,128]{2,1,0:T(8,128)S(1)}, f32[2,48,128]{2,1,0:T(8,128)S(1)}, u32[]{:S(2)}, u32[]{:S(2)}) %collective-permute-start) | collective-permute-done | bytes 49184 | tf_op jit(solution)/shard_map/ppermute | solution.py:175
  17.8 13.1 %all-gather = f32[8,2,48,128]{3,2,1,0:T(8,128)S(1)} all-gather(f32[2,2,48,128]{3,2,1,0:T(8,128)S(1)} %pad_maximum_fusion), channel_id=2, replica_groups=mesh['y'=8,'zh'=2,'x'=4,'zl'=4,'c'=2] {'zl'}, dimensions={0}, use_global_device_ids=true | all-gather | bytes 491520 | tf_op jit(solution)/shard_map/all_gather | solution.py:176
  30.9 0.0 all-to-all-done
  30.9 4.9 %collective-permute-start.5 = (f32[4,2,2,48,128]{4,3,2,1,0:T(8,128)S(1)}, f32[4,2,2,48,128]{4,3,2,1,0:T(8,128)S(1)}, u32[]{:S(2)}, u32[]{:S(2)}) collective-permute-start(f32[4,2,2,48,128]{4,3,2,1,0:T(8,128)S(1)} %bitcast.20), channel_id=1, source_target_pairs={{0,1},{1,0},{2,3},{3,2},{4,5},{5,4},{6,7},{7,6},{8,9},{9,8},{10,11... | collective-permute-start | bytes 1179656 | tf_op jit(solution)/shard_map/ppermute | solution.py:180
  35.8 3.2 %collective-permute-start.1 = (f32[8,2,8,128]{3,2,1,0:T(8,128)S(1)}, f32[8,2,8,128]{3,2,1,0:T(8,128)S(1)}, u32[]{:S(2)}, u32[]{:S(2)}) collective-permute-start(f32[8,2,8,128]{3,2,1,0:T(8,128)S(1)} %get-tuple-element.33), channel_id=1, source_target_pairs={{0,64},{64,128},{128,192},{192,256},{256,320},{320,384},{384,448},... | collective-permute-start | bytes 196616 | tf_op jit(solution)/shard_map/ppermute | solution.py:181
  39.0 1.3 %collective-permute-start.2 = (f32[8,2,8,128]{3,2,1,0:T(8,128)S(1)}, f32[8,2,8,128]{3,2,1,0:T(8,128)S(1)}, u32[]{:S(2)}, u32[]{:S(2)}) collective-permute-start(f32[8,2,8,128]{3,2,1,0:T(8,128)S(1)} %get-tuple-element.32), channel_id=1, source_target_pairs={{64,0},{128,64},{192,128},{256,192},{320,256},{384,320},{448,384},... | collective-permute-start | bytes 196616 | tf_op jit(solution)/shard_map/ppermute | solution.py:182
  40.3 0.2 collective-permute-done.1.south
  40.5 3.5 %collective-permute-done.2.north = f32[8,2,8,128]{3,2,1,0:T(8,128)S(1)} collective-permute-done((f32[8,2,8,128]{3,2,1,0:T(8,128)S(1)}, f32[8,2,8,128]{3,2,1,0:T(8,128)S(1)}, u32[]{:S(2)}, u32[]{:S(2)}) %collective-permute-start.2) | collective-permute-done | bytes 65568 | tf_op jit(solution)/shard_map/ppermute | solution.py:182
  44.1 3.0 %collective-permute-start.3 = (f32[8,48,128]{2,1,0:T(8,128)S(1)}, f32[8,48,128]{2,1,0:T(8,128)S(1)}, u32[]{:S(2)}, u32[]{:S(2)}) collective-permute-start(f32[8,48,128]{2,1,0:T(8,128)S(1)} %get-tuple-element.18.second), channel_id=1, source_target_pairs={{0,8},{8,16},{16,24},{1,9},{9,17},{17,25},{2,10},{10,18},{18,26},{... | collective-permute-start | bytes 589832 | tf_op jit(solution)/shard_map/ppermute | solution.py:185
  47.1 1.3 %collective-permute-start.4 = (f32[8,48,128]{2,1,0:T(8,128)S(1)}, f32[8,48,128]{2,1,0:T(8,128)S(1)}, u32[]{:S(2)}, u32[]{:S(2)}) collective-permute-start(f32[8,48,128]{2,1,0:T(8,128)S(1)} %get-tuple-element.19.first), channel_id=1, source_target_pairs={{8,0},{16,8},{24,16},{9,1},{17,9},{25,17},{10,2},{18,10},{26,18},{... | collective-permute-start | bytes 589832 | tf_op jit(solution)/shard_map/ppermute | solution.py:186
  48.4 0.1 stack.35
  48.5 0.0 collective-permute-done.5.other
  48.5 1.3 %coefficients.1 = (f32[32,48,128]{2,1,0:T(8,128)S(1)}, f32[32,48,128]{2,1,0:T(8,128)S(1)}, f32[32,48,128]{2,1,0:T(8,128)S(1)}, f32[32,48,128]{2,1,0:T(8,128)S(1)...) custom-call(s32[5]{0:T(128)S(1)} %convert_element_type.5.edge, ...), custom_call_target="tpu_custom_call" | custom-call | tf_op jit(solution)/shard_map/coefficients/pallas_call | solution.py:191
  49.9 0.0 collective-permute-done.3.low
  49.9 3.6 %collective-permute-done.4.high = f32[8,48,128]{2,1,0:T(8,128)S(1)} collective-permute-done((f32[8,48,128]{2,1,0:T(8,128)S(1)}, f32[8,48,128]{2,1,0:T(8,128)S(1)}, u32[]{:S(2)}, u32[]{:S(2)}) %collective-permute-start.4) | collective-permute-done | bytes 196640 | tf_op jit(solution)/shard_map/ppermute | solution.py:186
  53.5 3.2 %fine.1 = (f32[8,2,32,128]{3,2,1,0:T(8,128)}, f32[2,8,2,16,128]{4,3,2,1,0:T(8,128)S(1)}) custom-call(f32[8,48,128]{2,1,0:T(8,128)S(1)} %collective-permute-done.3.low, f32[8,48,128]{2,1,0:T(8,128)S(1)} %get-tuple-element.19.first, f32[8,48,128]{2,1,0:T(8,128)S(1)} %get-tuple-element.18.second, f32[8,48,128]{2,1,0:T(8,128)S(1)} %collective-permute-done.4.high, ...), custom_call_target="tpu_custom_call" | custom-call | tf_op jit(solution)/shard_map/fine/pallas_call | solution.py:194
  56.7 7.2 %all-to-all-start.1 = ((f32[8,2,32,128]{3,2,1,0:T(8,128)}), f32[8,2,32,128]{3,2,1,0:T(8,128)S(1)}, u32[]{:S(2)}, u32[]{:S(2)}) async-start(f32[8,2,32,128]{3,2,1,0:T(8,128)} %get-tuple-element.29), calls=%async_computation.1 | async-start | bytes 524288 | tf_op jit(solution)/shard_map/all_to_all | solution.py:139
  63.8 0.2 copy.8
  64.0 0.1 reshape.20.blocks
  64.2 0.6 copy-done.4
  64.7 0.1 reshape.21.counts
  64.8 8.5 %all-to-all-done.1.tiles = f32[8,2,32,128]{3,2,1,0:T(8,128)S(1)} async-done(((f32[8,2,32,128]{3,2,1,0:T(8,128)}), f32[8,2,32,128]{3,2,1,0:T(8,128)S(1)}, u32[]{:S(2)}, u32[]{:S(2)}) %all-to-all-start.1) | async-done | bytes 262176 | tf_op jit(solution)/shard_map/all_to_all | solution.py:139
  73.3 0.7 pick.1
  74.0 10.3 %all_to_all.20 = f32[16,2,8,128]{3,2,1,0:T(8,128)S(1)} all-to-all(f32[16,2,8,128]{3,2,1,0:T(8,128)S(1)} %pick.1), channel_id=1, replica_groups=mesh['y'=8,'zh'=2,'x'=4,'zl'=4,'c'=2] {'y'}, dimensions={0} | all-to-all | bytes 262144 | tf_op jit(solution)/shard_map/all_to_all | solution.py:139
  84.3 0.8 pack.1
  85.1 12.7 %all-to-all-start.3 = ((f32[16,2,24,128]{3,2,1,0:T(8,128)}), f32[16,2,24,128]{3,2,1,0:T(8,128)S(1)}, u32[]{:S(2)}, u32[]{:S(2)}) async-start(f32[16,2,24,128]{3,2,1,0:T(8,128)} %bitcast.13), calls=%async_computation.3 | async-start | bytes 786432 | tf_op jit(solution)/shard_map/all_to_all | solution.py:139
  97.8 14.5 %all-to-all-done.3.received = f32[16,2,24,128]{3,2,1,0:T(8,128)S(1)} async-done(((f32[16,2,24,128]{3,2,1,0:T(8,128)}), f32[16,2,24,128]{3,2,1,0:T(8,128)S(1)}, u32[]{:S(2)}, u32[]{:S(2)}) %all-to-all-start.3) | async-done | bytes 393248 | tf_op jit(solution)/shard_map/all_to_all | solution.py:139
  112.4 0.8 advance.1
  (14 shorter events, 0.1 us)
Async XLA Ops:
  0.6 97.2 %copy-start = (f32[2,256,128]{2,1,0:T(8,128)S(1)}, f32[2,256,128]{2,1,0:T(8,128)}, u32[]{:S(2)}) copy-start(f32[2,256,128]{2,1,0:T(8,128)} %param.7) | copy-start | bytes 786436
  0.6 12.0 %copy-start.2 = (f32[2,256,128]{2,1,0:T(8,128)S(1)}, f32[2,256,128]{2,1,0:T(8,128)}, u32[]{:S(2)}) copy-start(f32[2,256,128]{2,1,0:T(8,128)} %param.6) | copy-start | bytes 786436
  0.7 30.3 %all-to-all-start = ((f32[16,2,16,128]{3,2,1,0:T(8,128)}), f32[16,2,16,128]{3,2,1,0:T(8,128)S(1)}, u32[]{:S(2)}, u32[]{:S(2)}) async-start(f32[16,2,16,128]{3,2,1,0:T(8,128)} %states.1), calls=%async_computation | async-start | bytes 524288 | tf_op jit(solution)/shard_map/all_to_all | solution.py:139
  12.7 5.2 %collective-permute-start = (f32[2,48,128]{2,1,0:T(8,128)S(1)}, f32[2,48,128]{2,1,0:T(8,128)S(1)}, u32[]{:S(2)}, u32[]{:S(2)}) collective-permute-start(f32[2,48,128]{2,1,0:T(8,128)S(1)} %pad_dynamic-slice_fusion), channel_id=1, source_target_pairs={{4,12},{6,14},{12,20},{14,22},{20,28},{22,30},{8,0},{10,2},{16,8},... | collective-permute-start | bytes 147464 | tf_op jit(solution)/shard_map/ppermute | solution.py:175
  30.9 17.6 %collective-permute-start.5 = (f32[4,2,2,48,128]{4,3,2,1,0:T(8,128)S(1)}, f32[4,2,2,48,128]{4,3,2,1,0:T(8,128)S(1)}, u32[]{:S(2)}, u32[]{:S(2)}) collective-permute-start(f32[4,2,2,48,128]{4,3,2,1,0:T(8,128)S(1)} %bitcast.20), channel_id=1, source_target_pairs={{0,1},{1,0},{2,3},{3,2},{4,5},{5,4},{6,7},{7,6},{8,9},{9,8},{10,11... | collective-permute-start | bytes 1179656 | tf_op jit(solution)/shard_map/ppermute | solution.py:180
  35.8 4.7 %collective-permute-start.1 = (f32[8,2,8,128]{3,2,1,0:T(8,128)S(1)}, f32[8,2,8,128]{3,2,1,0:T(8,128)S(1)}, u32[]{:S(2)}, u32[]{:S(2)}) collective-permute-start(f32[8,2,8,128]{3,2,1,0:T(8,128)S(1)} %get-tuple-element.33), channel_id=1, source_target_pairs={{0,64},{64,128},{128,192},{192,256},{256,320},{320,384},{384,448},... | collective-permute-start | bytes 196616 | tf_op jit(solution)/shard_map/ppermute | solution.py:181
  39.0 5.0 %collective-permute-start.2 = (f32[8,2,8,128]{3,2,1,0:T(8,128)S(1)}, f32[8,2,8,128]{3,2,1,0:T(8,128)S(1)}, u32[]{:S(2)}, u32[]{:S(2)}) collective-permute-start(f32[8,2,8,128]{3,2,1,0:T(8,128)S(1)} %get-tuple-element.32), channel_id=1, source_target_pairs={{64,0},{128,64},{192,128},{256,192},{320,256},{384,320},{448,384},... | collective-permute-start | bytes 196616 | tf_op jit(solution)/shard_map/ppermute | solution.py:182
  44.1 5.8 %collective-permute-start.3 = (f32[8,48,128]{2,1,0:T(8,128)S(1)}, f32[8,48,128]{2,1,0:T(8,128)S(1)}, u32[]{:S(2)}, u32[]{:S(2)}) collective-permute-start(f32[8,48,128]{2,1,0:T(8,128)S(1)} %get-tuple-element.18.second), channel_id=1, source_target_pairs={{0,8},{8,16},{16,24},{1,9},{9,17},{17,25},{2,10},{10,18},{18,26},{... | collective-permute-start | bytes 589832 | tf_op jit(solution)/shard_map/ppermute | solution.py:185
  47.1 6.4 %collective-permute-start.4 = (f32[8,48,128]{2,1,0:T(8,128)S(1)}, f32[8,48,128]{2,1,0:T(8,128)S(1)}, u32[]{:S(2)}, u32[]{:S(2)}) collective-permute-start(f32[8,48,128]{2,1,0:T(8,128)S(1)} %get-tuple-element.19.first), channel_id=1, source_target_pairs={{8,0},{16,8},{24,16},{9,1},{17,9},{25,17},{10,2},{18,10},{26,18},{... | collective-permute-start | bytes 589832 | tf_op jit(solution)/shard_map/ppermute | solution.py:186
  56.7 7.2 %copy-start.3 = (s32[16,16,2]{1,2,0:T(2,128)S(1)}, s32[16,16,2]{1,2,0:T(2,128)}, u32[]{:S(2)}) copy-start(s32[16,16,2]{1,2,0:T(2,128)} %param.8) | copy-start | bytes 6148
  56.7 16.6 %all-to-all-start.1 = ((f32[8,2,32,128]{3,2,1,0:T(8,128)}), f32[8,2,32,128]{3,2,1,0:T(8,128)S(1)}, u32[]{:S(2)}, u32[]{:S(2)}) async-start(f32[8,2,32,128]{3,2,1,0:T(8,128)} %get-tuple-element.29), calls=%async_computation.1 | async-start | bytes 524288 | tf_op jit(solution)/shard_map/all_to_all | solution.py:139
  64.0 0.7 copy-start.4
  85.1 27.3 %copy-start.1 = (f32[16,2,16,128]{3,2,1,0:T(8,128)S(1)}, f32[16,2,16,128]{3,2,1,0:T(8,128)}, u32[]{:S(2)}) copy-start(f32[16,2,16,128]{3,2,1,0:T(8,128)} %states.1) | copy-start | bytes 786436
  85.1 27.3 %all-to-all-start.3 = ((f32[16,2,24,128]{3,2,1,0:T(8,128)}), f32[16,2,24,128]{3,2,1,0:T(8,128)S(1)}, u32[]{:S(2)}, u32[]{:S(2)}) async-start(f32[16,2,24,128]{3,2,1,0:T(8,128)} %bitcast.13), calls=%async_computation.3 | async-start | bytes 786432 | tf_op jit(solution)/shard_map/all_to_all | solution.py:139

commit v3 on v2

--- a/solution.py
+++ b/solution.py
@@ -13,6 +13,8 @@
 RING = ("zh", "zl", "c")
 SLAB = ("x", "zl", "c")
 CUTS = ("y", "zh")
+CHIPS = ("zh", "zl")
+RING_OFFSETS = (0, -1, 1, -2)
 
 VMEM = pl.BlockSpec(memory_space=pltpu.VMEM)
 SMEM = pl.BlockSpec(memory_space=pltpu.SMEM)
@@ -34,11 +36,12 @@
     depth, rows, lanes = kappa.shape
     core = edge[4]
     for part, source in ((core, mine), (1 - core, other)):
-        for j in range(4):
-            side = 4 * (j - 2) if j >= 2 else 24 + 4 * j
+        for i, offset in enumerate(RING_OFFSETS):
+            j = (edge[5] + offset) & 3
+            side = jnp.where(j >= 2, 4 * (j - 2), 24 + 4 * j)
             for k in range(2):
-                kappa[8 + 4 * j + 2 * part + k] = source[j, 0, k]
-                kappa[side + 2 * part + k] = source[j, 1, k]
+                kappa[8 + 4 * j + 2 * part + k] = source[i, 0, k]
+                kappa[side + 2 * part + k] = source[i, 1, k]
 
     row = lax.broadcasted_iota(jnp.int32, (rows, lanes), 0)
     lane = lax.broadcasted_iota(jnp.int32, (rows, lanes), 1)
@@ -173,10 +176,19 @@
     near += [((i, j), (i - 1, j)) for i in range(1, nx) for j in (0, 1)]
     flat = [(p * 4 + q, r * 4 + s) for (p, q), (r, s) in near]
     side_kappa = lax.ppermute(kappa, ("x", "zl"), flat)
-    mine = lax.all_gather(jnp.stack([kappa, side_kappa]), "zl")
+    pieces = jnp.stack([kappa, side_kappa])
+    around = lax.axis_size(CHIPS)
+    mine = jnp.stack(
+        [pieces]
+        + [
+            lax.ppermute(
+                pieces, CHIPS, [(i, (i - offset) % around) for i in range(around)]
+            )
+            for offset in RING_OFFSETS[1:]
+        ]
+    )
 
     own = exchange(states, RING).reshape(2, half, thick, own_rows, lanes)
-    own, mine = lax.optimization_barrier((own, mine))
     other = lax.ppermute(mine, "c", [(0, 1), (1, 0)])
     south = lax.ppermute(own[1, :, :, own_rows - FINE :], "y", y_up)
     north = lax.ppermute(own[0, :, :, :FINE], "y", y_down)
@@ -185,7 +197,8 @@
     low = lax.ppermute(second, "x", x_up)
     high = lax.ppermute(first, "x", x_down)
 
-    edge = jnp.stack([y > 0, y < ny - 1, x > 0, x < nx - 1, c > 0]).astype(jnp.int32)
+    flags = [y > 0, y < ny - 1, x > 0, x < nx - 1, c, lax.axis_index("zl")]
+    edge = jnp.stack([flag.astype(jnp.int32) for flag in flags])
     deep = half * thick
     region = (deep + 2 * FINE, wide, lanes)
     coefficients = call(

time: 114 us -> 114 us (level)
  blocking collectives: 23.4 us -> 10.3 us
  starting transfers between devices: 46.8 us -> 54.2 us
  waiting for transfers between devices: 34.2 us -> 40.5 us
    all_gather x1 -> x0, blocking collectives: 13.1 us -> none  [body(): mine = lax.all_gather(jnp.stack([kappa, side_kappa]), 'zl')]
    ppermute x0 -> x3, starting transfers between devices: none -> 8.6 us  [body(): lax.ppermute(pieces, CHIPS, [(i, (i - offset) % around) for i in range(ar...]
    ppermute x0 -> x3, waiting for transfers between devices: none -> 6.24 us  [body(): lax.ppermute(pieces, CHIPS, [(i, (i - offset) % around) for i in range(ar...]
    all_to_all x3, starting transfers between devices: 31.8 us -> 30.6 us  [exchange(): return lax.all_to_all(value, axes, 0, 0, tiled=True)]
  transfers between devices with their start and end apart: 9 -> 12, of which waited for: 6 -> 7; matrix products, arithmetic and copies ran while one was open for 0% -> 0% of each run, Pallas kernels for 1% -> 1%
where the time goes in v3:
time: 114 us
  starting transfers between devices  54.2 us (48%)
  waiting for transfers between devices  40.5 us (36%)
  blocking collectives  10.3 us (9%)
  Pallas kernels  6.8 us (6%)
    all_to_all x3, starting transfers between devices, exchange(): return lax.all_to_all(value, axes, 0, 0, tiled=True)  30.6 us
    all_to_all x3, waiting for transfers between devices, exchange(): return lax.all_to_all(value, axes, 0, 0, tiled=True)  23 us
    all_to_all x1, blocking collectives, exchange(): return lax.all_to_all(value, axes, 0, 0, tiled=True)  10.3 us
    ppermute x3, starting transfers between devices, body(): lax.ppermute(pieces, CHIPS, [(i, (i - offset) % around) for i in range(ar...  8.6 us
    ppermute x3, waiting for transfers between devices, body(): lax.ppermute(pieces, CHIPS, [(i, (i - offset) % around) for i in range(ar...  6.24 us
    ppermute x1, starting transfers between devices, body(): other = lax.ppermute(mine, 'c', [(0, 1), (1, 0)])  4.45 us
    ppermute x1, waiting for transfers between devices, body(): side_kappa = lax.ppermute(kappa, ('x', 'zl'), flat)  3.83 us
    ppermute x1, waiting for transfers between devices, body(): high = lax.ppermute(first, 'x', x_down)  3.65 us
  transfers between devices with their start and end apart: 12, of which 7 were waited for; matrix products, arithmetic and copies ran while one was open for 0% of the time, Pallas kernels for 1%

profile of v3, /device:TPU:1, one launch (start us, length us, event | category | flops | bytes accessed | tf_op | source)
XLA Modules:
  0.0 113.7 jit_solution(9304002907787318336)
XLA Ops:
  0.6 0.0 copy-start
  0.7 12.0 %all-to-all-start = ((f32[16,2,16,128]{3,2,1,0:T(8,128)}), f32[16,2,16,128]{3,2,1,0:T(8,128)S(1)}, u32[]{:S(2)}, u32[]{:S(2)}) async-start(f32[16,2,16,128]{3,2,1,0:T(8,128)} %states.1), calls=%async_computation | async-start | bytes 524288 | tf_op jit(solution)/shard_map/all_to_all | solution.py:142
  12.7 1.3 %collective-permute-start.4 = (f32[2,48,128]{2,1,0:T(8,128)S(1)}, f32[2,48,128]{2,1,0:T(8,128)S(1)}, u32[]{:S(2)}, u32[]{:S(2)}) collective-permute-start(f32[2,48,128]{2,1,0:T(8,128)S(1)} %pad_dynamic-slice_fusion), channel_id=1, source_target_pairs={{4,12},{6,14},{12,20},{14,22},{20,28},{22,30},{8,0},{10,2},{16,8},... | collective-permute-start | bytes 147464 | tf_op jit(solution)/shard_map/ppermute | solution.py:178
  14.0 3.8 %collective-permute-done.4 = f32[2,48,128]{2,1,0:T(8,128)S(1)} collective-permute-done((f32[2,48,128]{2,1,0:T(8,128)S(1)}, f32[2,48,128]{2,1,0:T(8,128)S(1)}, u32[]{:S(2)}, u32[]{:S(2)}) %collective-permute-start.4) | collective-permute-done | bytes 49184 | tf_op jit(solution)/shard_map/ppermute | solution.py:178
  17.8 3.3 %collective-permute-start.5 = (f32[2,2,48,128]{3,2,1,0:T(8,128)S(1)}, f32[2,2,48,128]{3,2,1,0:T(8,128)S(1)}, u32[]{:S(2)}, u32[]{:S(2)}) collective-permute-start(f32[2,2,48,128]{3,2,1,0:T(8,128)S(1)} %get-tuple-element.31), channel_id=1, source_target_pairs={{0,2},{2,4},{4,6},{6,32},{32,34},{34,36},{36,38},{38,0},{1,3},{3,5... | collective-permute-start | bytes 294920 | tf_op jit(solution)/shard_map/ppermute | solution.py:184
  21.1 3.2 %collective-permute-start.6 = (f32[2,2,48,128]{3,2,1,0:T(8,128)S(1)}, f32[2,2,48,128]{3,2,1,0:T(8,128)S(1)}, u32[]{:S(2)}, u32[]{:S(2)}) collective-permute-start(f32[2,2,48,128]{3,2,1,0:T(8,128)S(1)} %get-tuple-element.31), channel_id=1, source_target_pairs={{0,38},{2,0},{4,2},{6,4},{32,6},{34,32},{36,34},{38,36},{1,39},{3,... | collective-permute-start | bytes 294920 | tf_op jit(solution)/shard_map/ppermute | solution.py:184
  24.3 2.1 %collective-permute-start.7 = (f32[2,2,48,128]{3,2,1,0:T(8,128)S(1)}, f32[2,2,48,128]{3,2,1,0:T(8,128)S(1)}, u32[]{:S(2)}, u32[]{:S(2)}) collective-permute-start(f32[2,2,48,128]{3,2,1,0:T(8,128)S(1)} %get-tuple-element.31), channel_id=1, source_target_pairs={{0,4},{2,6},{4,32},{6,34},{32,36},{34,38},{36,0},{38,2},{1,5},{3,7... | collective-permute-start | bytes 294920 | tf_op jit(solution)/shard_map/ppermute | solution.py:184
  26.5 0.0 collective-permute-done.6
  26.5 6.2 %collective-permute-done.7 = f32[2,2,48,128]{3,2,1,0:T(8,128)S(1)} collective-permute-done((f32[2,2,48,128]{3,2,1,0:T(8,128)S(1)}, f32[2,2,48,128]{3,2,1,0:T(8,128)S(1)}, u32[]{:S(2)}, u32[]{:S(2)}) %collective-permute-start.7) | collective-permute-done | bytes 98336 | tf_op jit(solution)/shard_map/ppermute | solution.py:184
  32.7 4.5 %collective-permute-start.8 = (f32[4,2,2,48,128]{4,3,2,1,0:T(8,128)S(1)}, f32[4,2,2,48,128]{4,3,2,1,0:T(8,128)S(1)}, u32[]{:S(2)}, u32[]{:S(2)}) collective-permute-start(f32[4,2,2,48,128]{4,3,2,1,0:T(8,128)S(1)} %pad_maximum_fusion.mine), channel_id=1, source_target_pairs={{0,1},{1,0},{2,3},{3,2},{4,5},{5,4},{6,7},{7,6},{8,9},{9,8},{10,11... | collective-permute-start | bytes 1179656 | tf_op jit(solution)/shard_map/ppermute | solution.py:192
  37.2 3.2 %collective-permute-start = (f32[8,2,8,128]{3,2,1,0:T(8,128)S(1)}, f32[8,2,8,128]{3,2,1,0:T(8,128)S(1)}, u32[]{:S(2)}, u32[]{:S(2)}) collective-permute-start(f32[8,2,8,128]{3,2,1,0:T(8,128)S(1)} %get-tuple-element.29), channel_id=1, source_target_pairs={{0,64},{64,128},{128,192},{192,256},{256,320},{320,384},{384,448},... | collective-permute-start | bytes 196616 | tf_op jit(solution)/shard_map/ppermute | solution.py:193
  40.4 1.3 %collective-permute-start.1 = (f32[8,2,8,128]{3,2,1,0:T(8,128)S(1)}, f32[8,2,8,128]{3,2,1,0:T(8,128)S(1)}, u32[]{:S(2)}, u32[]{:S(2)}) collective-permute-start(f32[8,2,8,128]{3,2,1,0:T(8,128)S(1)} %get-tuple-element.28), channel_id=1, source_target_pairs={{64,0},{128,64},{192,128},{256,192},{320,256},{384,320},{448,384},... | collective-permute-start | bytes 196616 | tf_op jit(solution)/shard_map/ppermute | solution.py:194
  41.7 0.2 collective-permute-done.south
  41.9 3.5 %collective-permute-done.1.north = f32[8,2,8,128]{3,2,1,0:T(8,128)S(1)} collective-permute-done((f32[8,2,8,128]{3,2,1,0:T(8,128)S(1)}, f32[8,2,8,128]{3,2,1,0:T(8,128)S(1)}, u32[]{:S(2)}, u32[]{:S(2)}) %collective-permute-start.1) | collective-permute-done | bytes 65568 | tf_op jit(solution)/shard_map/ppermute | solution.py:194
  45.5 3.4 %collective-permute-start.2 = (f32[8,48,128]{2,1,0:T(8,128)S(1)}, f32[8,48,128]{2,1,0:T(8,128)S(1)}, u32[]{:S(2)}, u32[]{:S(2)}) collective-permute-start(f32[8,48,128]{2,1,0:T(8,128)S(1)} %get-tuple-element.15.second), channel_id=1, source_target_pairs={{0,8},{8,16},{16,24},{1,9},{9,17},{17,25},{2,10},{10,18},{18,26},{... | collective-permute-start | bytes 589832 | tf_op jit(solution)/shard_map/ppermute | solution.py:197
  48.9 1.3 %collective-permute-start.3 = (f32[8,48,128]{2,1,0:T(8,128)S(1)}, f32[8,48,128]{2,1,0:T(8,128)S(1)}, u32[]{:S(2)}, u32[]{:S(2)}) collective-permute-start(f32[8,48,128]{2,1,0:T(8,128)S(1)} %get-tuple-element.16.first), channel_id=1, source_target_pairs={{8,0},{16,8},{24,16},{9,1},{17,9},{25,17},{10,2},{18,10},{26,18},{... | collective-permute-start | bytes 589832 | tf_op jit(solution)/shard_map/ppermute | solution.py:198
  50.2 0.1 stack.67.edge
  50.3 1.3 %coefficients.1 = (f32[32,48,128]{2,1,0:T(8,128)S(1)}, f32[32,48,128]{2,1,0:T(8,128)S(1)}, f32[32,48,128]{2,1,0:T(8,128)S(1)}, f32[32,48,128]{2,1,0:T(8,128)S(1)...) custom-call(s32[6]{0:T(128)S(1)} %stack.67.edge, ...), custom_call_target="tpu_custom_call" | custom-call | tf_op jit(solution)/shard_map/coefficients/pallas_call | solution.py:204
  51.7 3.7 %collective-permute-done.3.high = f32[8,48,128]{2,1,0:T(8,128)S(1)} collective-permute-done((f32[8,48,128]{2,1,0:T(8,128)S(1)}, f32[8,48,128]{2,1,0:T(8,128)S(1)}, u32[]{:S(2)}, u32[]{:S(2)}) %collective-permute-start.3) | collective-permute-done | bytes 196640 | tf_op jit(solution)/shard_map/ppermute | solution.py:198
  55.3 3.2 %fine.1 = (f32[8,2,32,128]{3,2,1,0:T(8,128)}, f32[2,8,2,16,128]{4,3,2,1,0:T(8,128)S(1)}) custom-call(f32[8,48,128]{2,1,0:T(8,128)S(1)} %collective-permute-done.2.low, f32[8,48,128]{2,1,0:T(8,128)S(1)} %get-tuple-element.16.first, f32[8,48,128]{2,1,0:T(8,128)S(1)} %get-tuple-element.15.second, f32[8,48,128]{2,1,0:T(8,128)S(1)} %collective-permute-done.3.high, ...), custom_call_target="tpu_custom_call" | custom-call | tf_op jit(solution)/shard_map/fine/pallas_call | solution.py:207
  58.5 7.2 %all-to-all-start.1 = ((f32[8,2,32,128]{3,2,1,0:T(8,128)}), f32[8,2,32,128]{3,2,1,0:T(8,128)S(1)}, u32[]{:S(2)}, u32[]{:S(2)}) async-start(f32[8,2,32,128]{3,2,1,0:T(8,128)} %get-tuple-element.25), calls=%async_computation.1 | async-start | bytes 524288 | tf_op jit(solution)/shard_map/all_to_all | solution.py:142
  65.6 0.2 copy.7
  65.8 0.1 reshape.20.blocks
  65.9 0.6 copy-done.4
  66.5 0.1 reshape.21.counts
  66.6 8.5 %all-to-all-done.1.tiles = f32[8,2,32,128]{3,2,1,0:T(8,128)S(1)} async-done(((f32[8,2,32,128]{3,2,1,0:T(8,128)}), f32[8,2,32,128]{3,2,1,0:T(8,128)S(1)}, u32[]{:S(2)}, u32[]{:S(2)}) %all-to-all-start.1) | async-done | bytes 262176 | tf_op jit(solution)/shard_map/all_to_all | solution.py:142
  75.1 0.7 pick.1
  75.8 10.3 %all_to_all.20 = f32[16,2,8,128]{3,2,1,0:T(8,128)S(1)} all-to-all(f32[16,2,8,128]{3,2,1,0:T(8,128)S(1)} %pick.1), channel_id=1, replica_groups=mesh['y'=8,'zh'=2,'x'=4,'zl'=4,'c'=2] {'y'}, dimensions={0} | all-to-all | bytes 262144 | tf_op jit(solution)/shard_map/all_to_all | solution.py:142
  86.1 0.8 pack.1
  86.9 11.5 %all-to-all-start.3 = ((f32[16,2,24,128]{3,2,1,0:T(8,128)}), f32[16,2,24,128]{3,2,1,0:T(8,128)S(1)}, u32[]{:S(2)}, u32[]{:S(2)}) async-start(f32[16,2,24,128]{3,2,1,0:T(8,128)} %bitcast.17), calls=%async_computation.3 | async-start | bytes 786432 | tf_op jit(solution)/shard_map/all_to_all | solution.py:142
  98.4 14.5 %all-to-all-done.3.received = f32[16,2,24,128]{3,2,1,0:T(8,128)S(1)} async-done(((f32[16,2,24,128]{3,2,1,0:T(8,128)}), f32[16,2,24,128]{3,2,1,0:T(8,128)S(1)}, u32[]{:S(2)}, u32[]{:S(2)}) %all-to-all-start.3) | async-done | bytes 393248 | tf_op jit(solution)/shard_map/all_to_all | solution.py:142
  112.9 0.8 advance.1
  (19 shorter events, 0.1 us)
Async XLA Ops:
  0.6 97.8 %copy-start = (f32[2,256,128]{2,1,0:T(8,128)S(1)}, f32[2,256,128]{2,1,0:T(8,128)}, u32[]{:S(2)}) copy-start(f32[2,256,128]{2,1,0:T(8,128)} %param.7) | copy-start | bytes 786436
  0.6 12.0 %copy-start.2 = (f32[2,256,128]{2,1,0:T(8,128)S(1)}, f32[2,256,128]{2,1,0:T(8,128)}, u32[]{:S(2)}) copy-start(f32[2,256,128]{2,1,0:T(8,128)} %param.6) | copy-start | bytes 786436
  0.7 36.6 %all-to-all-start = ((f32[16,2,16,128]{3,2,1,0:T(8,128)}), f32[16,2,16,128]{3,2,1,0:T(8,128)S(1)}, u32[]{:S(2)}, u32[]{:S(2)}) async-start(f32[16,2,16,128]{3,2,1,0:T(8,128)} %states.1), calls=%async_computation | async-start | bytes 524288 | tf_op jit(solution)/shard_map/all_to_all | solution.py:142
  12.7 5.2 %collective-permute-start.4 = (f32[2,48,128]{2,1,0:T(8,128)S(1)}, f32[2,48,128]{2,1,0:T(8,128)S(1)}, u32[]{:S(2)}, u32[]{:S(2)}) collective-permute-start(f32[2,48,128]{2,1,0:T(8,128)S(1)} %pad_dynamic-slice_fusion), channel_id=1, source_target_pairs={{4,12},{6,14},{12,20},{14,22},{20,28},{22,30},{8,0},{10,2},{16,8},... | collective-permute-start | bytes 147464 | tf_op jit(solution)/shard_map/ppermute | solution.py:178
  17.8 8.6 %collective-permute-start.5 = (f32[2,2,48,128]{3,2,1,0:T(8,128)S(1)}, f32[2,2,48,128]{3,2,1,0:T(8,128)S(1)}, u32[]{:S(2)}, u32[]{:S(2)}) collective-permute-start(f32[2,2,48,128]{3,2,1,0:T(8,128)S(1)} %get-tuple-element.31), channel_id=1, source_target_pairs={{0,2},{2,4},{4,6},{6,32},{32,34},{34,36},{36,38},{38,0},{1,3},{3,5... | collective-permute-start | bytes 294920 | tf_op jit(solution)/shard_map/ppermute | solution.py:184
  21.1 5.4 %collective-permute-start.6 = (f32[2,2,48,128]{3,2,1,0:T(8,128)S(1)}, f32[2,2,48,128]{3,2,1,0:T(8,128)S(1)}, u32[]{:S(2)}, u32[]{:S(2)}) collective-permute-start(f32[2,2,48,128]{3,2,1,0:T(8,128)S(1)} %get-tuple-element.31), channel_id=1, source_target_pairs={{0,38},{2,0},{4,2},{6,4},{32,6},{34,32},{36,34},{38,36},{1,39},{3,... | collective-permute-start | bytes 294920 | tf_op jit(solution)/shard_map/ppermute | solution.py:184
  24.3 8.4 %collective-permute-start.7 = (f32[2,2,48,128]{3,2,1,0:T(8,128)S(1)}, f32[2,2,48,128]{3,2,1,0:T(8,128)S(1)}, u32[]{:S(2)}, u32[]{:S(2)}) collective-permute-start(f32[2,2,48,128]{3,2,1,0:T(8,128)S(1)} %get-tuple-element.31), channel_id=1, source_target_pairs={{0,4},{2,6},{4,32},{6,34},{32,36},{34,38},{36,0},{38,2},{1,5},{3,7... | collective-permute-start | bytes 294920 | tf_op jit(solution)/shard_map/ppermute | solution.py:184
  32.7 17.6 %collective-permute-start.8 = (f32[4,2,2,48,128]{4,3,2,1,0:T(8,128)S(1)}, f32[4,2,2,48,128]{4,3,2,1,0:T(8,128)S(1)}, u32[]{:S(2)}, u32[]{:S(2)}) collective-permute-start(f32[4,2,2,48,128]{4,3,2,1,0:T(8,128)S(1)} %pad_maximum_fusion.mine), channel_id=1, source_target_pairs={{0,1},{1,0},{2,3},{3,2},{4,5},{5,4},{6,7},{7,6},{8,9},{9,8},{10,11... | collective-permute-start | bytes 1179656 | tf_op jit(solution)/shard_map/ppermute | solution.py:192
  37.2 4.7 %collective-permute-start = (f32[8,2,8,128]{3,2,1,0:T(8,128)S(1)}, f32[8,2,8,128]{3,2,1,0:T(8,128)S(1)}, u32[]{:S(2)}, u32[]{:S(2)}) collective-permute-start(f32[8,2,8,128]{3,2,1,0:T(8,128)S(1)} %get-tuple-element.29), channel_id=1, source_target_pairs={{0,64},{64,128},{128,192},{192,256},{256,320},{320,384},{384,448},... | collective-permute-start | bytes 196616 | tf_op jit(solution)/shard_map/ppermute | solution.py:193
  40.4 5.0 %collective-permute-start.1 = (f32[8,2,8,128]{3,2,1,0:T(8,128)S(1)}, f32[8,2,8,128]{3,2,1,0:T(8,128)S(1)}, u32[]{:S(2)}, u32[]{:S(2)}) collective-permute-start(f32[8,2,8,128]{3,2,1,0:T(8,128)S(1)} %get-tuple-element.28), channel_id=1, source_target_pairs={{64,0},{128,64},{192,128},{256,192},{320,256},{384,320},{448,384},... | collective-permute-start | bytes 196616 | tf_op jit(solution)/shard_map/ppermute | solution.py:194
  45.5 6.2 %collective-permute-start.2 = (f32[8,48,128]{2,1,0:T(8,128)S(1)}, f32[8,48,128]{2,1,0:T(8,128)S(1)}, u32[]{:S(2)}, u32[]{:S(2)}) collective-permute-start(f32[8,48,128]{2,1,0:T(8,128)S(1)} %get-tuple-element.15.second), channel_id=1, source_target_pairs={{0,8},{8,16},{16,24},{1,9},{9,17},{17,25},{2,10},{10,18},{18,26},{... | collective-permute-start | bytes 589832 | tf_op jit(solution)/shard_map/ppermute | solution.py:197
  48.9 6.4 %collective-permute-start.3 = (f32[8,48,128]{2,1,0:T(8,128)S(1)}, f32[8,48,128]{2,1,0:T(8,128)S(1)}, u32[]{:S(2)}, u32[]{:S(2)}) collective-permute-start(f32[8,48,128]{2,1,0:T(8,128)S(1)} %get-tuple-element.16.first), channel_id=1, source_target_pairs={{8,0},{16,8},{24,16},{9,1},{17,9},{25,17},{10,2},{18,10},{26,18},{... | collective-permute-start | bytes 589832 | tf_op jit(solution)/shard_map/ppermute | solution.py:198
  58.5 7.2 %copy-start.3 = (s32[16,16,2]{1,2,0:T(2,128)S(1)}, s32[16,16,2]{1,2,0:T(2,128)}, u32[]{:S(2)}) copy-start(s32[16,16,2]{1,2,0:T(2,128)} %param.8) | copy-start | bytes 6148
  58.5 16.6 %all-to-all-start.1 = ((f32[8,2,32,128]{3,2,1,0:T(8,128)}), f32[8,2,32,128]{3,2,1,0:T(8,128)S(1)}, u32[]{:S(2)}, u32[]{:S(2)}) async-start(f32[8,2,32,128]{3,2,1,0:T(8,128)} %get-tuple-element.25), calls=%async_computation.1 | async-start | bytes 524288 | tf_op jit(solution)/shard_map/all_to_all | solution.py:142
  65.8 0.7 copy-start.4
  86.9 26.1 %copy-start.1 = (f32[16,2,16,128]{3,2,1,0:T(8,128)S(1)}, f32[16,2,16,128]{3,2,1,0:T(8,128)}, u32[]{:S(2)}) copy-start(f32[16,2,16,128]{3,2,1,0:T(8,128)} %states.1) | copy-start | bytes 786436
  86.9 26.1 %all-to-all-start.3 = ((f32[16,2,24,128]{3,2,1,0:T(8,128)}), f32[16,2,24,128]{3,2,1,0:T(8,128)S(1)}, u32[]{:S(2)}, u32[]{:S(2)}) async-start(f32[16,2,24,128]{3,2,1,0:T(8,128)} %bitcast.17), calls=%async_computation.3 | async-start | bytes 786432 | tf_op jit(solution)/shard_map/all_to_all | solution.py:142

commit v4 on v3

--- a/solution.py
+++ b/solution.py
@@ -19,17 +19,6 @@
 VMEM = pl.BlockSpec(memory_space=pltpu.VMEM)
 SMEM = pl.BlockSpec(memory_space=pltpu.SMEM)
 PARAMS = pltpu.CompilerParams(vmem_limit_bytes=40 * 2**20)
-
-
-def join_kernel(own, south, north, first, second):
-    for out, start in ((first, 0), (second, 4)):
-        for j in range(4):
-            for k in range(2):
-                layer = 2 * j + k
-                out[layer, 0:8] = south[start + j, k]
-                out[layer, 8:24] = own[0, start + j, k]
-                out[layer, 24:40] = own[1, start + j, k]
-                out[layer, 40:48] = north[start + j, k]
 
 
 def coefficient_kernel(edge, mine, other, c0, zp, zm, yp, ym, xp, xm, kappa):
@@ -71,11 +60,16 @@
         xm[z] = west * (mask * not_first)
 
 
-def fine_kernel(low, first, second, high, c0, zp, zm, yp, ym, xp, xm, out, ends, u):
+def fine_kernel(low, own, high, c0, zp, zm, yp, ym, xp, xm, out, ends, u):
     depth, rows, lanes = u.shape
-    parts = (low, first, second, high)
+
+    def given(z):
+        part, layer = (low, z) if z < 8 else (own, z - 8) if z < 24 else (high, z - 24)
+        near, far = part[0, layer // 2, layer % 2], part[1, layer // 2, layer % 2]
+        return jnp.concatenate([far[16:24], near[0:16], far[0:16], near[16:24]])
+
     for step in range(1, FINE + 1):
-        at = (lambda z: parts[z // 8][z % 8]) if step == 1 else (lambda z: u[z])
+        at = given if step == 1 else (lambda z: u[z])
         below, here = at(step - 1), at(step)
         for z in range(step, depth - step):
             above = at(z + 1)
@@ -158,17 +152,21 @@
 
 def body(states, diffusivity, coarse_gain, read_block, read_count):
     slices, thick, own_rows, lanes = states.shape
-    y, x, c = lax.axis_index("y"), lax.axis_index("x"), lax.axis_index("c")
+    y, zh = lax.axis_index("y"), lax.axis_index("zh")
+    x, c = lax.axis_index("x"), lax.axis_index("c")
     ny, nx = lax.axis_size("y"), lax.axis_size("x")
     me = lax.axis_index(RING)
     cut = lax.axis_index(CUTS)
     tile_rows = 2 * own_rows
     wide = tile_rows + 2 * FINE
     half = slices // 2
-    y_up = [(i, i + 1) for i in range(ny - 1)]
-    y_down = [(i + 1, i) for i in range(ny - 1)]
     x_up = [(i, i + 1) for i in range(nx - 1)]
     x_down = [(i + 1, i) for i in range(nx - 1)]
+
+    edge_rows = jnp.where(zh == 1, states[:, :, own_rows - FINE :], states[:, :, :FINE])
+    pairs = [(i, i + 2) for i in range(1, 2 * ny - 2, 2)]
+    pairs += [(i, i - 2) for i in range(2, 2 * ny, 2)]
+    side_rows = lax.ppermute(edge_rows, CUTS, pairs)
 
     padded = jnp.pad(diffusivity, ((0, 0), (FINE, FINE), (0, 0)))
     kappa = lax.dynamic_slice_in_dim(padded, y * tile_rows, wide, 1)
@@ -176,26 +174,22 @@
     near += [((i, j), (i - 1, j)) for i in range(1, nx) for j in (0, 1)]
     flat = [(p * 4 + q, r * 4 + s) for (p, q), (r, s) in near]
     side_kappa = lax.ppermute(kappa, ("x", "zl"), flat)
+
+    block = jnp.concatenate([states, side_rows], axis=2)
     pieces = jnp.stack([kappa, side_kappa])
+    block, pieces = lax.optimization_barrier((block, pieces))
+    own = exchange(block, RING).reshape(2, half, thick, own_rows + FINE, lanes)
     around = lax.axis_size(CHIPS)
-    mine = jnp.stack(
-        [pieces]
-        + [
-            lax.ppermute(
-                pieces, CHIPS, [(i, (i - offset) % around) for i in range(around)]
-            )
-            for offset in RING_OFFSETS[1:]
-        ]
-    )
-
-    own = exchange(states, RING).reshape(2, half, thick, own_rows, lanes)
+    ring = [
+        lax.ppermute(pieces, CHIPS, [(i, (i - offset) % around) for i in range(around)])
+        for offset in RING_OFFSETS[1:]
+    ]
+    lower, upper = own[:, : half // 2], own[:, half // 2 :]
+    lower, upper, *ring = lax.optimization_barrier((lower, upper, *ring))
+    low = lax.ppermute(upper, "x", x_up)
+    high = lax.ppermute(lower, "x", x_down)
+    mine = jnp.stack([pieces, *ring])
     other = lax.ppermute(mine, "c", [(0, 1), (1, 0)])
-    south = lax.ppermute(own[1, :, :, own_rows - FINE :], "y", y_up)
-    north = lax.ppermute(own[0, :, :, :FINE], "y", y_down)
-    part = (FINE, wide, lanes)
-    first, second = call(join_kernel, "join", [part] * 2, [VMEM] * 3)(own, south, north)
-    low = lax.ppermute(second, "x", x_up)
-    high = lax.ppermute(first, "x", x_down)
 
     flags = [y > 0, y < ny - 1, x > 0, x < nx - 1, c, lax.axis_index("zl")]
     edge = jnp.stack([flag.astype(jnp.int32) for flag in flags])
@@ -208,9 +202,9 @@
         fine_kernel,
         "fine",
         [(ny, deep // ny, tile_rows, lanes), (2, half, thick, own_rows, lanes)],
-        [VMEM] * 11,
+        [VMEM] * 10,
         [region],
-    )(low, first, second, high, *coefficients)
+    )(low, own, high, *coefficients)
 
     tiles = exchange(fine, "y")
     (picked,) = call(

time: 114 us -> 114 us (level)
  starting transfers between devices: 54.2 us -> 48.3 us
  waiting for transfers between devices: 40.5 us -> 42.7 us
  other arithmetic: 0.04 us -> 1.86 us
    all_to_all x3, waiting for transfers between devices: 23 us -> 28.7 us  [exchange(): return lax.all_to_all(value, axes, 0, 0, tiled=True)]
    ppermute x4 -> x3, starting transfers between devices: 9.19 us -> 5.73 us  [the longest x1 3.15 us: body(): low = lax.ppermute(upper, 'x', x_up)]
    ppermute x4 -> x3, waiting for transfers between devices: 7.36 us -> 5.35 us  [the longest x1 3.8 us: body(): high = lax.ppermute(lower, 'x', x_down)]
    all_to_all x3, starting transfers between devices: 30.6 us -> 28.8 us  [exchange(): return lax.all_to_all(value, axes, 0, 0, tiled=True)]
    ppermute x3, waiting for transfers between devices: 6.24 us -> 4.55 us  [body(): lax.ppermute(pieces, CHIPS, [(i, (i - offset) % around) for i in range(ar...]
    ppermute x1, starting transfers between devices: 4.45 us -> 2.84 us  [body(): other = lax.ppermute(mine, 'c', [(0, 1), (1, 0)])]
  transfers between devices with their start and end apart: 12 -> 11, of which waited for: 7 -> 7; matrix products, arithmetic and copies ran while one was open for 0% -> 0% of each run, Pallas kernels for 1% -> 1%
where the time goes in v4:
time: 114 us; the launch traced here: 113 us
  starting transfers between devices  48.3 us (42%)
  waiting for transfers between devices  42.7 us (37%)
  blocking collectives  10.6 us (9%)
  Pallas kernels  7.39 us (6%)
  other arithmetic  1.86 us (2%)
    all_to_all x3, starting transfers between devices, exchange(): return lax.all_to_all(value, axes, 0, 0, tiled=True)  28.8 us
    all_to_all x3, waiting for transfers between devices, exchange(): return lax.all_to_all(value, axes, 0, 0, tiled=True)  28.7 us
    all_to_all x1, blocking collectives, exchange(): return lax.all_to_all(value, axes, 0, 0, tiled=True)  10.6 us
    ppermute x3, starting transfers between devices, body(): lax.ppermute(pieces, CHIPS, [(i, (i - offset) % around) for i in range(ar...  9.46 us
    ppermute x3, waiting for transfers between devices, body(): lax.ppermute(pieces, CHIPS, [(i, (i - offset) % around) for i in range(ar...  4.55 us
    ppermute x1, waiting for transfers between devices, body(): side_kappa = lax.ppermute(kappa, ('x', 'zl'), flat)  4.1 us
    ppermute x1, waiting for transfers between devices, body(): high = lax.ppermute(lower, 'x', x_down)  3.8 us
    pallas_call x1, Pallas kernels, body(): call(fine_kernel, 'fine', [(ny, deep // ny, tile_rows, lanes), (2, half,...  3.76 us
  transfers between devices with their start and end apart: 11, of which 7 were waited for; matrix products, arithmetic and copies ran while one was open for 0% of the time, Pallas kernels for 1%

profile of v4, /device:TPU:1, one launch (start us, length us, event | category | flops | bytes accessed | tf_op | source)
XLA Modules:
  0.0 112.8 jit_solution(8720424102280221288)
XLA Ops:
  0.6 0.0 copy-start
  0.7 1.0 slice_select_fusion
  1.7 1.3 %collective-permute-start = (f32[16,2,8,128]{3,2,1,0:T(8,128)S(1)}, f32[16,2,8,128]{3,2,1,0:T(8,128)S(1)}, u32[]{:S(2)}, u32[]{:S(2)}) collective-permute-start(f32[16,2,8,128]{3,2,1,0:T(8,128)S(1)} %slice_select_fusion), channel_id=1, source_target_pairs={{32,96},{96,160},{160,224},{224,288},{288,352},{352,416},{416,480}... | collective-permute-start | bytes 393224 | tf_op jit(solution)/shard_map/ppermute | solution.py:169
  3.1 1.4 %collective-permute-start.1 = (f32[2,48,128]{2,1,0:T(8,128)S(1)}, f32[2,48,128]{2,1,0:T(8,128)S(1)}, u32[]{:S(2)}, u32[]{:S(2)}) collective-permute-start(f32[2,48,128]{2,1,0:T(8,128)S(1)} %pad_dynamic-slice_fusion), channel_id=1, source_target_pairs={{4,12},{6,14},{12,20},{14,22},{20,28},{22,30},{8,0},{10,2},{16,8},... | collective-permute-start | bytes 147464 | tf_op jit(solution)/shard_map/ppermute | solution.py:176
  4.5 4.1 %collective-permute-done.1 = f32[2,48,128]{2,1,0:T(8,128)S(1)} collective-permute-done((f32[2,48,128]{2,1,0:T(8,128)S(1)}, f32[2,48,128]{2,1,0:T(8,128)S(1)}, u32[]{:S(2)}, u32[]{:S(2)}) %collective-permute-start.1) | collective-permute-done | bytes 49184 | tf_op jit(solution)/shard_map/ppermute | solution.py:176
  8.6 0.8 pad_maximum_fusion
  9.4 14.6 %all-to-all-start = ((f32[16,2,24,128]{3,2,1,0:T(8,128)}), f32[16,2,24,128]{3,2,1,0:T(8,128)S(1)}, u32[]{:S(2)}, u32[]{:S(2)}) async-start(f32[16,2,24,128]{3,2,1,0:T(8,128)} %pad_maximum_fusion), calls=%async_computation | async-start | bytes 786432 | tf_op jit(solution)/shard_map/all_to_all | solution.py:136
  24.0 3.3 %collective-permute-start.2 = (f32[2,2,48,128]{3,2,1,0:T(8,128)S(1)}, f32[2,2,48,128]{3,2,1,0:T(8,128)S(1)}, u32[]{:S(2)}, u32[]{:S(2)}) collective-permute-start(f32[2,2,48,128]{3,2,1,0:T(8,128)S(1)} %pad_maximum_fusion.2), channel_id=1, source_target_pairs={{0,2},{2,4},{4,6},{6,32},{32,34},{34,36},{36,38},{38,0},{1,3},{3,5... | collective-permute-start | bytes 294920 | tf_op jit(solution)/shard_map/ppermute | solution.py:184
  27.3 3.2 %collective-permute-start.3 = (f32[2,2,48,128]{3,2,1,0:T(8,128)S(1)}, f32[2,2,48,128]{3,2,1,0:T(8,128)S(1)}, u32[]{:S(2)}, u32[]{:S(2)}) collective-permute-start(f32[2,2,48,128]{3,2,1,0:T(8,128)S(1)} %pad_maximum_fusion.2), channel_id=1, source_target_pairs={{0,38},{2,0},{4,2},{6,4},{32,6},{34,32},{36,34},{38,36},{1,39},{3,... | collective-permute-start | bytes 294920 | tf_op jit(solution)/shard_map/ppermute | solution.py:184
  30.5 3.0 %collective-permute-start.4 = (f32[2,2,48,128]{3,2,1,0:T(8,128)S(1)}, f32[2,2,48,128]{3,2,1,0:T(8,128)S(1)}, u32[]{:S(2)}, u32[]{:S(2)}) collective-permute-start(f32[2,2,48,128]{3,2,1,0:T(8,128)S(1)} %pad_maximum_fusion.2), channel_id=1, source_target_pairs={{0,4},{2,6},{4,32},{6,34},{32,36},{34,38},{36,0},{38,2},{1,5},{3,7... | collective-permute-start | bytes 294920 | tf_op jit(solution)/shard_map/ppermute | solution.py:184
  33.5 5.1 %all-to-all-done = f32[16,2,24,128]{3,2,1,0:T(8,128)S(1)} async-done(((f32[16,2,24,128]{3,2,1,0:T(8,128)}), f32[16,2,24,128]{3,2,1,0:T(8,128)S(1)}, u32[]{:S(2)}, u32[]{:S(2)}) %all-to-all-start) | async-done | bytes 393248 | tf_op jit(solution)/shard_map/all_to_all | solution.py:136
  38.6 4.5 %collective-permute-done.4 = f32[2,2,48,128]{3,2,1,0:T(8,128)S(1)} collective-permute-done((f32[2,2,48,128]{3,2,1,0:T(8,128)S(1)}, f32[2,2,48,128]{3,2,1,0:T(8,128)S(1)}, u32[]{:S(2)}, u32[]{:S(2)}) %collective-permute-start.4) | collective-permute-done | bytes 98336 | tf_op jit(solution)/shard_map/ppermute | solution.py:184
  43.2 2.8 %collective-permute-start.7 = (f32[4,2,2,48,128]{4,3,2,1,0:T(8,128)S(1)}, f32[4,2,2,48,128]{4,3,2,1,0:T(8,128)S(1)}, u32[]{:S(2)}, u32[]{:S(2)}) collective-permute-start(f32[4,2,2,48,128]{4,3,2,1,0:T(8,128)S(1)} %pad_maximum_fusion.1.mine), channel_id=1, source_target_pairs={{0,1},{1,0},{2,3},{3,2},{4,5},{5,4},{6,7},{7,6},{8,9},{9,8},{10,11... | collective-permute-start | bytes 1179656 | tf_op jit(solution)/shard_map/ppermute | solution.py:192
  46.0 3.1 %collective-permute-start.5 = (f32[2,4,2,24,128]{4,3,2,1,0:T(8,128)S(1)}, f32[2,4,2,24,128]{4,3,2,1,0:T(8,128)S(1)}, u32[]{:S(2)}, u32[]{:S(2)}) collective-permute-start(f32[2,4,2,24,128]{4,3,2,1,0:T(8,128)S(1)} %get-tuple-element.22), channel_id=1, source_target_pairs={{0,8},{8,16},{16,24},{1,9},{9,17},{17,25},{2,10},{10,18},{18,26},{... | collective-permute-start | bytes 589832 | tf_op jit(solution)/shard_map/ppermute | solution.py:189
  49.2 1.3 %collective-permute-start.6 = (f32[2,4,2,24,128]{4,3,2,1,0:T(8,128)S(1)}, f32[2,4,2,24,128]{4,3,2,1,0:T(8,128)S(1)}, u32[]{:S(2)}, u32[]{:S(2)}) collective-permute-start(f32[2,4,2,24,128]{4,3,2,1,0:T(8,128)S(1)} %get-tuple-element.23), channel_id=1, source_target_pairs={{8,0},{16,8},{24,16},{9,1},{17,9},{25,17},{10,2},{18,10},{26,18},{... | collective-permute-start | bytes 589832 | tf_op jit(solution)/shard_map/ppermute | solution.py:190
  50.5 0.1 stack.70.edge
  50.6 1.3 %coefficients.1 = (f32[32,48,128]{2,1,0:T(8,128)S(1)}, f32[32,48,128]{2,1,0:T(8,128)S(1)}, f32[32,48,128]{2,1,0:T(8,128)S(1)}, f32[32,48,128]{2,1,0:T(8,128)S(1)...) custom-call(s32[6]{0:T(128)S(1)} %stack.70.edge, ...), custom_call_target="tpu_custom_call" | custom-call | tf_op jit(solution)/shard_map/coefficients/pallas_call | solution.py:198
  51.9 1.5 %collective-permute-done.5.low = f32[2,4,2,24,128]{4,3,2,1,0:T(8,128)S(1)} collective-permute-done((f32[2,4,2,24,128]{4,3,2,1,0:T(8,128)S(1)}, f32[2,4,2,24,128]{4,3,2,1,0:T(8,128)S(1)}, u32[]{:S(2)}, u32[]{:S(2)}) %collective-permute-start.5) | collective-permute-done | bytes 196640 | tf_op jit(solution)/shard_map/ppermute | solution.py:189
  53.5 3.8 %collective-permute-done.6.high = f32[2,4,2,24,128]{4,3,2,1,0:T(8,128)S(1)} collective-permute-done((f32[2,4,2,24,128]{4,3,2,1,0:T(8,128)S(1)}, f32[2,4,2,24,128]{4,3,2,1,0:T(8,128)S(1)}, u32[]{:S(2)}, u32[]{:S(2)}) %collective-permute-start.6) | collective-permute-done | bytes 196640 | tf_op jit(solution)/shard_map/ppermute | solution.py:190
  57.3 3.8 %fine.1 = (f32[8,2,32,128]{3,2,1,0:T(8,128)}, f32[2,8,2,16,128]{4,3,2,1,0:T(8,128)S(1)}) custom-call(f32[2,4,2,24,128]{4,3,2,1,0:T(8,128)S(1)} %collective-permute-done.5.low, f32[2,8,2,24,128]{4,3,2,1,0:T(8,128)S(1)} %bitcast.19, f32[2,4,2,24,128]{4,3,2,1,0:T(8,128)S(1)} %collective-permute-done.6.high, f32[32,48,128]{2,1,0:T(8,128)S(1)} %get-tuple-element.27.c0, ...), custom_call_target="tpu_custom_call" | custom-call | tf_op jit(solution)/shard_map/fine/pallas_call | solution.py:201
  61.0 6.1 %all-to-all-start.1 = ((f32[8,2,32,128]{3,2,1,0:T(8,128)}), f32[8,2,32,128]{3,2,1,0:T(8,128)S(1)}, u32[]{:S(2)}, u32[]{:S(2)}) async-start(f32[8,2,32,128]{3,2,1,0:T(8,128)} %get-tuple-element.35), calls=%async_computation.1 | async-start | bytes 524288 | tf_op jit(solution)/shard_map/all_to_all | solution.py:136
  67.1 0.2 copy.7
  67.3 0.1 reshape.20.blocks
  67.4 0.6 copy-done.4
  68.0 0.1 reshape.21.counts
  68.0 9.1 %all-to-all-done.1.tiles = f32[8,2,32,128]{3,2,1,0:T(8,128)S(1)} async-done(((f32[8,2,32,128]{3,2,1,0:T(8,128)}), f32[8,2,32,128]{3,2,1,0:T(8,128)S(1)}, u32[]{:S(2)}, u32[]{:S(2)}) %all-to-all-start.1) | async-done | bytes 262176 | tf_op jit(solution)/shard_map/all_to_all | solution.py:136
  77.2 0.7 pick.1
  77.9 10.6 %all_to_all.20 = f32[16,2,8,128]{3,2,1,0:T(8,128)S(1)} all-to-all(f32[16,2,8,128]{3,2,1,0:T(8,128)S(1)} %pick.1), channel_id=1, replica_groups=mesh['y'=8,'zh'=2,'x'=4,'zl'=4,'c'=2] {'y'}, dimensions={0} | all-to-all | bytes 262144 | tf_op jit(solution)/shard_map/all_to_all | solution.py:136
  88.5 0.8 pack.1
  89.3 8.2 %all-to-all-start.3 = ((f32[16,2,24,128]{3,2,1,0:T(8,128)}), f32[16,2,24,128]{3,2,1,0:T(8,128)S(1)}, u32[]{:S(2)}, u32[]{:S(2)}) async-start(f32[16,2,24,128]{3,2,1,0:T(8,128)} %bitcast.15), calls=%async_computation.3 | async-start | bytes 786432 | tf_op jit(solution)/shard_map/all_to_all | solution.py:136
  97.5 14.5 %all-to-all-done.3.received = f32[16,2,24,128]{3,2,1,0:T(8,128)S(1)} async-done(((f32[16,2,24,128]{3,2,1,0:T(8,128)}), f32[16,2,24,128]{3,2,1,0:T(8,128)S(1)}, u32[]{:S(2)}, u32[]{:S(2)}) %all-to-all-start.3) | async-done | bytes 393248 | tf_op jit(solution)/shard_map/all_to_all | solution.py:136
  112.0 0.8 advance.1
  (18 shorter events, 0.1 us)
Async XLA Ops:
  0.6 96.8 %copy-start = (f32[2,256,128]{2,1,0:T(8,128)S(1)}, f32[2,256,128]{2,1,0:T(8,128)}, u32[]{:S(2)}) copy-start(f32[2,256,128]{2,1,0:T(8,128)} %param.7) | copy-start | bytes 786436
  0.6 2.4 %copy-start.2 = (f32[2,256,128]{2,1,0:T(8,128)S(1)}, f32[2,256,128]{2,1,0:T(8,128)}, u32[]{:S(2)}) copy-start(f32[2,256,128]{2,1,0:T(8,128)} %param.6) | copy-start | bytes 786436
  1.7 6.9 %collective-permute-start = (f32[16,2,8,128]{3,2,1,0:T(8,128)S(1)}, f32[16,2,8,128]{3,2,1,0:T(8,128)S(1)}, u32[]{:S(2)}, u32[]{:S(2)}) collective-permute-start(f32[16,2,8,128]{3,2,1,0:T(8,128)S(1)} %slice_select_fusion), channel_id=1, source_target_pairs={{32,96},{96,160},{160,224},{224,288},{288,352},{352,416},{416,480}... | collective-permute-start | bytes 393224 | tf_op jit(solution)/shard_map/ppermute | solution.py:169
  3.0 5.6 %copy-start.1 = (f32[16,2,16,128]{3,2,1,0:T(8,128)S(1)}, f32[16,2,16,128]{3,2,1,0:T(8,128)}, u32[]{:S(2)}) copy-start(f32[16,2,16,128]{3,2,1,0:T(8,128)} %states.1) | copy-start | bytes 786436
  3.1 5.6 %collective-permute-start.1 = (f32[2,48,128]{2,1,0:T(8,128)S(1)}, f32[2,48,128]{2,1,0:T(8,128)S(1)}, u32[]{:S(2)}, u32[]{:S(2)}) collective-permute-start(f32[2,48,128]{2,1,0:T(8,128)S(1)} %pad_dynamic-slice_fusion), channel_id=1, source_target_pairs={{4,12},{6,14},{12,20},{14,22},{20,28},{22,30},{8,0},{10,2},{16,8},... | collective-permute-start | bytes 147464 | tf_op jit(solution)/shard_map/ppermute | solution.py:176
  9.4 29.1 %all-to-all-start = ((f32[16,2,24,128]{3,2,1,0:T(8,128)}), f32[16,2,24,128]{3,2,1,0:T(8,128)S(1)}, u32[]{:S(2)}, u32[]{:S(2)}) async-start(f32[16,2,24,128]{3,2,1,0:T(8,128)} %pad_maximum_fusion), calls=%async_computation | async-start | bytes 786432 | tf_op jit(solution)/shard_map/all_to_all | solution.py:136
  24.0 14.6 %collective-permute-start.2 = (f32[2,2,48,128]{3,2,1,0:T(8,128)S(1)}, f32[2,2,48,128]{3,2,1,0:T(8,128)S(1)}, u32[]{:S(2)}, u32[]{:S(2)}) collective-permute-start(f32[2,2,48,128]{3,2,1,0:T(8,128)S(1)} %pad_maximum_fusion.2), channel_id=1, source_target_pairs={{0,2},{2,4},{4,6},{6,32},{32,34},{34,36},{36,38},{38,0},{1,3},{3,5... | collective-permute-start | bytes 294920 | tf_op jit(solution)/shard_map/ppermute | solution.py:184
  27.3 11.3 %collective-permute-start.3 = (f32[2,2,48,128]{3,2,1,0:T(8,128)S(1)}, f32[2,2,48,128]{3,2,1,0:T(8,128)S(1)}, u32[]{:S(2)}, u32[]{:S(2)}) collective-permute-start(f32[2,2,48,128]{3,2,1,0:T(8,128)S(1)} %pad_maximum_fusion.2), channel_id=1, source_target_pairs={{0,38},{2,0},{4,2},{6,4},{32,6},{34,32},{36,34},{38,36},{1,39},{3,... | collective-permute-start | bytes 294920 | tf_op jit(solution)/shard_map/ppermute | solution.py:184
  30.5 12.6 %collective-permute-start.4 = (f32[2,2,48,128]{3,2,1,0:T(8,128)S(1)}, f32[2,2,48,128]{3,2,1,0:T(8,128)S(1)}, u32[]{:S(2)}, u32[]{:S(2)}) collective-permute-start(f32[2,2,48,128]{3,2,1,0:T(8,128)S(1)} %pad_maximum_fusion.2), channel_id=1, source_target_pairs={{0,4},{2,6},{4,32},{6,34},{32,36},{34,38},{36,0},{38,2},{1,5},{3,7... | collective-permute-start | bytes 294920 | tf_op jit(solution)/shard_map/ppermute | solution.py:184
  43.2 7.4 %collective-permute-start.7 = (f32[4,2,2,48,128]{4,3,2,1,0:T(8,128)S(1)}, f32[4,2,2,48,128]{4,3,2,1,0:T(8,128)S(1)}, u32[]{:S(2)}, u32[]{:S(2)}) collective-permute-start(f32[4,2,2,48,128]{4,3,2,1,0:T(8,128)S(1)} %pad_maximum_fusion.1.mine), channel_id=1, source_target_pairs={{0,1},{1,0},{2,3},{3,2},{4,5},{5,4},{6,7},{7,6},{8,9},{9,8},{10,11... | collective-permute-start | bytes 1179656 | tf_op jit(solution)/shard_map/ppermute | solution.py:192
  46.0 7.4 %collective-permute-start.5 = (f32[2,4,2,24,128]{4,3,2,1,0:T(8,128)S(1)}, f32[2,4,2,24,128]{4,3,2,1,0:T(8,128)S(1)}, u32[]{:S(2)}, u32[]{:S(2)}) collective-permute-start(f32[2,4,2,24,128]{4,3,2,1,0:T(8,128)S(1)} %get-tuple-element.22), channel_id=1, source_target_pairs={{0,8},{8,16},{16,24},{1,9},{9,17},{17,25},{2,10},{10,18},{18,26},{... | collective-permute-start | bytes 589832 | tf_op jit(solution)/shard_map/ppermute | solution.py:189
  49.2 8.1 %collective-permute-start.6 = (f32[2,4,2,24,128]{4,3,2,1,0:T(8,128)S(1)}, f32[2,4,2,24,128]{4,3,2,1,0:T(8,128)S(1)}, u32[]{:S(2)}, u32[]{:S(2)}) collective-permute-start(f32[2,4,2,24,128]{4,3,2,1,0:T(8,128)S(1)} %get-tuple-element.23), channel_id=1, source_target_pairs={{8,0},{16,8},{24,16},{9,1},{17,9},{25,17},{10,2},{18,10},{26,18},{... | collective-permute-start | bytes 589832 | tf_op jit(solution)/shard_map/ppermute | solution.py:190
  61.0 6.1 %copy-start.3 = (s32[16,16,2]{1,2,0:T(2,128)S(1)}, s32[16,16,2]{1,2,0:T(2,128)}, u32[]{:S(2)}) copy-start(s32[16,16,2]{1,2,0:T(2,128)} %param.8) | copy-start | bytes 6148
  61.0 16.1 %all-to-all-start.1 = ((f32[8,2,32,128]{3,2,1,0:T(8,128)}), f32[8,2,32,128]{3,2,1,0:T(8,128)S(1)}, u32[]{:S(2)}, u32[]{:S(2)}) async-start(f32[8,2,32,128]{3,2,1,0:T(8,128)} %get-tuple-element.35), calls=%async_computation.1 | async-start | bytes 524288 | tf_op jit(solution)/shard_map/all_to_all | solution.py:136
  67.3 0.7 copy-start.4
  89.3 22.7 %all-to-all-start.3 = ((f32[16,2,24,128]{3,2,1,0:T(8,128)}), f32[16,2,24,128]{3,2,1,0:T(8,128)S(1)}, u32[]{:S(2)}, u32[]{:S(2)}) async-start(f32[16,2,24,128]{3,2,1,0:T(8,128)} %bitcast.15), calls=%async_computation.3 | async-start | bytes 786432 | tf_op jit(solution)/shard_map/all_to_all | solution.py:136

commit v5 on v4

--- a/solution.py
+++ b/solution.py
@@ -21,17 +21,23 @@
 PARAMS = pltpu.CompilerParams(vmem_limit_bytes=40 * 2**20)
 
 
-def coefficient_kernel(edge, mine, other, c0, zp, zm, yp, ym, xp, xm, kappa):
-    depth, rows, lanes = kappa.shape
-    core = edge[4]
-    for part, source in ((core, mine), (1 - core, other)):
+def gather_kernel(place, mine, other, first, second, kappa):
+    for part, source in ((place[0], mine), (1 - place[0], other)):
         for i, offset in enumerate(RING_OFFSETS):
-            j = (edge[5] + offset) & 3
-            side = jnp.where(j >= 2, 4 * (j - 2), 24 + 4 * j)
+            j = (place[1] + offset) & 3
             for k in range(2):
-                kappa[8 + 4 * j + 2 * part + k] = source[i, 0, k]
-                kappa[side + 2 * part + k] = source[i, 1, k]
-
+                kappa[4 * j + 2 * part + k] = source[i, k]
+    for z in range(FINE):
+        first[z] = kappa[z]
+        second[z] = kappa[FINE + z]
+
+
+def coefficient_kernel(
+    edge, low, first, second, high, c0, zp, zm, yp, ym, xp, xm
+):
+    depth, rows, lanes = c0.shape
+    parts = (low, first, second, high)
+    at = lambda z: parts[z // 8][z % 8]
     row = lax.broadcasted_iota(jnp.int32, (rows, lanes), 0)
     lane = lax.broadcasted_iota(jnp.int32, (rows, lanes), 1)
     inside = jnp.where(
@@ -41,11 +47,11 @@
     above = inside * edge[3].astype(jnp.float32)
     not_first = jnp.where(lane == 0, 0.0, 1.0)
     not_last = jnp.where(lane == lanes - 1, 0.0, 1.0)
+    down, here = 0.5 * (at(0) + at(1)), at(1)
     for z in range(1, depth - 1):
         mask = below if z < 8 else above if z >= depth - 8 else inside
-        here = kappa[z]
-        up = 0.5 * (here + kappa[z + 1])
-        down = 0.5 * (here + kappa[z - 1])
+        after = at(z + 1)
+        up = 0.5 * (here + after)
         north = 0.5 * (here + pltpu.roll(here, rows - 1, 0))
         south = 0.5 * (here + pltpu.roll(here, 1, 0))
         east = 0.5 * (here + pltpu.roll(here, lanes - 1, 1) * not_last)
@@ -58,6 +64,7 @@
         ym[z] = south * mask
         xp[z] = east * (mask * not_last)
         xm[z] = west * (mask * not_first)
+        down, here = up, after
 
 
 def fine_kernel(low, own, high, c0, zp, zm, yp, ym, xp, xm, out, ends, u):
@@ -163,41 +170,43 @@
     x_up = [(i, i + 1) for i in range(nx - 1)]
     x_down = [(i + 1, i) for i in range(nx - 1)]
 
-    edge_rows = jnp.where(zh == 1, states[:, :, own_rows - FINE :], states[:, :, :FINE])
+    edge_rows = lax.dynamic_slice_in_dim(states, zh * (own_rows - FINE), FINE, 2)
     pairs = [(i, i + 2) for i in range(1, 2 * ny - 2, 2)]
     pairs += [(i, i - 2) for i in range(2, 2 * ny, 2)]
     side_rows = lax.ppermute(edge_rows, CUTS, pairs)
 
     padded = jnp.pad(diffusivity, ((0, 0), (FINE, FINE), (0, 0)))
     kappa = lax.dynamic_slice_in_dim(padded, y * tile_rows, wide, 1)
-    near = [((i, j), (i + 1, j)) for i in range(nx - 1) for j in (2, 3)]
-    near += [((i, j), (i - 1, j)) for i in range(1, nx) for j in (0, 1)]
-    flat = [(p * 4 + q, r * 4 + s) for (p, q), (r, s) in near]
-    side_kappa = lax.ppermute(kappa, ("x", "zl"), flat)
-
-    block = jnp.concatenate([states, side_rows], axis=2)
-    pieces = jnp.stack([kappa, side_kappa])
-    block, pieces = lax.optimization_barrier((block, pieces))
-    own = exchange(block, RING).reshape(2, half, thick, own_rows + FINE, lanes)
     around = lax.axis_size(CHIPS)
     ring = [
-        lax.ppermute(pieces, CHIPS, [(i, (i - offset) % around) for i in range(around)])
+        lax.ppermute(kappa, CHIPS, [(i, (i - offset) % around) for i in range(around)])
         for offset in RING_OFFSETS[1:]
     ]
-    lower, upper = own[:, : half // 2], own[:, half // 2 :]
-    lower, upper, *ring = lax.optimization_barrier((lower, upper, *ring))
-    low = lax.ppermute(upper, "x", x_up)
-    high = lax.ppermute(lower, "x", x_down)
-    mine = jnp.stack([pieces, *ring])
+
+    block = jnp.concatenate([states, side_rows], axis=2)
+    block, kappa, *ring = lax.optimization_barrier((block, kappa, *ring))
+    own = exchange(block, RING).reshape(2, half, thick, own_rows + FINE, lanes)
+
+    mine = jnp.stack([kappa, *ring])
     other = lax.ppermute(mine, "c", [(0, 1), (1, 0)])
-
-    flags = [y > 0, y < ny - 1, x > 0, x < nx - 1, c, lax.axis_index("zl")]
+    place = jnp.stack([c, lax.axis_index("zl")])
+    part = (FINE, wide, lanes)
+    k_first, k_second = call(
+        gather_kernel, "gather", [part] * 2, [SMEM, VMEM, VMEM], [(2 * FINE, *part[1:])]
+    )(place, mine, other)
+    k_low = lax.ppermute(k_second, "x", x_up)
+    k_high = lax.ppermute(k_first, "x", x_down)
+
+    low = lax.ppermute(own[:, half // 2 :], "x", x_up)
+    high = lax.ppermute(own[:, : half // 2], "x", x_down)
+
+    flags = [y > 0, y < ny - 1, x > 0, x < nx - 1]
     edge = jnp.stack([flag.astype(jnp.int32) for flag in flags])
     deep = half * thick
     region = (deep + 2 * FINE, wide, lanes)
     coefficients = call(
-        coefficient_kernel, "coefficients", [region] * 7, [SMEM, VMEM, VMEM], [region]
-    )(edge, mine, other)
+        coefficient_kernel, "coefficients", [region] * 7, [SMEM] + [VMEM] * 4
+    )(edge, k_low, k_first, k_second, k_high)
     fine, ends = call(
         fine_kernel,
         "fine",

time: 114 us -> 114 us (level)
    ppermute x6 -> x7, starting transfers between devices: 15.3 us -> 26.1 us  [the longest x3 17.3 us: body(): lax.ppermute(kappa, CHIPS, [(i, (i - offset) % around) for i in range(aro...]
    all_to_all x3, starting transfers between devices: 28.8 us -> 19.2 us  [exchange(): return lax.all_to_all(value, axes, 0, 0, tiled=True)]
    ppermute x6 -> x7, waiting for transfers between devices: 14 us -> 10.4 us  [the longest x1 4.38 us: body(): high = lax.ppermute(own[:, :half // 2], 'x', x_down)]
    all_to_all x3, waiting for transfers between devices: 28.7 us -> 30.7 us  [exchange(): return lax.all_to_all(value, axes, 0, 0, tiled=True)]
    ppermute x1, waiting for transfers between devices: 0.01 us -> 1.23 us  [body(): other = lax.ppermute(mine, 'c', [(0, 1), (1, 0)])]
  transfers between devices with their start and end apart: 11 -> 12, of which waited for: 7 -> 7; matrix products, arithmetic and copies ran while one was open for 0% -> 1% of each run, Pallas kernels for 1% -> 2%
where the time goes in v5:
time: 114 us; the launch traced here: 113 us
  starting transfers between devices  48.6 us (43%)
  waiting for transfers between devices  42.4 us (37%)
  blocking collectives  10.3 us (9%)
  Pallas kernels  7.89 us (7%)
  local copies, waits for them, and re-layouts  2 us (2%)
    all_to_all x3, waiting for transfers between devices, exchange(): return lax.all_to_all(value, axes, 0, 0, tiled=True)  30.7 us
    all_to_all x3, starting transfers between devices, exchange(): return lax.all_to_all(value, axes, 0, 0, tiled=True)  19.2 us
    ppermute x3, starting transfers between devices, body(): lax.ppermute(kappa, CHIPS, [(i, (i - offset) % around) for i in range(aro...  17.3 us
    all_to_all x1, blocking collectives, exchange(): return lax.all_to_all(value, axes, 0, 0, tiled=True)  10.3 us
    ppermute x1, waiting for transfers between devices, body(): high = lax.ppermute(own[:, :half // 2], 'x', x_down)  4.38 us
    ppermute x3, waiting for transfers between devices, body(): lax.ppermute(kappa, CHIPS, [(i, (i - offset) % around) for i in range(aro...  4.32 us
    pallas_call x1, Pallas kernels, body(): call(fine_kernel, 'fine', [(ny, deep // ny, tile_rows, lanes), (2, half,...  3.76 us
    ppermute x1, starting transfers between devices, body(): k_low = lax.ppermute(k_second, 'x', x_up)  3.13 us
  transfers between devices with their start and end apart: 12, of which 7 were waited for; matrix products, arithmetic and copies ran while one was open for 1% of the time, Pallas kernels for 2%

profile of v5, /device:TPU:1, one launch (start us, length us, event | category | flops | bytes accessed | tf_op | source)
XLA Modules:
  0.0 112.9 jit_solution(312891950143924058)
XLA Ops:
  0.7 1.0 constant_dynamic-slice_fusion.1
  1.7 1.3 %collective-permute-start = (f32[16,2,8,128]{3,2,1,0:T(8,128)S(1)}, f32[16,2,8,128]{3,2,1,0:T(8,128)S(1)}, u32[]{:S(2)}, u32[]{:S(2)}) collective-permute-start(f32[16,2,8,128]{3,2,1,0:T(8,128)S(1)} %constant_dynamic-slice_fusion.1), channel_id=1, source_target_pairs={{32,96},{96,160},{160,224},{224,288},{288,352},{352,416},{416,480}... | collective-permute-start | bytes 393224 | tf_op jit(solution)/shard_map/ppermute | solution.py:176
  3.0 4.8 %collective-permute-start.1 = (f32[2,48,128]{2,1,0:T(8,128)S(1)}, f32[2,48,128]{2,1,0:T(8,128)S(1)}, u32[]{:S(2)}, u32[]{:S(2)}) collective-permute-start(f32[2,48,128]{2,1,0:T(8,128)S(1)} %pad_dynamic-slice_fusion), channel_id=1, source_target_pairs={{0,2},{2,4},{4,6},{6,32},{32,34},{34,36},{36,38},{38,0},{1,3},{3,5... | collective-permute-start | bytes 147464 | tf_op jit(solution)/shard_map/ppermute | solution.py:182
  7.8 10.5 %collective-permute-start.2 = (f32[2,48,128]{2,1,0:T(8,128)S(1)}, f32[2,48,128]{2,1,0:T(8,128)S(1)}, u32[]{:S(2)}, u32[]{:S(2)}) collective-permute-start(f32[2,48,128]{2,1,0:T(8,128)S(1)} %pad_dynamic-slice_fusion), channel_id=1, source_target_pairs={{0,38},{2,0},{4,2},{6,4},{32,6},{34,32},{36,34},{38,36},{1,39},{3,... | collective-permute-start | bytes 147464 | tf_op jit(solution)/shard_map/ppermute | solution.py:182
  18.3 1.9 %collective-permute-start.3 = (f32[2,48,128]{2,1,0:T(8,128)S(1)}, f32[2,48,128]{2,1,0:T(8,128)S(1)}, u32[]{:S(2)}, u32[]{:S(2)}) collective-permute-start(f32[2,48,128]{2,1,0:T(8,128)S(1)} %pad_dynamic-slice_fusion), channel_id=1, source_target_pairs={{0,4},{2,6},{4,32},{6,34},{32,36},{34,38},{36,0},{38,2},{1,5},{3,7... | collective-permute-start | bytes 147464 | tf_op jit(solution)/shard_map/ppermute | solution.py:182
  20.3 0.8 pad_maximum_fusion
  21.1 4.3 %collective-permute-done.3 = f32[2,48,128]{2,1,0:T(8,128)S(1)} collective-permute-done((f32[2,48,128]{2,1,0:T(8,128)S(1)}, f32[2,48,128]{2,1,0:T(8,128)S(1)}, u32[]{:S(2)}, u32[]{:S(2)}) %collective-permute-start.3) | collective-permute-done | bytes 49184 | tf_op jit(solution)/shard_map/ppermute | solution.py:182
  25.4 6.8 %all-to-all-start = ((f32[16,2,24,128]{3,2,1,0:T(8,128)}), f32[16,2,24,128]{3,2,1,0:T(8,128)S(1)}, u32[]{:S(2)}, u32[]{:S(2)}) async-start(f32[16,2,24,128]{3,2,1,0:T(8,128)} %pad_maximum_fusion), calls=%async_computation | async-start | bytes 786432 | tf_op jit(solution)/shard_map/all_to_all | solution.py:143
  32.2 2.0 %collective-permute-start.6 = (f32[4,2,48,128]{3,2,1,0:T(8,128)S(1)}, f32[4,2,48,128]{3,2,1,0:T(8,128)S(1)}, u32[]{:S(2)}, u32[]{:S(2)}) collective-permute-start(f32[4,2,48,128]{3,2,1,0:T(8,128)S(1)} %pad_maximum_fusion.1.mine), channel_id=1, source_target_pairs={{0,1},{1,0},{2,3},{3,2},{4,5},{5,4},{6,7},{7,6},{8,9},{9,8},{10,11... | collective-permute-start | bytes 589832 | tf_op jit(solution)/shard_map/ppermute | solution.py:191
  34.3 1.2 %collective-permute-done.6.other = f32[4,2,48,128]{3,2,1,0:T(8,128)S(1)} collective-permute-done((f32[4,2,48,128]{3,2,1,0:T(8,128)S(1)}, f32[4,2,48,128]{3,2,1,0:T(8,128)S(1)}, u32[]{:S(2)}, u32[]{:S(2)}) %collective-permute-start.6) | collective-permute-done | bytes 196640 | tf_op jit(solution)/shard_map/ppermute | solution.py:191
  35.5 0.6 gather.1
  36.1 3.1 %collective-permute-start.7 = (f32[8,48,128]{2,1,0:T(8,128)S(1)}, f32[8,48,128]{2,1,0:T(8,128)S(1)}, u32[]{:S(2)}, u32[]{:S(2)}) collective-permute-start(f32[8,48,128]{2,1,0:T(8,128)S(1)} %get-tuple-element.25.second), channel_id=1, source_target_pairs={{0,8},{8,16},{16,24},{1,9},{9,17},{17,25},{2,10},{10,18},{18,26},{... | collective-permute-start | bytes 589832 | tf_op jit(solution)/shard_map/ppermute | solution.py:197
  39.2 1.3 %collective-permute-start.8 = (f32[8,48,128]{2,1,0:T(8,128)S(1)}, f32[8,48,128]{2,1,0:T(8,128)S(1)}, u32[]{:S(2)}, u32[]{:S(2)}) collective-permute-start(f32[8,48,128]{2,1,0:T(8,128)S(1)} %get-tuple-element.26.first), channel_id=1, source_target_pairs={{8,0},{16,8},{24,16},{9,1},{17,9},{25,17},{10,2},{18,10},{26,18},{... | collective-permute-start | bytes 589832 | tf_op jit(solution)/shard_map/ppermute | solution.py:198
  40.5 6.2 %all-to-all-done = f32[16,2,24,128]{3,2,1,0:T(8,128)S(1)} async-done(((f32[16,2,24,128]{3,2,1,0:T(8,128)}), f32[16,2,24,128]{3,2,1,0:T(8,128)S(1)}, u32[]{:S(2)}, u32[]{:S(2)}) %all-to-all-start) | async-done | bytes 393248 | tf_op jit(solution)/shard_map/all_to_all | solution.py:143
  46.7 3.1 %collective-permute-start.4 = (f32[2,4,2,24,128]{4,3,2,1,0:T(8,128)S(1)}, f32[2,4,2,24,128]{4,3,2,1,0:T(8,128)S(1)}, u32[]{:S(2)}, u32[]{:S(2)}) collective-permute-start(f32[2,4,2,24,128]{4,3,2,1,0:T(8,128)S(1)} %get-tuple-element.39), channel_id=1, source_target_pairs={{0,8},{8,16},{16,24},{1,9},{9,17},{17,25},{2,10},{10,18},{18,26},{... | collective-permute-start | bytes 589832 | tf_op jit(solution)/shard_map/ppermute | solution.py:200
  49.9 1.3 %collective-permute-start.5 = (f32[2,4,2,24,128]{4,3,2,1,0:T(8,128)S(1)}, f32[2,4,2,24,128]{4,3,2,1,0:T(8,128)S(1)}, u32[]{:S(2)}, u32[]{:S(2)}) collective-permute-start(f32[2,4,2,24,128]{4,3,2,1,0:T(8,128)S(1)} %get-tuple-element.38), channel_id=1, source_target_pairs={{8,0},{16,8},{24,16},{9,1},{17,9},{25,17},{10,2},{18,10},{26,18},{... | collective-permute-start | bytes 589832 | tf_op jit(solution)/shard_map/ppermute | solution.py:201
  51.3 1.3 %coefficients.1 = (f32[32,48,128]{2,1,0:T(8,128)S(1)}, f32[32,48,128]{2,1,0:T(8,128)S(1)}, f32[32,48,128]{2,1,0:T(8,128)S(1)}, f32[32,48,128]{2,1,0:T(8,128)S(1)...) custom-call(s32[4]{0:T(128)S(1)} %add_convert_fusion.edge, ...), custom_call_target="tpu_custom_call" | custom-call | tf_op jit(solution)/shard_map/coefficients/pallas_call | solution.py:207
  52.5 1.7 %collective-permute-done.4.low = f32[2,4,2,24,128]{4,3,2,1,0:T(8,128)S(1)} collective-permute-done((f32[2,4,2,24,128]{4,3,2,1,0:T(8,128)S(1)}, f32[2,4,2,24,128]{4,3,2,1,0:T(8,128)S(1)}, u32[]{:S(2)}, u32[]{:S(2)}) %collective-permute-start.4) | collective-permute-done | bytes 196640 | tf_op jit(solution)/shard_map/ppermute | solution.py:200
  54.3 4.4 %collective-permute-done.5.high = f32[2,4,2,24,128]{4,3,2,1,0:T(8,128)S(1)} collective-permute-done((f32[2,4,2,24,128]{4,3,2,1,0:T(8,128)S(1)}, f32[2,4,2,24,128]{4,3,2,1,0:T(8,128)S(1)}, u32[]{:S(2)}, u32[]{:S(2)}) %collective-permute-start.5) | collective-permute-done | bytes 196640 | tf_op jit(solution)/shard_map/ppermute | solution.py:201
  58.6 3.8 %fine.1 = (f32[8,2,32,128]{3,2,1,0:T(8,128)}, f32[2,8,2,16,128]{4,3,2,1,0:T(8,128)S(1)}) custom-call(f32[2,4,2,24,128]{4,3,2,1,0:T(8,128)S(1)} %collective-permute-done.4.low, f32[2,8,2,24,128]{4,3,2,1,0:T(8,128)S(1)} %bitcast.16, f32[2,4,2,24,128]{4,3,2,1,0:T(8,128)S(1)} %collective-permute-done.5.high, f32[32,48,128]{2,1,0:T(8,128)S(1)} %get-tuple-element.27.c0, ...), custom_call_target="tpu_custom_call" | custom-call | tf_op jit(solution)/shard_map/fine/pallas_call | solution.py:210
  62.4 6.1 %all-to-all-start.1 = ((f32[8,2,32,128]{3,2,1,0:T(8,128)}), f32[8,2,32,128]{3,2,1,0:T(8,128)S(1)}, u32[]{:S(2)}, u32[]{:S(2)}) async-start(f32[8,2,32,128]{3,2,1,0:T(8,128)} %get-tuple-element.35), calls=%async_computation.1 | async-start | bytes 524288 | tf_op jit(solution)/shard_map/all_to_all | solution.py:143
  68.5 0.2 copy.7
  68.6 0.1 reshape.20.blocks
  68.8 0.6 copy-done.4
  69.3 0.1 reshape.21.counts
  69.4 10.0 %all-to-all-done.1.tiles = f32[8,2,32,128]{3,2,1,0:T(8,128)S(1)} async-done(((f32[8,2,32,128]{3,2,1,0:T(8,128)}), f32[8,2,32,128]{3,2,1,0:T(8,128)S(1)}, u32[]{:S(2)}, u32[]{:S(2)}) %all-to-all-start.1) | async-done | bytes 262176 | tf_op jit(solution)/shard_map/all_to_all | solution.py:143
  79.4 0.7 pick.1
  80.2 10.3 %all_to_all.20 = f32[16,2,8,128]{3,2,1,0:T(8,128)S(1)} all-to-all(f32[16,2,8,128]{3,2,1,0:T(8,128)S(1)} %pick.1), channel_id=1, replica_groups=mesh['y'=8,'zh'=2,'x'=4,'zl'=4,'c'=2] {'y'}, dimensions={0} | all-to-all | bytes 262144 | tf_op jit(solution)/shard_map/all_to_all | solution.py:143
  90.5 0.8 pack.1
  91.2 6.3 %all-to-all-start.3 = ((f32[16,2,24,128]{3,2,1,0:T(8,128)}), f32[16,2,24,128]{3,2,1,0:T(8,128)S(1)}, u32[]{:S(2)}, u32[]{:S(2)}) async-start(f32[16,2,24,128]{3,2,1,0:T(8,128)} %bitcast.13), calls=%async_computation.3 | async-start | bytes 786432 | tf_op jit(solution)/shard_map/all_to_all | solution.py:143
  97.6 14.5 %all-to-all-done.3.received = f32[16,2,24,128]{3,2,1,0:T(8,128)S(1)} async-done(((f32[16,2,24,128]{3,2,1,0:T(8,128)}), f32[16,2,24,128]{3,2,1,0:T(8,128)S(1)}, u32[]{:S(2)}, u32[]{:S(2)}) %all-to-all-start.3) | async-done | bytes 393248 | tf_op jit(solution)/shard_map/all_to_all | solution.py:143
  112.1 0.8 advance.1
  (20 shorter events, 0.3 us)
Async XLA Ops:
  0.6 97.0 %copy-start = (f32[2,256,128]{2,1,0:T(8,128)S(1)}, f32[2,256,128]{2,1,0:T(8,128)}, u32[]{:S(2)}) copy-start(f32[2,256,128]{2,1,0:T(8,128)} %param.7) | copy-start | bytes 786436
  0.6 2.3 %copy-start.2 = (f32[2,256,128]{2,1,0:T(8,128)S(1)}, f32[2,256,128]{2,1,0:T(8,128)}, u32[]{:S(2)}) copy-start(f32[2,256,128]{2,1,0:T(8,128)} %param.6) | copy-start | bytes 786436
  0.7 19.6 %copy-start.1 = (f32[16,2,16,128]{3,2,1,0:T(8,128)S(1)}, f32[16,2,16,128]{3,2,1,0:T(8,128)}, u32[]{:S(2)}) copy-start(f32[16,2,16,128]{3,2,1,0:T(8,128)} %states.1) | copy-start | bytes 786436
  1.7 18.6 %collective-permute-start = (f32[16,2,8,128]{3,2,1,0:T(8,128)S(1)}, f32[16,2,8,128]{3,2,1,0:T(8,128)S(1)}, u32[]{:S(2)}, u32[]{:S(2)}) collective-permute-start(f32[16,2,8,128]{3,2,1,0:T(8,128)S(1)} %constant_dynamic-slice_fusion.1), channel_id=1, source_target_pairs={{32,96},{96,160},{160,224},{224,288},{288,352},{352,416},{416,480}... | collective-permute-start | bytes 393224 | tf_op jit(solution)/shard_map/ppermute | solution.py:176
  3.0 18.1 %collective-permute-start.1 = (f32[2,48,128]{2,1,0:T(8,128)S(1)}, f32[2,48,128]{2,1,0:T(8,128)S(1)}, u32[]{:S(2)}, u32[]{:S(2)}) collective-permute-start(f32[2,48,128]{2,1,0:T(8,128)S(1)} %pad_dynamic-slice_fusion), channel_id=1, source_target_pairs={{0,2},{2,4},{4,6},{6,32},{32,34},{34,36},{36,38},{38,0},{1,3},{3,5... | collective-permute-start | bytes 147464 | tf_op jit(solution)/shard_map/ppermute | solution.py:182
  7.8 13.2 %collective-permute-start.2 = (f32[2,48,128]{2,1,0:T(8,128)S(1)}, f32[2,48,128]{2,1,0:T(8,128)S(1)}, u32[]{:S(2)}, u32[]{:S(2)}) collective-permute-start(f32[2,48,128]{2,1,0:T(8,128)S(1)} %pad_dynamic-slice_fusion), channel_id=1, source_target_pairs={{0,38},{2,0},{4,2},{6,4},{32,6},{34,32},{36,34},{38,36},{1,39},{3,... | collective-permute-start | bytes 147464 | tf_op jit(solution)/shard_map/ppermute | solution.py:182
  18.3 7.0 %collective-permute-start.3 = (f32[2,48,128]{2,1,0:T(8,128)S(1)}, f32[2,48,128]{2,1,0:T(8,128)S(1)}, u32[]{:S(2)}, u32[]{:S(2)}) collective-permute-start(f32[2,48,128]{2,1,0:T(8,128)S(1)} %pad_dynamic-slice_fusion), channel_id=1, source_target_pairs={{0,4},{2,6},{4,32},{6,34},{32,36},{34,38},{36,0},{38,2},{1,5},{3,7... | collective-permute-start | bytes 147464 | tf_op jit(solution)/shard_map/ppermute | solution.py:182
  25.4 21.3 %all-to-all-start = ((f32[16,2,24,128]{3,2,1,0:T(8,128)}), f32[16,2,24,128]{3,2,1,0:T(8,128)S(1)}, u32[]{:S(2)}, u32[]{:S(2)}) async-start(f32[16,2,24,128]{3,2,1,0:T(8,128)} %pad_maximum_fusion), calls=%async_computation | async-start | bytes 786432 | tf_op jit(solution)/shard_map/all_to_all | solution.py:143
  32.2 3.3 %collective-permute-start.6 = (f32[4,2,48,128]{3,2,1,0:T(8,128)S(1)}, f32[4,2,48,128]{3,2,1,0:T(8,128)S(1)}, u32[]{:S(2)}, u32[]{:S(2)}) collective-permute-start(f32[4,2,48,128]{3,2,1,0:T(8,128)S(1)} %pad_maximum_fusion.1.mine), channel_id=1, source_target_pairs={{0,1},{1,0},{2,3},{3,2},{4,5},{5,4},{6,7},{7,6},{8,9},{9,8},{10,11... | collective-permute-start | bytes 589832 | tf_op jit(solution)/shard_map/ppermute | solution.py:191
  36.1 15.2 %collective-permute-start.7 = (f32[8,48,128]{2,1,0:T(8,128)S(1)}, f32[8,48,128]{2,1,0:T(8,128)S(1)}, u32[]{:S(2)}, u32[]{:S(2)}) collective-permute-start(f32[8,48,128]{2,1,0:T(8,128)S(1)} %get-tuple-element.25.second), channel_id=1, source_target_pairs={{0,8},{8,16},{16,24},{1,9},{9,17},{17,25},{2,10},{10,18},{18,26},{... | collective-permute-start | bytes 589832 | tf_op jit(solution)/shard_map/ppermute | solution.py:197
  39.2 12.0 %collective-permute-start.8 = (f32[8,48,128]{2,1,0:T(8,128)S(1)}, f32[8,48,128]{2,1,0:T(8,128)S(1)}, u32[]{:S(2)}, u32[]{:S(2)}) collective-permute-start(f32[8,48,128]{2,1,0:T(8,128)S(1)} %get-tuple-element.26.first), channel_id=1, source_target_pairs={{8,0},{16,8},{24,16},{9,1},{17,9},{25,17},{10,2},{18,10},{26,18},{... | collective-permute-start | bytes 589832 | tf_op jit(solution)/shard_map/ppermute | solution.py:198
  46.7 7.5 %collective-permute-start.4 = (f32[2,4,2,24,128]{4,3,2,1,0:T(8,128)S(1)}, f32[2,4,2,24,128]{4,3,2,1,0:T(8,128)S(1)}, u32[]{:S(2)}, u32[]{:S(2)}) collective-permute-start(f32[2,4,2,24,128]{4,3,2,1,0:T(8,128)S(1)} %get-tuple-element.39), channel_id=1, source_target_pairs={{0,8},{8,16},{16,24},{1,9},{9,17},{17,25},{2,10},{10,18},{18,26},{... | collective-permute-start | bytes 589832 | tf_op jit(solution)/shard_map/ppermute | solution.py:200
  49.9 8.8 %collective-permute-start.5 = (f32[2,4,2,24,128]{4,3,2,1,0:T(8,128)S(1)}, f32[2,4,2,24,128]{4,3,2,1,0:T(8,128)S(1)}, u32[]{:S(2)}, u32[]{:S(2)}) collective-permute-start(f32[2,4,2,24,128]{4,3,2,1,0:T(8,128)S(1)} %get-tuple-element.38), channel_id=1, source_target_pairs={{8,0},{16,8},{24,16},{9,1},{17,9},{25,17},{10,2},{18,10},{26,18},{... | collective-permute-start | bytes 589832 | tf_op jit(solution)/shard_map/ppermute | solution.py:201
  62.4 6.1 %copy-start.3 = (s32[16,16,2]{1,2,0:T(2,128)S(1)}, s32[16,16,2]{1,2,0:T(2,128)}, u32[]{:S(2)}) copy-start(s32[16,16,2]{1,2,0:T(2,128)} %param.8) | copy-start | bytes 6148
  62.4 17.0 %all-to-all-start.1 = ((f32[8,2,32,128]{3,2,1,0:T(8,128)}), f32[8,2,32,128]{3,2,1,0:T(8,128)S(1)}, u32[]{:S(2)}, u32[]{:S(2)}) async-start(f32[8,2,32,128]{3,2,1,0:T(8,128)} %get-tuple-element.35), calls=%async_computation.1 | async-start | bytes 524288 | tf_op jit(solution)/shard_map/all_to_all | solution.py:143
  68.6 0.7 copy-start.4
  91.2 20.9 %all-to-all-start.3 = ((f32[16,2,24,128]{3,2,1,0:T(8,128)}), f32[16,2,24,128]{3,2,1,0:T(8,128)S(1)}, u32[]{:S(2)}, u32[]{:S(2)}) async-start(f32[16,2,24,128]{3,2,1,0:T(8,128)} %bitcast.13), calls=%async_computation.3 | async-start | bytes 786432 | tf_op jit(solution)/shard_map/all_to_all | solution.py:143

commit v6 on v5

--- a/solution.py
+++ b/solution.py
@@ -10,26 +10,49 @@
 BY = 4
 COURANT = 0.45
 
-RING = ("zh", "zl", "c")
+NEAR = ("zl", "c")
 SLAB = ("x", "zl", "c")
 CUTS = ("y", "zh")
-CHIPS = ("zh", "zl")
-RING_OFFSETS = (0, -1, 1, -2)
 
 VMEM = pl.BlockSpec(memory_space=pltpu.VMEM)
 SMEM = pl.BlockSpec(memory_space=pltpu.SMEM)
 PARAMS = pltpu.CompilerParams(vmem_limit_bytes=40 * 2**20)
 
 
-def gather_kernel(place, mine, other, first, second, kappa):
-    for part, source in ((place[0], mine), (1 - place[0], other)):
-        for i, offset in enumerate(RING_OFFSETS):
-            j = (place[1] + offset) & 3
-            for k in range(2):
-                kappa[4 * j + 2 * part + k] = source[i, k]
+def rows_kernel(place, kappa, *outs):
+    thick, grid_rows, lanes = kappa.shape
+    rows = outs[0].shape[1]
+    for m, out in enumerate(outs):
+        first = (place[0] ^ m) * (rows - 2 * FINE) - FINE
+        for r in range(0, rows, 8):
+            row = first + r
+            fits = jnp.where(row >= 0, jnp.where(row < grid_rows, 1, 0), 0)
+            start = pl.multiple_of(jnp.clip(row, 0, grid_rows - 8), 8)
+            keep = jnp.full((8, lanes), fits) == 1
+            for k in range(thick):
+                tile = kappa[k, pl.ds(start, 8), :]
+                out[k, r : r + 8] = jnp.where(keep, tile, 0.0)
+
+
+def gather_kernel(place, *refs):
+    *pieces, first, second, kappa = refs
+    for m, piece in enumerate(pieces):
+        j = place[0] ^ m
+        for k in range(2):
+            kappa[2 * j + k] = piece[k]
     for z in range(FINE):
         first[z] = kappa[z]
         second[z] = kappa[FINE + z]
+
+
+def spread_kernel(slab, out):
+    tiles, cuts = out.shape[0], slab.shape[0]
+    nothing = jnp.zeros(out.shape[1:2] + (8,) + out.shape[3:], jnp.float32)
+    for t in range(tiles):
+        out[t, :, 0:8] = slab[2 * t - 1, :, 8:16] if t > 0 else nothing
+        out[t, :, 8:24] = slab[2 * t]
+        out[t, :, 24:40] = slab[2 * t + 1]
+        out[t, :, 40:48] = slab[2 * t + 2, :, 0:8] if 2 * t + 2 < cuts else nothing
 
 
 def coefficient_kernel(
@@ -67,13 +90,12 @@
         down, here = up, after
 
 
-def fine_kernel(low, own, high, c0, zp, zm, yp, ym, xp, xm, out, ends, u):
+def fine_kernel(low, own, high, c0, zp, zm, yp, ym, xp, xm, out, u):
     depth, rows, lanes = u.shape
 
     def given(z):
         part, layer = (low, z) if z < 8 else (own, z - 8) if z < 24 else (high, z - 24)
-        near, far = part[0, layer // 2, layer % 2], part[1, layer // 2, layer % 2]
-        return jnp.concatenate([far[16:24], near[0:16], far[0:16], near[16:24]])
+        return part[layer // 2, layer % 2]
 
     for step in range(1, FINE + 1):
         at = given if step == 1 else (lambda z: u[z])
@@ -92,16 +114,13 @@
             if step < FINE:
                 u[z] = new
             else:
-                q, k = (z - 8) // 2, z % 2
-                out[q, k] = new[8 : rows - 8]
-                ends[0, q, k] = new[8:24]
-                ends[1, q, k] = new[24:40]
+                out[(z - 8) // 2, z % 2] = new[8 : rows - 8]
             below, here = here, above
 
 
 def pick_kernel(blocks, counts, me, tiles, out):
-    slices = out.shape[0]
-    upper = lax.broadcasted_iota(jnp.int32, out.shape[2:], 0) >= BY
+    slices, _, _, lanes = out.shape
+    upper = lax.broadcasted_iota(jnp.int32, (2 * BY, lanes), 0) >= BY
     for d in range(slices):
         count = counts[d * slices + me[0]]
         first = blocks[(d * slices + me[0]) * 2]
@@ -116,14 +135,8 @@
                 chosen = jnp.where(jnp.full(tile.shape, fits) == 1, tile, turned)
                 return jnp.where(jnp.full(tile.shape, live) == 1, chosen, 0.0)
 
-            out[d, k] = jnp.where(upper, half(second, 1), half(first, 0))
-
-
-def pack_kernel(ends, picked, out):
-    for h in range(2):
-        for q in range(8):
-            out[h, q, :, 0:16] = ends[h, q]
-            out[h, q, :, 16:24] = picked[q, h]
+            out[d, k, 0:16] = tiles[d // 2, k, 16 * (d % 2) : 16 * (d % 2) + 16]
+            out[d, k, 16:24] = jnp.where(upper, half(second, 1), half(first, 0))
 
 
 def advance_kernel(received, states, gain, new_states, fetched):
@@ -159,76 +172,66 @@
 
 def body(states, diffusivity, coarse_gain, read_block, read_count):
     slices, thick, own_rows, lanes = states.shape
-    y, zh = lax.axis_index("y"), lax.axis_index("zh")
-    x, c = lax.axis_index("x"), lax.axis_index("c")
-    ny, nx = lax.axis_size("y"), lax.axis_size("x")
-    me = lax.axis_index(RING)
-    cut = lax.axis_index(CUTS)
-    tile_rows = 2 * own_rows
+    x, near, cut = lax.axis_index("x"), lax.axis_index(NEAR), lax.axis_index(CUTS)
+    nx, tiles = lax.axis_size("x"), lax.axis_size(NEAR)
+    tile_rows = diffusivity.shape[1] // tiles
     wide = tile_rows + 2 * FINE
-    half = slices // 2
+    deep = tiles * thick
     x_up = [(i, i + 1) for i in range(nx - 1)]
     x_down = [(i + 1, i) for i in range(nx - 1)]
 
-    edge_rows = lax.dynamic_slice_in_dim(states, zh * (own_rows - FINE), FINE, 2)
-    pairs = [(i, i + 2) for i in range(1, 2 * ny - 2, 2)]
-    pairs += [(i, i - 2) for i in range(2, 2 * ny, 2)]
-    side_rows = lax.ppermute(edge_rows, CUTS, pairs)
-
-    padded = jnp.pad(diffusivity, ((0, 0), (FINE, FINE), (0, 0)))
-    kappa = lax.dynamic_slice_in_dim(padded, y * tile_rows, wide, 1)
-    around = lax.axis_size(CHIPS)
-    ring = [
-        lax.ppermute(kappa, CHIPS, [(i, (i - offset) % around) for i in range(around)])
-        for offset in RING_OFFSETS[1:]
+    place = near[None]
+    sends = call(rows_kernel, "rows", [(thick, wide, lanes)] * tiles, [SMEM, VMEM])(
+        place, diffusivity
+    )
+    pieces = [
+        lax.ppermute(send, NEAR, [(i, i ^ m) for i in range(tiles)]) if m else send
+        for m, send in enumerate(sends)
     ]
 
-    block = jnp.concatenate([states, side_rows], axis=2)
-    block, kappa, *ring = lax.optimization_barrier((block, kappa, *ring))
-    own = exchange(block, RING).reshape(2, half, thick, own_rows + FINE, lanes)
-
-    mine = jnp.stack([kappa, *ring])
-    other = lax.ppermute(mine, "c", [(0, 1), (1, 0)])
-    place = jnp.stack([c, lax.axis_index("zl")])
+    slab = exchange(states, CUTS)
+    early = 7
+    slab, *pieces[:early] = lax.optimization_barrier((slab, *pieces[:early]))
+    (spread,) = call(
+        spread_kernel, "spread", [(tiles, thick, wide, lanes)], [VMEM]
+    )(slab)
+    own = exchange(spread, NEAR)
+    low = lax.ppermute(own[tiles // 2 :], "x", x_up)
+    high = lax.ppermute(own[: tiles // 2], "x", x_down)
+
     part = (FINE, wide, lanes)
     k_first, k_second = call(
-        gather_kernel, "gather", [part] * 2, [SMEM, VMEM, VMEM], [(2 * FINE, *part[1:])]
-    )(place, mine, other)
+        gather_kernel,
+        "gather",
+        [part] * 2,
+        [SMEM] + [VMEM] * tiles,
+        [(deep, wide, lanes)],
+    )(place, *pieces)
     k_low = lax.ppermute(k_second, "x", x_up)
     k_high = lax.ppermute(k_first, "x", x_down)
 
-    low = lax.ppermute(own[:, half // 2 :], "x", x_up)
-    high = lax.ppermute(own[:, : half // 2], "x", x_down)
-
-    flags = [y > 0, y < ny - 1, x > 0, x < nx - 1]
+    flags = [near > 0, near < tiles - 1, x > 0, x < nx - 1]
     edge = jnp.stack([flag.astype(jnp.int32) for flag in flags])
-    deep = half * thick
     region = (deep + 2 * FINE, wide, lanes)
     coefficients = call(
         coefficient_kernel, "coefficients", [region] * 7, [SMEM] + [VMEM] * 4
     )(edge, k_low, k_first, k_second, k_high)
-    fine, ends = call(
+    (fine,) = call(
         fine_kernel,
         "fine",
-        [(ny, deep // ny, tile_rows, lanes), (2, half, thick, own_rows, lanes)],
+        [(tiles, thick, tile_rows, lanes)],
         [VMEM] * 10,
         [region],
     )(low, own, high, *coefficients)
 
-    tiles = exchange(fine, "y")
-    (picked,) = call(
+    rows = exchange(fine, NEAR)
+    (payload,) = call(
         pick_kernel,
         "pick",
-        [(slices, thick, 2 * BY, lanes)],
+        [(slices, thick, own_rows + 2 * BY, lanes)],
         [SMEM, SMEM, SMEM, VMEM],
-    )(read_block.reshape(-1), read_count.reshape(-1), me[None], tiles)
-    picked = exchange(picked, "y").reshape(ny, 2, thick, 2 * BY, lanes)
-    (payload,) = call(
-        pack_kernel, "pack", [(2, half, thick, own_rows + 2 * BY, lanes)], [VMEM] * 2
-    )(ends, picked)
-    received = exchange(
-        payload.reshape(slices, thick, own_rows + 2 * BY, lanes), RING
-    )
+    )(read_block.reshape(-1), read_count.reshape(-1), cut[None], rows)
+    received = exchange(payload, CUTS)
     gain = lax.dynamic_slice_in_dim(coarse_gain, cut * own_rows, own_rows, 1)
     new_states, fetched = call(
         advance_kernel,

time: 114 us -> 124 us (1.088)
  starting transfers between devices: 48.6 us -> 74.5 us
  blocking collectives: 10.3 us -> 0 us
  waiting for transfers between devices: 42.4 us -> 37.6 us
    all_to_all x3 -> x4, starting transfers between devices: 19.2 us -> 39.7 us  [exchange(): return lax.all_to_all(value, axes, 0, 0, tiled=True)]
    all_to_all x1 -> x0, blocking collectives: 10.3 us -> none  [exchange(): return lax.all_to_all(value, axes, 0, 0, tiled=True)]
    all_to_all x3 -> x4, waiting for transfers between devices: 30.7 us -> 24.4 us  [exchange(): return lax.all_to_all(value, axes, 0, 0, tiled=True)]
    ppermute x7 -> x9, starting transfers between devices: 25 us -> 29.5 us  [the longest x7 25.1 us: body(): lax.ppermute(send, NEAR, [(i, i ^ m) for i in range(tiles)])]
    ppermute x7 -> x9, waiting for transfers between devices: 11.7 us -> 13.2 us  [the longest x7 8.61 us: body(): lax.ppermute(send, NEAR, [(i, i ^ m) for i in range(tiles)])]
    pallas_call x4 -> x5, Pallas kernels: 5.86 us -> 5.66 us  [the longest x1 3.17 us: body(): call(fine_kernel, 'fine', [(tiles, thick, tile_rows, lanes)], [VMEM] * 10...]
  transfers between devices with their start and end apart: 12 -> 15, of which waited for: 7 -> 7; matrix products, arithmetic and copies ran while one was open for 1% -> 0% of each run, Pallas kernels for 2% -> 1%
where the time goes in v6:
time: 124 us; the launch traced here: 122 us
  starting transfers between devices  74.5 us (60%)
  waiting for transfers between devices  37.6 us (30%)
  Pallas kernels  7.7 us (6%)
    all_to_all x4, starting transfers between devices, exchange(): return lax.all_to_all(value, axes, 0, 0, tiled=True)  39.7 us
    ppermute x7, starting transfers between devices, body(): lax.ppermute(send, NEAR, [(i, i ^ m) for i in range(tiles)])  25.1 us
    all_to_all x4, waiting for transfers between devices, exchange(): return lax.all_to_all(value, axes, 0, 0, tiled=True)  24.4 us
    ppermute x7, waiting for transfers between devices, body(): lax.ppermute(send, NEAR, [(i, i ^ m) for i in range(tiles)])  8.61 us
    ppermute x1, starting transfers between devices, body(): k_low = lax.ppermute(k_second, 'x', x_up)  4 us
    pallas_call x1, Pallas kernels, body(): call(fine_kernel, 'fine', [(tiles, thick, tile_rows, lanes)], [VMEM] * 10...  3.17 us
    ppermute x1, starting transfers between devices, body(): low = lax.ppermute(own[tiles // 2:], 'x', x_up)  3.12 us
  transfers between devices with their start and end apart: 15, of which 7 were waited for; matrix products, arithmetic and copies ran while one was open for 0% of the time, Pallas kernels for 1%

profile of v6, /device:TPU:1, one launch (start us, length us, event | category | flops | bytes accessed | tf_op | source)
XLA Modules:
  0.0 121.8 jit_solution(5184160901772436617)
XLA Ops:
  0.7 16.3 %all-to-all-start = ((f32[16,2,16,128]{3,2,1,0:T(8,128)}), f32[16,2,16,128]{3,2,1,0:T(8,128)S(1)}, u32[]{:S(2)}, u32[]{:S(2)}) async-start(f32[16,2,16,128]{3,2,1,0:T(8,128)} %states.1), calls=%async_computation | async-start | bytes 524288 | tf_op jit(solution)/shard_map/all_to_all | solution.py:156
  17.0 0.2 rows.1
  17.2 2.9 %collective-permute-start = (f32[2,48,128]{2,1,0:T(8,128)S(1)}, f32[2,48,128]{2,1,0:T(8,128)S(1)}, u32[]{:S(2)}, u32[]{:S(2)}) collective-permute-start(f32[2,48,128]{2,1,0:T(8,128)S(1)} %get-tuple-element.30), channel_id=1, source_target_pairs={{0,1},{1,0},{2,3},{3,2},{4,5},{5,4},{6,7},{7,6},{8,9},{9,8},{10,11... | collective-permute-start | bytes 147464 | tf_op jit(solution)/shard_map/ppermute | solution.py:188
  20.1 3.1 %collective-permute-start.1 = (f32[2,48,128]{2,1,0:T(8,128)S(1)}, f32[2,48,128]{2,1,0:T(8,128)S(1)}, u32[]{:S(2)}, u32[]{:S(2)}) collective-permute-start(f32[2,48,128]{2,1,0:T(8,128)S(1)} %get-tuple-element.31), channel_id=1, source_target_pairs={{0,2},{1,3},{2,0},{3,1},{4,6},{5,7},{6,4},{7,5},{8,10},{9,11},{10,... | collective-permute-start | bytes 147464 | tf_op jit(solution)/shard_map/ppermute | solution.py:188
  23.2 2.4 %collective-permute-start.2 = (f32[2,48,128]{2,1,0:T(8,128)S(1)}, f32[2,48,128]{2,1,0:T(8,128)S(1)}, u32[]{:S(2)}, u32[]{:S(2)}) collective-permute-start(f32[2,48,128]{2,1,0:T(8,128)S(1)} %get-tuple-element.32), channel_id=1, source_target_pairs={{0,3},{1,2},{2,1},{3,0},{4,7},{5,6},{6,5},{7,4},{8,11},{9,10},{10,... | collective-permute-start | bytes 147464 | tf_op jit(solution)/shard_map/ppermute | solution.py:188
  25.6 4.0 %collective-permute-start.3 = (f32[2,48,128]{2,1,0:T(8,128)S(1)}, f32[2,48,128]{2,1,0:T(8,128)S(1)}, u32[]{:S(2)}, u32[]{:S(2)}) collective-permute-start(f32[2,48,128]{2,1,0:T(8,128)S(1)} %get-tuple-element.33), channel_id=1, source_target_pairs={{0,4},{1,5},{2,6},{3,7},{4,0},{5,1},{6,2},{7,3},{8,12},{9,13},{10,... | collective-permute-start | bytes 147464 | tf_op jit(solution)/shard_map/ppermute | solution.py:188
  29.6 2.6 %collective-permute-start.4 = (f32[2,48,128]{2,1,0:T(8,128)S(1)}, f32[2,48,128]{2,1,0:T(8,128)S(1)}, u32[]{:S(2)}, u32[]{:S(2)}) collective-permute-start(f32[2,48,128]{2,1,0:T(8,128)S(1)} %get-tuple-element.34), channel_id=1, source_target_pairs={{0,5},{1,4},{2,7},{3,6},{4,1},{5,0},{6,3},{7,2},{8,13},{9,12},{10,... | collective-permute-start | bytes 147464 | tf_op jit(solution)/shard_map/ppermute | solution.py:188
  32.2 4.9 %collective-permute-start.5 = (f32[2,48,128]{2,1,0:T(8,128)S(1)}, f32[2,48,128]{2,1,0:T(8,128)S(1)}, u32[]{:S(2)}, u32[]{:S(2)}) collective-permute-start(f32[2,48,128]{2,1,0:T(8,128)S(1)} %get-tuple-element.35), channel_id=1, source_target_pairs={{0,6},{1,7},{2,4},{3,5},{4,2},{5,3},{6,0},{7,1},{8,14},{9,15},{10,... | collective-permute-start | bytes 147464 | tf_op jit(solution)/shard_map/ppermute | solution.py:188
  37.1 0.2 collective-permute-done.4.refs_5_
  37.3 1.9 %collective-permute-done.5.refs_6_ = f32[2,48,128]{2,1,0:T(8,128)S(1)} collective-permute-done((f32[2,48,128]{2,1,0:T(8,128)S(1)}, f32[2,48,128]{2,1,0:T(8,128)S(1)}, u32[]{:S(2)}, u32[]{:S(2)}) %collective-permute-start.5) | collective-permute-done | bytes 49184 | tf_op jit(solution)/shard_map/ppermute | solution.py:188
  39.2 0.8 spread.1
  40.0 5.4 %all-to-all-start.1 = ((f32[8,2,48,128]{3,2,1,0:T(8,128)}), f32[8,2,48,128]{3,2,1,0:T(8,128)S(1)}, u32[]{:S(2)}, u32[]{:S(2)}) async-start(f32[8,2,48,128]{3,2,1,0:T(8,128)} %spread.1), calls=%async_computation.1 | async-start | bytes 786432 | tf_op jit(solution)/shard_map/all_to_all | solution.py:156
  45.4 5.3 %collective-permute-start.8 = (f32[2,48,128]{2,1,0:T(8,128)S(1)}, f32[2,48,128]{2,1,0:T(8,128)S(1)}, u32[]{:S(2)}, u32[]{:S(2)}) collective-permute-start(f32[2,48,128]{2,1,0:T(8,128)S(1)} %get-tuple-element.44), channel_id=1, source_target_pairs={{0,7},{1,6},{2,5},{3,4},{4,3},{5,2},{6,1},{7,0},{8,15},{9,14},{10,... | collective-permute-start | bytes 147464 | tf_op jit(solution)/shard_map/ppermute | solution.py:188
  50.7 6.5 %collective-permute-done.8.refs_7_ = f32[2,48,128]{2,1,0:T(8,128)S(1)} collective-permute-done((f32[2,48,128]{2,1,0:T(8,128)S(1)}, f32[2,48,128]{2,1,0:T(8,128)S(1)}, u32[]{:S(2)}, u32[]{:S(2)}) %collective-permute-start.8) | collective-permute-done | bytes 49184 | tf_op jit(solution)/shard_map/ppermute | solution.py:188
  57.3 1.3 %collective-permute-start.10 = (f32[8,48,128]{2,1,0:T(8,128)S(1)}, f32[8,48,128]{2,1,0:T(8,128)S(1)}, u32[]{:S(2)}, u32[]{:S(2)}) collective-permute-start(f32[8,48,128]{2,1,0:T(8,128)S(1)} %get-tuple-element.46.first), channel_id=1, source_target_pairs={{8,0},{16,8},{24,16},{9,1},{17,9},{25,17},{10,2},{18,10},{26,18},{... | collective-permute-start | bytes 589832 | tf_op jit(solution)/shard_map/ppermute | solution.py:211
  58.6 4.0 %collective-permute-start.9 = (f32[8,48,128]{2,1,0:T(8,128)S(1)}, f32[8,48,128]{2,1,0:T(8,128)S(1)}, u32[]{:S(2)}, u32[]{:S(2)}) collective-permute-start(f32[8,48,128]{2,1,0:T(8,128)S(1)} %get-tuple-element.45.second), channel_id=1, source_target_pairs={{0,8},{8,16},{16,24},{1,9},{9,17},{17,25},{2,10},{10,18},{18,26},{... | collective-permute-start | bytes 589832 | tf_op jit(solution)/shard_map/ppermute | solution.py:210
  62.6 3.1 %collective-permute-start.6 = (f32[4,2,48,128]{3,2,1,0:T(8,128)S(1)}, f32[4,2,48,128]{3,2,1,0:T(8,128)S(1)}, u32[]{:S(2)}, u32[]{:S(2)}) collective-permute-start(f32[4,2,48,128]{3,2,1,0:T(8,128)S(1)} %get-tuple-element.57), channel_id=1, source_target_pairs={{0,8},{8,16},{16,24},{1,9},{9,17},{17,25},{2,10},{10,18},{18,26},{... | collective-permute-start | bytes 589832 | tf_op jit(solution)/shard_map/ppermute | solution.py:199
  65.7 1.3 %collective-permute-start.7 = (f32[4,2,48,128]{3,2,1,0:T(8,128)S(1)}, f32[4,2,48,128]{3,2,1,0:T(8,128)S(1)}, u32[]{:S(2)}, u32[]{:S(2)}) collective-permute-start(f32[4,2,48,128]{3,2,1,0:T(8,128)S(1)} %get-tuple-element.56), channel_id=1, source_target_pairs={{8,0},{16,8},{24,16},{9,1},{17,9},{25,17},{10,2},{18,10},{26,18},{... | collective-permute-start | bytes 589832 | tf_op jit(solution)/shard_map/ppermute | solution.py:200
  67.1 1.3 %coefficients.1 = (f32[32,48,128]{2,1,0:T(8,128)S(1)}, f32[32,48,128]{2,1,0:T(8,128)S(1)}, f32[32,48,128]{2,1,0:T(8,128)S(1)}, f32[32,48,128]{2,1,0:T(8,128)S(1)...) custom-call(s32[4]{0:T(128)S(1)} %add_convert_fusion.edge, ...), custom_call_target="tpu_custom_call" | custom-call | tf_op jit(solution)/shard_map/coefficients/pallas_call | solution.py:216
  68.4 2.1 %collective-permute-done.6.low = f32[4,2,48,128]{3,2,1,0:T(8,128)S(1)} collective-permute-done((f32[4,2,48,128]{3,2,1,0:T(8,128)S(1)}, f32[4,2,48,128]{3,2,1,0:T(8,128)S(1)}, u32[]{:S(2)}, u32[]{:S(2)}) %collective-permute-start.6) | collective-permute-done | bytes 196640 | tf_op jit(solution)/shard_map/ppermute | solution.py:199
  70.5 2.4 %collective-permute-done.7.high = f32[4,2,48,128]{3,2,1,0:T(8,128)S(1)} collective-permute-done((f32[4,2,48,128]{3,2,1,0:T(8,128)S(1)}, f32[4,2,48,128]{3,2,1,0:T(8,128)S(1)}, u32[]{:S(2)}, u32[]{:S(2)}) %collective-permute-start.7) | collective-permute-done | bytes 196640 | tf_op jit(solution)/shard_map/ppermute | solution.py:200
  73.0 3.2 %fine.1 = f32[8,2,32,128]{3,2,1,0:T(8,128)} custom-call(f32[4,2,48,128]{3,2,1,0:T(8,128)S(1)} %collective-permute-done.6.low, f32[8,2,48,128]{3,2,1,0:T(8,128)S(1)} %all-to-all-done.1.own, f32[4,2,48,128]{3,2,1,0:T(8,128)S(1)} %collective-permute-done.7.high, f32[32,48,128]{2,1,0:T(8,128)S(1)} %get-tuple-element.47.c0, ...), custom_call_target="tpu_custom_call" | custom-call | tf_op jit(solution)/shard_map/fine/pallas_call | solution.py:219
  76.1 6.1 %all-to-all-start.2 = ((f32[8,2,32,128]{3,2,1,0:T(8,128)}), f32[8,2,32,128]{3,2,1,0:T(8,128)S(1)}, u32[]{:S(2)}, u32[]{:S(2)}) async-start(f32[8,2,32,128]{3,2,1,0:T(8,128)} %fine.1), calls=%async_computation.2 | async-start | bytes 524288 | tf_op jit(solution)/shard_map/all_to_all | solution.py:156
  82.3 0.2 copy.7
  82.4 0.1 reshape.10.blocks
  82.6 0.6 copy-done.4
  83.1 0.1 reshape.11.counts
  83.2 7.8 %all-to-all-done.2.tiles = f32[8,2,32,128]{3,2,1,0:T(8,128)S(1)} async-done(((f32[8,2,32,128]{3,2,1,0:T(8,128)}), f32[8,2,32,128]{3,2,1,0:T(8,128)S(1)}, u32[]{:S(2)}, u32[]{:S(2)}) %all-to-all-start.2) | async-done | bytes 262176 | tf_op jit(solution)/shard_map/all_to_all | solution.py:156
  91.0 1.5 %pick.1 = f32[16,2,24,128]{3,2,1,0:T(8,128)} custom-call(s32[512]{0:T(512)S(1)} %reshape.10.blocks, s32[256]{0:T(256)S(1)} %reshape.11.counts, s32[1]{0:T(128)} %bitcast.me, f32[8,2,32,128]{3,2,1,0:T(8,128)S(1)} %all-to-all-done.2.tiles), custom_call_target="tpu_custom_call" | custom-call | tf_op jit(solution)/shard_map/pick/pallas_call | solution.py:228
  92.4 11.9 %all-to-all-start.3 = ((f32[16,2,24,128]{3,2,1,0:T(8,128)}), f32[16,2,24,128]{3,2,1,0:T(8,128)S(1)}, u32[]{:S(2)}, u32[]{:S(2)}) async-start(f32[16,2,24,128]{3,2,1,0:T(8,128)} %pick.1), calls=%async_computation.3 | async-start | bytes 786432 | tf_op jit(solution)/shard_map/all_to_all | solution.py:156
  104.3 16.7 %all-to-all-done.3.received = f32[16,2,24,128]{3,2,1,0:T(8,128)S(1)} async-done(((f32[16,2,24,128]{3,2,1,0:T(8,128)}), f32[16,2,24,128]{3,2,1,0:T(8,128)S(1)}, u32[]{:S(2)}, u32[]{:S(2)}) %all-to-all-start.3) | async-done | bytes 393248 | tf_op jit(solution)/shard_map/all_to_all | solution.py:156
  121.0 0.8 advance.1
  (21 shorter events, 0.2 us)
Async XLA Ops:
  0.6 103.7 %copy-start = (f32[2,256,128]{2,1,0:T(8,128)S(1)}, f32[2,256,128]{2,1,0:T(8,128)}, u32[]{:S(2)}) copy-start(f32[2,256,128]{2,1,0:T(8,128)} %param.7) | copy-start | bytes 786436
  0.6 16.4 %copy-start.2 = (f32[2,256,128]{2,1,0:T(8,128)S(1)}, f32[2,256,128]{2,1,0:T(8,128)}, u32[]{:S(2)}) copy-start(f32[2,256,128]{2,1,0:T(8,128)} %kappa.1) | copy-start | bytes 786436
  0.7 38.6 %all-to-all-start = ((f32[16,2,16,128]{3,2,1,0:T(8,128)}), f32[16,2,16,128]{3,2,1,0:T(8,128)S(1)}, u32[]{:S(2)}, u32[]{:S(2)}) async-start(f32[16,2,16,128]{3,2,1,0:T(8,128)} %states.1), calls=%async_computation | async-start | bytes 524288 | tf_op jit(solution)/shard_map/all_to_all | solution.py:156
  17.2 14.9 %collective-permute-start = (f32[2,48,128]{2,1,0:T(8,128)S(1)}, f32[2,48,128]{2,1,0:T(8,128)S(1)}, u32[]{:S(2)}, u32[]{:S(2)}) collective-permute-start(f32[2,48,128]{2,1,0:T(8,128)S(1)} %get-tuple-element.30), channel_id=1, source_target_pairs={{0,1},{1,0},{2,3},{3,2},{4,5},{5,4},{6,7},{7,6},{8,9},{9,8},{10,11... | collective-permute-start | bytes 147464 | tf_op jit(solution)/shard_map/ppermute | solution.py:188
  20.1 17.0 %collective-permute-start.1 = (f32[2,48,128]{2,1,0:T(8,128)S(1)}, f32[2,48,128]{2,1,0:T(8,128)S(1)}, u32[]{:S(2)}, u32[]{:S(2)}) collective-permute-start(f32[2,48,128]{2,1,0:T(8,128)S(1)} %get-tuple-element.31), channel_id=1, source_target_pairs={{0,2},{1,3},{2,0},{3,1},{4,6},{5,7},{6,4},{7,5},{8,10},{9,11},{10,... | collective-permute-start | bytes 147464 | tf_op jit(solution)/shard_map/ppermute | solution.py:188
  23.2 13.9 %collective-permute-start.2 = (f32[2,48,128]{2,1,0:T(8,128)S(1)}, f32[2,48,128]{2,1,0:T(8,128)S(1)}, u32[]{:S(2)}, u32[]{:S(2)}) collective-permute-start(f32[2,48,128]{2,1,0:T(8,128)S(1)} %get-tuple-element.32), channel_id=1, source_target_pairs={{0,3},{1,2},{2,1},{3,0},{4,7},{5,6},{6,5},{7,4},{8,11},{9,10},{10,... | collective-permute-start | bytes 147464 | tf_op jit(solution)/shard_map/ppermute | solution.py:188
  25.6 11.5 %collective-permute-start.3 = (f32[2,48,128]{2,1,0:T(8,128)S(1)}, f32[2,48,128]{2,1,0:T(8,128)S(1)}, u32[]{:S(2)}, u32[]{:S(2)}) collective-permute-start(f32[2,48,128]{2,1,0:T(8,128)S(1)} %get-tuple-element.33), channel_id=1, source_target_pairs={{0,4},{1,5},{2,6},{3,7},{4,0},{5,1},{6,2},{7,3},{8,12},{9,13},{10,... | collective-permute-start | bytes 147464 | tf_op jit(solution)/shard_map/ppermute | solution.py:188
  29.6 7.7 %collective-permute-start.4 = (f32[2,48,128]{2,1,0:T(8,128)S(1)}, f32[2,48,128]{2,1,0:T(8,128)S(1)}, u32[]{:S(2)}, u32[]{:S(2)}) collective-permute-start(f32[2,48,128]{2,1,0:T(8,128)S(1)} %get-tuple-element.34), channel_id=1, source_target_pairs={{0,5},{1,4},{2,7},{3,6},{4,1},{5,0},{6,3},{7,2},{8,13},{9,12},{10,... | collective-permute-start | bytes 147464 | tf_op jit(solution)/shard_map/ppermute | solution.py:188
  32.2 7.1 %collective-permute-start.5 = (f32[2,48,128]{2,1,0:T(8,128)S(1)}, f32[2,48,128]{2,1,0:T(8,128)S(1)}, u32[]{:S(2)}, u32[]{:S(2)}) collective-permute-start(f32[2,48,128]{2,1,0:T(8,128)S(1)} %get-tuple-element.35), channel_id=1, source_target_pairs={{0,6},{1,7},{2,4},{3,5},{4,2},{5,3},{6,0},{7,1},{8,14},{9,15},{10,... | collective-permute-start | bytes 147464 | tf_op jit(solution)/shard_map/ppermute | solution.py:188
  40.0 22.6 %all-to-all-start.1 = ((f32[8,2,48,128]{3,2,1,0:T(8,128)}), f32[8,2,48,128]{3,2,1,0:T(8,128)S(1)}, u32[]{:S(2)}, u32[]{:S(2)}) async-start(f32[8,2,48,128]{3,2,1,0:T(8,128)} %spread.1), calls=%async_computation.1 | async-start | bytes 786432 | tf_op jit(solution)/shard_map/all_to_all | solution.py:156
  45.4 11.8 %collective-permute-start.8 = (f32[2,48,128]{2,1,0:T(8,128)S(1)}, f32[2,48,128]{2,1,0:T(8,128)S(1)}, u32[]{:S(2)}, u32[]{:S(2)}) collective-permute-start(f32[2,48,128]{2,1,0:T(8,128)S(1)} %get-tuple-element.44), channel_id=1, source_target_pairs={{0,7},{1,6},{2,5},{3,4},{4,3},{5,2},{6,1},{7,0},{8,15},{9,14},{10,... | collective-permute-start | bytes 147464 | tf_op jit(solution)/shard_map/ppermute | solution.py:188
  57.3 9.9 %collective-permute-start.10 = (f32[8,48,128]{2,1,0:T(8,128)S(1)}, f32[8,48,128]{2,1,0:T(8,128)S(1)}, u32[]{:S(2)}, u32[]{:S(2)}) collective-permute-start(f32[8,48,128]{2,1,0:T(8,128)S(1)} %get-tuple-element.46.first), channel_id=1, source_target_pairs={{8,0},{16,8},{24,16},{9,1},{17,9},{25,17},{10,2},{18,10},{26,18},{... | collective-permute-start | bytes 589832 | tf_op jit(solution)/shard_map/ppermute | solution.py:211
  58.6 8.6 %collective-permute-start.9 = (f32[8,48,128]{2,1,0:T(8,128)S(1)}, f32[8,48,128]{2,1,0:T(8,128)S(1)}, u32[]{:S(2)}, u32[]{:S(2)}) collective-permute-start(f32[8,48,128]{2,1,0:T(8,128)S(1)} %get-tuple-element.45.second), channel_id=1, source_target_pairs={{0,8},{8,16},{16,24},{1,9},{9,17},{17,25},{2,10},{10,18},{18,26},{... | collective-permute-start | bytes 589832 | tf_op jit(solution)/shard_map/ppermute | solution.py:210
  62.6 7.9 %collective-permute-start.6 = (f32[4,2,48,128]{3,2,1,0:T(8,128)S(1)}, f32[4,2,48,128]{3,2,1,0:T(8,128)S(1)}, u32[]{:S(2)}, u32[]{:S(2)}) collective-permute-start(f32[4,2,48,128]{3,2,1,0:T(8,128)S(1)} %get-tuple-element.57), channel_id=1, source_target_pairs={{0,8},{8,16},{16,24},{1,9},{9,17},{17,25},{2,10},{10,18},{18,26},{... | collective-permute-start | bytes 589832 | tf_op jit(solution)/shard_map/ppermute | solution.py:199
  65.7 7.2 %collective-permute-start.7 = (f32[4,2,48,128]{3,2,1,0:T(8,128)S(1)}, f32[4,2,48,128]{3,2,1,0:T(8,128)S(1)}, u32[]{:S(2)}, u32[]{:S(2)}) collective-permute-start(f32[4,2,48,128]{3,2,1,0:T(8,128)S(1)} %get-tuple-element.56), channel_id=1, source_target_pairs={{8,0},{16,8},{24,16},{9,1},{17,9},{25,17},{10,2},{18,10},{26,18},{... | collective-permute-start | bytes 589832 | tf_op jit(solution)/shard_map/ppermute | solution.py:200
  76.1 6.1 %copy-start.3 = (s32[16,16,2]{1,2,0:T(2,128)S(1)}, s32[16,16,2]{1,2,0:T(2,128)}, u32[]{:S(2)}) copy-start(s32[16,16,2]{1,2,0:T(2,128)} %param.8) | copy-start | bytes 6148
  76.1 14.8 %all-to-all-start.2 = ((f32[8,2,32,128]{3,2,1,0:T(8,128)}), f32[8,2,32,128]{3,2,1,0:T(8,128)S(1)}, u32[]{:S(2)}, u32[]{:S(2)}) async-start(f32[8,2,32,128]{3,2,1,0:T(8,128)} %fine.1), calls=%async_computation.2 | async-start | bytes 524288 | tf_op jit(solution)/shard_map/all_to_all | solution.py:156
  82.4 0.7 copy-start.4
  92.4 28.6 %copy-start.1 = (f32[16,2,16,128]{3,2,1,0:T(8,128)S(1)}, f32[16,2,16,128]{3,2,1,0:T(8,128)}, u32[]{:S(2)}) copy-start(f32[16,2,16,128]{3,2,1,0:T(8,128)} %states.1) | copy-start | bytes 786436
  92.4 28.6 %all-to-all-start.3 = ((f32[16,2,24,128]{3,2,1,0:T(8,128)}), f32[16,2,24,128]{3,2,1,0:T(8,128)S(1)}, u32[]{:S(2)}, u32[]{:S(2)}) async-start(f32[16,2,24,128]{3,2,1,0:T(8,128)} %pick.1), calls=%async_computation.3 | async-start | bytes 786432 | tf_op jit(solution)/shard_map/all_to_all | solution.py:156

commit v7 on v2

--- a/solution.py
+++ b/solution.py
@@ -13,6 +13,7 @@
 RING = ("zh", "zl", "c")
 SLAB = ("x", "zl", "c")
 CUTS = ("y", "zh")
+NEAR = ("zl", "c")
 
 VMEM = pl.BlockSpec(memory_space=pltpu.VMEM)
 SMEM = pl.BlockSpec(memory_space=pltpu.SMEM)
@@ -30,15 +31,13 @@
                 out[layer, 40:48] = north[start + j, k]
 
 
-def coefficient_kernel(edge, mine, other, c0, zp, zm, yp, ym, xp, xm, kappa):
-    depth, rows, lanes = kappa.shape
-    core = edge[4]
-    for part, source in ((core, mine), (1 - core, other)):
-        for j in range(4):
-            side = 4 * (j - 2) if j >= 2 else 24 + 4 * j
-            for k in range(2):
-                kappa[8 + 4 * j + 2 * part + k] = source[j, 0, k]
-                kappa[side + 2 * part + k] = source[j, 1, k]
+def coefficient_kernel(
+    edge, low, own, high, c0, zp, zm, yp, ym, xp, xm
+):
+    depth, rows, lanes = c0.shape
+
+    def at(z):
+        return low[z] if z < 8 else own[z - 8] if z < 24 else high[z - 24]
 
     row = lax.broadcasted_iota(jnp.int32, (rows, lanes), 0)
     lane = lax.broadcasted_iota(jnp.int32, (rows, lanes), 1)
@@ -49,11 +48,11 @@
     above = inside * edge[3].astype(jnp.float32)
     not_first = jnp.where(lane == 0, 0.0, 1.0)
     not_last = jnp.where(lane == lanes - 1, 0.0, 1.0)
+    down, here = 0.5 * (at(0) + at(1)), at(1)
     for z in range(1, depth - 1):
         mask = below if z < 8 else above if z >= depth - 8 else inside
-        here = kappa[z]
-        up = 0.5 * (here + kappa[z + 1])
-        down = 0.5 * (here + kappa[z - 1])
+        after = at(z + 1)
+        up = 0.5 * (here + after)
         north = 0.5 * (here + pltpu.roll(here, rows - 1, 0))
         south = 0.5 * (here + pltpu.roll(here, 1, 0))
         east = 0.5 * (here + pltpu.roll(here, lanes - 1, 1) * not_last)
@@ -66,13 +65,18 @@
         ym[z] = south * mask
         xp[z] = east * (mask * not_last)
         xm[z] = west * (mask * not_first)
+        down, here = up, after
 
 
 def fine_kernel(low, first, second, high, c0, zp, zm, yp, ym, xp, xm, out, ends, u):
     depth, rows, lanes = u.shape
     parts = (low, first, second, high)
+
+    def given(z):
+        return parts[z // 8][z % 8]
+
     for step in range(1, FINE + 1):
-        at = (lambda z: parts[z // 8][z % 8]) if step == 1 else (lambda z: u[z])
+        at = given if step == 1 else (lambda z: u[z])
         below, here = at(step - 1), at(step)
         for z in range(step, depth - step):
             above = at(z + 1)
@@ -155,42 +159,42 @@
 
 def body(states, diffusivity, coarse_gain, read_block, read_count):
     slices, thick, own_rows, lanes = states.shape
-    y, x, c = lax.axis_index("y"), lax.axis_index("x"), lax.axis_index("c")
+    y = lax.axis_index("y")
+    x = lax.axis_index("x")
     ny, nx = lax.axis_size("y"), lax.axis_size("x")
     me = lax.axis_index(RING)
     cut = lax.axis_index(CUTS)
     tile_rows = 2 * own_rows
     wide = tile_rows + 2 * FINE
     half = slices // 2
+    x_up = [(i, i + 1) for i in range(nx - 1)]
+    x_down = [(i + 1, i) for i in range(nx - 1)]
+
     y_up = [(i, i + 1) for i in range(ny - 1)]
     y_down = [(i + 1, i) for i in range(ny - 1)]
-    x_up = [(i, i + 1) for i in range(nx - 1)]
-    x_down = [(i + 1, i) for i in range(nx - 1)]
 
     padded = jnp.pad(diffusivity, ((0, 0), (FINE, FINE), (0, 0)))
     kappa = lax.dynamic_slice_in_dim(padded, y * tile_rows, wide, 1)
-    near = [((i, j), (i + 1, j)) for i in range(nx - 1) for j in (2, 3)]
-    near += [((i, j), (i - 1, j)) for i in range(1, nx) for j in (0, 1)]
-    flat = [(p * 4 + q, r * 4 + s) for (p, q), (r, s) in near]
-    side_kappa = lax.ppermute(kappa, ("x", "zl"), flat)
-    mine = lax.all_gather(jnp.stack([kappa, side_kappa]), "zl")
+    kappas = lax.all_gather(kappa, NEAR, tiled=True)
 
     own = exchange(states, RING).reshape(2, half, thick, own_rows, lanes)
-    own, mine = lax.optimization_barrier((own, mine))
-    other = lax.ppermute(mine, "c", [(0, 1), (1, 0)])
+    own, kappas = lax.optimization_barrier((own, kappas))
     south = lax.ppermute(own[1, :, :, own_rows - FINE :], "y", y_up)
     north = lax.ppermute(own[0, :, :, :FINE], "y", y_down)
+    k_low = lax.ppermute(kappas[half:], "x", x_up)
+    k_high = lax.ppermute(kappas[:half], "x", x_down)
     part = (FINE, wide, lanes)
     first, second = call(join_kernel, "join", [part] * 2, [VMEM] * 3)(own, south, north)
     low = lax.ppermute(second, "x", x_up)
     high = lax.ppermute(first, "x", x_down)
 
-    edge = jnp.stack([y > 0, y < ny - 1, x > 0, x < nx - 1, c > 0]).astype(jnp.int32)
+    flags = [y > 0, y < ny - 1, x > 0, x < nx - 1]
+    edge = jnp.stack([flag.astype(jnp.int32) for flag in flags])
     deep = half * thick
     region = (deep + 2 * FINE, wide, lanes)
     coefficients = call(
-        coefficient_kernel, "coefficients", [region] * 7, [SMEM, VMEM, VMEM], [region]
-    )(edge, mine, other)
+        coefficient_kernel, "coefficients", [region] * 7, [SMEM] + [VMEM] * 3
+    )(edge, k_low, kappas, k_high)
     fine, ends = call(
         fine_kernel,
         "fine",

time: 114 us -> 111 us (0.974)
  waiting for transfers between devices: 34.2 us -> 27.3 us
  blocking collectives: 23.4 us -> 28.7 us
  starting transfers between devices: 46.8 us -> 45.2 us
    all_gather x1, blocking collectives: 13.1 us -> 18.4 us  [body(): kappas = lax.all_gather(kappa, NEAR, tiled=True)]
    ppermute x1, waiting for transfers between devices: 3.52 us -> 0.01 us  [body(): north = lax.ppermute(own[0, :, :, :FINE], 'y', y_down)]
    ppermute x2, waiting for transfers between devices: 3.84 us -> 0.85 us  [the longest x1 0.85 us: body(): k_high = lax.ppermute(kappas[:half], 'x', x_down)]
    ppermute x2, starting transfers between devices: 6.18 us -> 4.42 us  [the longest x1 3.13 us: body(): k_low = lax.ppermute(kappas[half:], 'x', x_up)]
  transfers between devices with their start and end apart: 9 -> 9, of which waited for: 6 -> 4; matrix products, arithmetic and copies ran while one was open for 0% -> 0% of each run, Pallas kernels for 1% -> 1%
where the time goes in v7:
time: 111 us; the launch traced here: 110 us
  starting transfers between devices  45.2 us (41%)
  blocking collectives  28.7 us (26%)
  waiting for transfers between devices  27.3 us (25%)
  Pallas kernels  6.72 us (6%)
    all_to_all x3, starting transfers between devices, exchange(): return lax.all_to_all(value, axes, 0, 0, tiled=True)  31 us
    all_to_all x3, waiting for transfers between devices, exchange(): return lax.all_to_all(value, axes, 0, 0, tiled=True)  23 us
    all_gather x1, blocking collectives, body(): kappas = lax.all_gather(kappa, NEAR, tiled=True)  18.4 us
    all_to_all x1, blocking collectives, exchange(): return lax.all_to_all(value, axes, 0, 0, tiled=True)  10.3 us
    ppermute x1, starting transfers between devices, body(): low = lax.ppermute(second, 'x', x_up)  4 us
    ppermute x1, waiting for transfers between devices, body(): high = lax.ppermute(first, 'x', x_down)  3.49 us
    ppermute x1, starting transfers between devices, body(): south = lax.ppermute(own[1, :, :, own_rows - FINE:], 'y', y_up)  3.2 us
    pallas_call x1, Pallas kernels, body(): call(fine_kernel, 'fine', [(ny, deep // ny, tile_rows, lanes), (2, half,...  3.17 us
  transfers between devices with their start and end apart: 9, of which 4 were waited for; matrix products, arithmetic and copies ran while one was open for 0% of the time, Pallas kernels for 1%

profile of v7, /device:TPU:1, one launch (start us, length us, event | category | flops | bytes accessed | tf_op | source)
XLA Modules:
  0.0 109.8 jit_solution(4635721587855452301)
XLA Ops:
  0.6 0.0 copy-start
  0.6 0.0 copy-start.2
  0.7 12.0 %all-to-all-start = ((f32[16,2,16,128]{3,2,1,0:T(8,128)}), f32[16,2,16,128]{3,2,1,0:T(8,128)S(1)}, u32[]{:S(2)}, u32[]{:S(2)}) async-start(f32[16,2,16,128]{3,2,1,0:T(8,128)} %states.1), calls=%async_computation | async-start | bytes 524288 | tf_op jit(solution)/shard_map/all_to_all | solution.py:143
  12.7 18.4 %all_gather.3.own = f32[16,48,128]{2,1,0:T(8,128)S(1)} all-gather(f32[2,48,128]{2,1,0:T(8,128)S(1)} %pad_dynamic-slice_fusion), channel_id=1, replica_groups=mesh['y'=8,'zh'=2,'x'=4,'zl'=4,'c'=2] {'zl','c'}, dimensions={0}, use_global_device_ids=true | all-gather | bytes 442368 | tf_op jit(solution)/shard_map/all_gather | solution.py:178
  31.1 0.0 all-to-all-done
  31.1 3.2 %collective-permute-start = (f32[8,2,8,128]{3,2,1,0:T(8,128)S(1)}, f32[8,2,8,128]{3,2,1,0:T(8,128)S(1)}, u32[]{:S(2)}, u32[]{:S(2)}) collective-permute-start(f32[8,2,8,128]{3,2,1,0:T(8,128)S(1)} %get-tuple-element.35), channel_id=1, source_target_pairs={{0,64},{64,128},{128,192},{192,256},{256,320},{320,384},{384,448},... | collective-permute-start | bytes 196616 | tf_op jit(solution)/shard_map/ppermute | solution.py:182
  34.3 1.3 %collective-permute-start.1 = (f32[8,2,8,128]{3,2,1,0:T(8,128)S(1)}, f32[8,2,8,128]{3,2,1,0:T(8,128)S(1)}, u32[]{:S(2)}, u32[]{:S(2)}) collective-permute-start(f32[8,2,8,128]{3,2,1,0:T(8,128)S(1)} %get-tuple-element.34), channel_id=1, source_target_pairs={{64,0},{128,64},{192,128},{256,192},{320,256},{384,320},{448,384},... | collective-permute-start | bytes 196616 | tf_op jit(solution)/shard_map/ppermute | solution.py:183
  35.6 3.1 %collective-permute-start.4 = (f32[8,48,128]{2,1,0:T(8,128)S(1)}, f32[8,48,128]{2,1,0:T(8,128)S(1)}, u32[]{:S(2)}, u32[]{:S(2)}) collective-permute-start(f32[8,48,128]{2,1,0:T(8,128)S(1)} %get-tuple-element.33), channel_id=1, source_target_pairs={{0,8},{8,16},{16,24},{1,9},{9,17},{17,25},{2,10},{10,18},{18,26},{... | collective-permute-start | bytes 589832 | tf_op jit(solution)/shard_map/ppermute | solution.py:184
  38.8 1.3 %collective-permute-start.5 = (f32[8,48,128]{2,1,0:T(8,128)S(1)}, f32[8,48,128]{2,1,0:T(8,128)S(1)}, u32[]{:S(2)}, u32[]{:S(2)}) collective-permute-start(f32[8,48,128]{2,1,0:T(8,128)S(1)} %get-tuple-element.32), channel_id=1, source_target_pairs={{8,0},{16,8},{24,16},{9,1},{17,9},{25,17},{10,2},{18,10},{26,18},{... | collective-permute-start | bytes 589832 | tf_op jit(solution)/shard_map/ppermute | solution.py:185
  40.1 0.0 collective-permute-done.south
  40.1 0.0 collective-permute-done.1.north
  40.1 4.0 %collective-permute-start.2 = (f32[8,48,128]{2,1,0:T(8,128)S(1)}, f32[8,48,128]{2,1,0:T(8,128)S(1)}, u32[]{:S(2)}, u32[]{:S(2)}) collective-permute-start(f32[8,48,128]{2,1,0:T(8,128)S(1)} %get-tuple-element.18.second), channel_id=1, source_target_pairs={{0,8},{8,16},{16,24},{1,9},{9,17},{17,25},{2,10},{10,18},{18,26},{... | collective-permute-start | bytes 589832 | tf_op jit(solution)/shard_map/ppermute | solution.py:188
  44.1 1.3 %collective-permute-start.3 = (f32[8,48,128]{2,1,0:T(8,128)S(1)}, f32[8,48,128]{2,1,0:T(8,128)S(1)}, u32[]{:S(2)}, u32[]{:S(2)}) collective-permute-start(f32[8,48,128]{2,1,0:T(8,128)S(1)} %get-tuple-element.19.first), channel_id=1, source_target_pairs={{8,0},{16,8},{24,16},{9,1},{17,9},{25,17},{10,2},{18,10},{26,18},{... | collective-permute-start | bytes 589832 | tf_op jit(solution)/shard_map/ppermute | solution.py:189
  45.4 0.1 add_convert_fusion.edge
  45.5 0.0 collective-permute-done.4.low
  45.5 0.8 collective-permute-done.5.high
  46.4 1.2 %coefficients.1 = (f32[32,48,128]{2,1,0:T(8,128)S(1)}, f32[32,48,128]{2,1,0:T(8,128)S(1)}, f32[32,48,128]{2,1,0:T(8,128)S(1)}, f32[32,48,128]{2,1,0:T(8,128)S(1)...) custom-call(s32[4]{0:T(128)S(1)} %add_convert_fusion.edge, ...), custom_call_target="tpu_custom_call" | custom-call | tf_op jit(solution)/shard_map/coefficients/pallas_call | solution.py:195
  47.6 0.0 collective-permute-done.2.low
  47.6 3.5 %collective-permute-done.3.high = f32[8,48,128]{2,1,0:T(8,128)S(1)} collective-permute-done((f32[8,48,128]{2,1,0:T(8,128)S(1)}, f32[8,48,128]{2,1,0:T(8,128)S(1)}, u32[]{:S(2)}, u32[]{:S(2)}) %collective-permute-start.3) | collective-permute-done | bytes 196640 | tf_op jit(solution)/shard_map/ppermute | solution.py:189
  51.1 3.2 %fine.1 = (f32[8,2,32,128]{3,2,1,0:T(8,128)}, f32[2,8,2,16,128]{4,3,2,1,0:T(8,128)S(1)}) custom-call(f32[8,48,128]{2,1,0:T(8,128)S(1)} %collective-permute-done.2.low, f32[8,48,128]{2,1,0:T(8,128)S(1)} %get-tuple-element.19.first, f32[8,48,128]{2,1,0:T(8,128)S(1)} %get-tuple-element.18.second, f32[8,48,128]{2,1,0:T(8,128)S(1)} %collective-permute-done.3.high, ...), custom_call_target="tpu_custom_call" | custom-call | tf_op jit(solution)/shard_map/fine/pallas_call | solution.py:198
  54.3 8.7 %all-to-all-start.1 = ((f32[8,2,32,128]{3,2,1,0:T(8,128)}), f32[8,2,32,128]{3,2,1,0:T(8,128)S(1)}, u32[]{:S(2)}, u32[]{:S(2)}) async-start(f32[8,2,32,128]{3,2,1,0:T(8,128)} %get-tuple-element.29), calls=%async_computation.1 | async-start | bytes 524288 | tf_op jit(solution)/shard_map/all_to_all | solution.py:143
  63.0 0.2 copy.8
  63.1 0.1 reshape.20.blocks
  63.3 0.6 copy-done.4
  63.8 0.1 reshape.21.counts
  63.9 8.5 %all-to-all-done.1.tiles = f32[8,2,32,128]{3,2,1,0:T(8,128)S(1)} async-done(((f32[8,2,32,128]{3,2,1,0:T(8,128)}), f32[8,2,32,128]{3,2,1,0:T(8,128)S(1)}, u32[]{:S(2)}, u32[]{:S(2)}) %all-to-all-start.1) | async-done | bytes 262176 | tf_op jit(solution)/shard_map/all_to_all | solution.py:143
  72.4 0.7 pick.1
  73.1 10.3 %all_to_all.20 = f32[16,2,8,128]{3,2,1,0:T(8,128)S(1)} all-to-all(f32[16,2,8,128]{3,2,1,0:T(8,128)S(1)} %pick.1), channel_id=1, replica_groups=mesh['y'=8,'zh'=2,'x'=4,'zl'=4,'c'=2] {'y'}, dimensions={0} | all-to-all | bytes 262144 | tf_op jit(solution)/shard_map/all_to_all | solution.py:143
  83.4 0.8 pack.1
  84.2 10.3 %all-to-all-start.3 = ((f32[16,2,24,128]{3,2,1,0:T(8,128)}), f32[16,2,24,128]{3,2,1,0:T(8,128)S(1)}, u32[]{:S(2)}, u32[]{:S(2)}) async-start(f32[16,2,24,128]{3,2,1,0:T(8,128)} %bitcast.9), calls=%async_computation.3 | async-start | bytes 786432 | tf_op jit(solution)/shard_map/all_to_all | solution.py:143
  94.5 14.5 %all-to-all-done.3.received = f32[16,2,24,128]{3,2,1,0:T(8,128)S(1)} async-done(((f32[16,2,24,128]{3,2,1,0:T(8,128)}), f32[16,2,24,128]{3,2,1,0:T(8,128)S(1)}, u32[]{:S(2)}, u32[]{:S(2)}) %all-to-all-start.3) | async-done | bytes 393248 | tf_op jit(solution)/shard_map/all_to_all | solution.py:143
  109.1 0.8 advance.1
  (12 shorter events, 0.1 us)
Async XLA Ops:
  0.6 93.9 %copy-start = (f32[2,256,128]{2,1,0:T(8,128)S(1)}, f32[2,256,128]{2,1,0:T(8,128)}, u32[]{:S(2)}) copy-start(f32[2,256,128]{2,1,0:T(8,128)} %param.7) | copy-start | bytes 786436
  0.6 12.0 %copy-start.2 = (f32[2,256,128]{2,1,0:T(8,128)S(1)}, f32[2,256,128]{2,1,0:T(8,128)}, u32[]{:S(2)}) copy-start(f32[2,256,128]{2,1,0:T(8,128)} %param.6) | copy-start | bytes 786436
  0.7 30.4 %all-to-all-start = ((f32[16,2,16,128]{3,2,1,0:T(8,128)}), f32[16,2,16,128]{3,2,1,0:T(8,128)S(1)}, u32[]{:S(2)}, u32[]{:S(2)}) async-start(f32[16,2,16,128]{3,2,1,0:T(8,128)} %states.1), calls=%async_computation | async-start | bytes 524288 | tf_op jit(solution)/shard_map/all_to_all | solution.py:143
  31.1 9.0 %collective-permute-start = (f32[8,2,8,128]{3,2,1,0:T(8,128)S(1)}, f32[8,2,8,128]{3,2,1,0:T(8,128)S(1)}, u32[]{:S(2)}, u32[]{:S(2)}) collective-permute-start(f32[8,2,8,128]{3,2,1,0:T(8,128)S(1)} %get-tuple-element.35), channel_id=1, source_target_pairs={{0,64},{64,128},{128,192},{192,256},{256,320},{320,384},{384,448},... | collective-permute-start | bytes 196616 | tf_op jit(solution)/shard_map/ppermute | solution.py:182
  34.3 5.8 %collective-permute-start.1 = (f32[8,2,8,128]{3,2,1,0:T(8,128)S(1)}, f32[8,2,8,128]{3,2,1,0:T(8,128)S(1)}, u32[]{:S(2)}, u32[]{:S(2)}) collective-permute-start(f32[8,2,8,128]{3,2,1,0:T(8,128)S(1)} %get-tuple-element.34), channel_id=1, source_target_pairs={{64,0},{128,64},{192,128},{256,192},{320,256},{384,320},{448,384},... | collective-permute-start | bytes 196616 | tf_op jit(solution)/shard_map/ppermute | solution.py:183
  35.6 9.9 %collective-permute-start.4 = (f32[8,48,128]{2,1,0:T(8,128)S(1)}, f32[8,48,128]{2,1,0:T(8,128)S(1)}, u32[]{:S(2)}, u32[]{:S(2)}) collective-permute-start(f32[8,48,128]{2,1,0:T(8,128)S(1)} %get-tuple-element.33), channel_id=1, source_target_pairs={{0,8},{8,16},{16,24},{1,9},{9,17},{17,25},{2,10},{10,18},{18,26},{... | collective-permute-start | bytes 589832 | tf_op jit(solution)/shard_map/ppermute | solution.py:184
  38.8 7.6 %collective-permute-start.5 = (f32[8,48,128]{2,1,0:T(8,128)S(1)}, f32[8,48,128]{2,1,0:T(8,128)S(1)}, u32[]{:S(2)}, u32[]{:S(2)}) collective-permute-start(f32[8,48,128]{2,1,0:T(8,128)S(1)} %get-tuple-element.32), channel_id=1, source_target_pairs={{8,0},{16,8},{24,16},{9,1},{17,9},{25,17},{10,2},{18,10},{26,18},{... | collective-permute-start | bytes 589832 | tf_op jit(solution)/shard_map/ppermute | solution.py:185
  40.1 7.5 %collective-permute-start.2 = (f32[8,48,128]{2,1,0:T(8,128)S(1)}, f32[8,48,128]{2,1,0:T(8,128)S(1)}, u32[]{:S(2)}, u32[]{:S(2)}) collective-permute-start(f32[8,48,128]{2,1,0:T(8,128)S(1)} %get-tuple-element.18.second), channel_id=1, source_target_pairs={{0,8},{8,16},{16,24},{1,9},{9,17},{17,25},{2,10},{10,18},{18,26},{... | collective-permute-start | bytes 589832 | tf_op jit(solution)/shard_map/ppermute | solution.py:188
  44.1 7.0 %collective-permute-start.3 = (f32[8,48,128]{2,1,0:T(8,128)S(1)}, f32[8,48,128]{2,1,0:T(8,128)S(1)}, u32[]{:S(2)}, u32[]{:S(2)}) collective-permute-start(f32[8,48,128]{2,1,0:T(8,128)S(1)} %get-tuple-element.19.first), channel_id=1, source_target_pairs={{8,0},{16,8},{24,16},{9,1},{17,9},{25,17},{10,2},{18,10},{26,18},{... | collective-permute-start | bytes 589832 | tf_op jit(solution)/shard_map/ppermute | solution.py:189
  54.3 8.7 %copy-start.3 = (s32[16,16,2]{1,2,0:T(2,128)S(1)}, s32[16,16,2]{1,2,0:T(2,128)}, u32[]{:S(2)}) copy-start(s32[16,16,2]{1,2,0:T(2,128)} %param.8) | copy-start | bytes 6148
  54.3 18.1 %all-to-all-start.1 = ((f32[8,2,32,128]{3,2,1,0:T(8,128)}), f32[8,2,32,128]{3,2,1,0:T(8,128)S(1)}, u32[]{:S(2)}, u32[]{:S(2)}) async-start(f32[8,2,32,128]{3,2,1,0:T(8,128)} %get-tuple-element.29), calls=%async_computation.1 | async-start | bytes 524288 | tf_op jit(solution)/shard_map/all_to_all | solution.py:143
  63.1 0.7 copy-start.4
  84.2 24.9 %copy-start.1 = (f32[16,2,16,128]{3,2,1,0:T(8,128)S(1)}, f32[16,2,16,128]{3,2,1,0:T(8,128)}, u32[]{:S(2)}) copy-start(f32[16,2,16,128]{3,2,1,0:T(8,128)} %states.1) | copy-start | bytes 786436
  84.2 24.9 %all-to-all-start.3 = ((f32[16,2,24,128]{3,2,1,0:T(8,128)}), f32[16,2,24,128]{3,2,1,0:T(8,128)S(1)}, u32[]{:S(2)}, u32[]{:S(2)}) async-start(f32[16,2,24,128]{3,2,1,0:T(8,128)} %bitcast.9), calls=%async_computation.3 | async-start | bytes 786432 | tf_op jit(solution)/shard_map/all_to_all | solution.py:143

commit v8 on v7

--- a/solution.py
+++ b/solution.py
@@ -68,35 +68,66 @@
         down, here = up, after
 
 
-def fine_kernel(low, first, second, high, c0, zp, zm, yp, ym, xp, xm, out, ends, u):
-    depth, rows, lanes = u.shape
+def advance_layer(coefficients, z, below, here, above):
+    c0, zp, zm, yp, ym, xp, xm = coefficients
+    rows, lanes = here.shape
+    return (
+        (c0[z] * here + zp[z] * above)
+        + (zm[z] * below + yp[z] * pltpu.roll(here, rows - 1, 0))
+        + (ym[z] * pltpu.roll(here, 1, 0) + xp[z] * pltpu.roll(here, lanes - 1, 1))
+        + xm[z] * pltpu.roll(here, 1, 1)
+    )
+
+
+def inner_kernel(first, second, *refs):
+    *coefficients, kept, u = refs
+    for step in range(1, FINE):
+
+        def at(z):
+            if step == 1:
+                return first[z - 8] if z < 16 else second[z - 16]
+            return u[z - 8]
+
+        lowest, end = 8 + step, 24 - step
+        below, here = at(lowest - 1), at(lowest)
+        for z in range(lowest, end):
+            above = at(z + 1)
+            new = advance_layer(coefficients, z, below, here, above)
+            u[z - 8] = new
+            if z < lowest + 2:
+                kept[step - 1, z - lowest] = new
+            if z >= end - 2:
+                kept[step - 1, 4 + z - end] = new
+            below, here = here, above
+
+
+def fine_kernel(low, first, second, high, kept, *refs):
+    *coefficients, out, ends, u = refs
+    rows = low.shape[1]
     parts = (low, first, second, high)
-
-    def given(z):
-        return parts[z // 8][z % 8]
-
     for step in range(1, FINE + 1):
-        at = given if step == 1 else (lambda z: u[z])
-        below, here = at(step - 1), at(step)
-        for z in range(step, depth - step):
-            above = at(z + 1)
-            new = (
-                (c0[z] * here + zp[z] * above)
-                + (zm[z] * below + yp[z] * pltpu.roll(here, rows - 1, 0))
-                + (
-                    ym[z] * pltpu.roll(here, 1, 0)
-                    + xp[z] * pltpu.roll(here, lanes - 1, 1)
-                )
-                + xm[z] * pltpu.roll(here, 1, 1)
-            )
-            if step < FINE:
-                u[z] = new
-            else:
-                q, k = (z - 8) // 2, z % 2
-                out[q, k] = new[8 : rows - 8]
-                ends[0, q, k] = new[8:24]
-                ends[1, q, k] = new[24:40]
-            below, here = here, above
+        done = step - 1
+
+        def at(z):
+            if done == 0:
+                return parts[z // 8][z % 8]
+            if z < 8 + done or z >= 24 - done:
+                return u[z]
+            return kept[done - 1, z - 8 - done if z < 16 else 4 + z - 24 + done]
+
+        for start in (step, 24 - step):
+            below, here = at(start - 1), at(start)
+            for z in range(start, start + 8):
+                above = at(z + 1)
+                new = advance_layer(coefficients, z, below, here, above)
+                if step < FINE:
+                    u[z] = new
+                else:
+                    q, k = (z - 8) // 2, z % 2
+                    out[q, k] = new[8 : rows - 8]
+                    ends[0, q, k] = new[8:24]
+                    ends[1, q, k] = new[24:40]
+                below, here = here, above
 
 
 def pick_kernel(blocks, counts, me, tiles, out):
@@ -195,13 +226,16 @@
     coefficients = call(
         coefficient_kernel, "coefficients", [region] * 7, [SMEM] + [VMEM] * 3
     )(edge, k_low, kappas, k_high)
+    (kept,) = call(
+        inner_kernel, "inner", [(FINE - 1, 4, *part[1:])], [VMEM] * 9, [(deep, *part[1:])]
+    )(first, second, *coefficients)
     fine, ends = call(
         fine_kernel,
         "fine",
         [(ny, deep // ny, tile_rows, lanes), (2, half, thick, own_rows, lanes)],
-        [VMEM] * 11,
+        [VMEM] * 12,
         [region],
-    )(low, first, second, high, *coefficients)
+    )(low, first, second, high, kept, *coefficients)
 
     tiles = exchange(fine, "y")
     (picked,) = call(

time: 111 us -> 110 us (level)
  transfers between devices with their start and end apart: 9 -> 9, of which waited for: 4 -> 4; matrix products, arithmetic and copies ran while one was open for 0% -> 0% of each run, Pallas kernels for 1% -> 2%
where the time goes in v8:
time: 110 us; the launch traced here: 109 us
  starting transfers between devices  45.2 us (41%)
  blocking collectives  28.7 us (26%)
  waiting for transfers between devices  26.4 us (24%)
  Pallas kernels  6.83 us (6%)
    all_to_all x3, starting transfers between devices, exchange(): return lax.all_to_all(value, axes, 0, 0, tiled=True)  31 us
    all_to_all x3, waiting for transfers between devices, exchange(): return lax.all_to_all(value, axes, 0, 0, tiled=True)  23 us
    all_gather x1, blocking collectives, body(): kappas = lax.all_gather(kappa, NEAR, tiled=True)  18.4 us
    all_to_all x1, blocking collectives, exchange(): return lax.all_to_all(value, axes, 0, 0, tiled=True)  10.3 us
    ppermute x1, starting transfers between devices, body(): low = lax.ppermute(second, 'x', x_up)  4 us
    ppermute x1, starting transfers between devices, body(): south = lax.ppermute(own[1, :, :, own_rows - FINE:], 'y', y_up)  3.2 us
    ppermute x1, starting transfers between devices, body(): k_low = lax.ppermute(kappas[half:], 'x', x_up)  3.13 us
    ppermute x1, waiting for transfers between devices, body(): high = lax.ppermute(first, 'x', x_down)  2.59 us
  transfers between devices with their start and end apart: 9, of which 4 were waited for; matrix products, arithmetic and copies ran while one was open for 0% of the time, Pallas kernels for 2%

profile of v8, /device:TPU:1, one launch (start us, length us, event | category | flops | bytes accessed | tf_op | source)
XLA Modules:
  0.0 109.1 jit_solution(14912243902362558917)
XLA Ops:
  0.6 0.0 copy-start
  0.7 12.0 %all-to-all-start = ((f32[16,2,16,128]{3,2,1,0:T(8,128)}), f32[16,2,16,128]{3,2,1,0:T(8,128)S(1)}, u32[]{:S(2)}, u32[]{:S(2)}) async-start(f32[16,2,16,128]{3,2,1,0:T(8,128)} %states.1), calls=%async_computation | async-start | bytes 524288 | tf_op jit(solution)/shard_map/all_to_all | solution.py:174
  12.7 18.4 %all_gather.3.own = f32[16,48,128]{2,1,0:T(8,128)S(1)} all-gather(f32[2,48,128]{2,1,0:T(8,128)S(1)} %pad_dynamic-slice_fusion), channel_id=1, replica_groups=mesh['y'=8,'zh'=2,'x'=4,'zl'=4,'c'=2] {'zl','c'}, dimensions={0}, use_global_device_ids=true | all-gather | bytes 442368 | tf_op jit(solution)/shard_map/all_gather | solution.py:209
  31.1 0.0 all-to-all-done
  31.1 3.2 %collective-permute-start = (f32[8,2,8,128]{3,2,1,0:T(8,128)S(1)}, f32[8,2,8,128]{3,2,1,0:T(8,128)S(1)}, u32[]{:S(2)}, u32[]{:S(2)}) collective-permute-start(f32[8,2,8,128]{3,2,1,0:T(8,128)S(1)} %get-tuple-element.35), channel_id=1, source_target_pairs={{0,64},{64,128},{128,192},{192,256},{256,320},{320,384},{384,448},... | collective-permute-start | bytes 196616 | tf_op jit(solution)/shard_map/ppermute | solution.py:213
  34.3 1.3 %collective-permute-start.1 = (f32[8,2,8,128]{3,2,1,0:T(8,128)S(1)}, f32[8,2,8,128]{3,2,1,0:T(8,128)S(1)}, u32[]{:S(2)}, u32[]{:S(2)}) collective-permute-start(f32[8,2,8,128]{3,2,1,0:T(8,128)S(1)} %get-tuple-element.34), channel_id=1, source_target_pairs={{64,0},{128,64},{192,128},{256,192},{320,256},{384,320},{448,384},... | collective-permute-start | bytes 196616 | tf_op jit(solution)/shard_map/ppermute | solution.py:214
  35.6 3.1 %collective-permute-start.4 = (f32[8,48,128]{2,1,0:T(8,128)S(1)}, f32[8,48,128]{2,1,0:T(8,128)S(1)}, u32[]{:S(2)}, u32[]{:S(2)}) collective-permute-start(f32[8,48,128]{2,1,0:T(8,128)S(1)} %get-tuple-element.33), channel_id=1, source_target_pairs={{0,8},{8,16},{16,24},{1,9},{9,17},{17,25},{2,10},{10,18},{18,26},{... | collective-permute-start | bytes 589832 | tf_op jit(solution)/shard_map/ppermute | solution.py:215
  38.8 1.3 %collective-permute-start.5 = (f32[8,48,128]{2,1,0:T(8,128)S(1)}, f32[8,48,128]{2,1,0:T(8,128)S(1)}, u32[]{:S(2)}, u32[]{:S(2)}) collective-permute-start(f32[8,48,128]{2,1,0:T(8,128)S(1)} %get-tuple-element.32), channel_id=1, source_target_pairs={{8,0},{16,8},{24,16},{9,1},{17,9},{25,17},{10,2},{18,10},{26,18},{... | collective-permute-start | bytes 589832 | tf_op jit(solution)/shard_map/ppermute | solution.py:216
  40.1 0.0 collective-permute-done.south
  40.1 0.0 collective-permute-done.1.north
  40.1 4.0 %collective-permute-start.2 = (f32[8,48,128]{2,1,0:T(8,128)S(1)}, f32[8,48,128]{2,1,0:T(8,128)S(1)}, u32[]{:S(2)}, u32[]{:S(2)}) collective-permute-start(f32[8,48,128]{2,1,0:T(8,128)S(1)} %get-tuple-element.18.second), channel_id=1, source_target_pairs={{0,8},{8,16},{16,24},{1,9},{9,17},{17,25},{2,10},{10,18},{18,26},{... | collective-permute-start | bytes 589832 | tf_op jit(solution)/shard_map/ppermute | solution.py:219
  44.1 1.3 %collective-permute-start.3 = (f32[8,48,128]{2,1,0:T(8,128)S(1)}, f32[8,48,128]{2,1,0:T(8,128)S(1)}, u32[]{:S(2)}, u32[]{:S(2)}) collective-permute-start(f32[8,48,128]{2,1,0:T(8,128)S(1)} %get-tuple-element.19.first), channel_id=1, source_target_pairs={{8,0},{16,8},{24,16},{9,1},{17,9},{25,17},{10,2},{18,10},{26,18},{... | collective-permute-start | bytes 589832 | tf_op jit(solution)/shard_map/ppermute | solution.py:220
  45.4 0.1 add_convert_fusion.edge
  45.5 0.0 collective-permute-done.4.low
  45.5 0.8 collective-permute-done.5.high
  46.4 1.2 %coefficients.1 = (f32[32,48,128]{2,1,0:T(8,128)S(1)}, f32[32,48,128]{2,1,0:T(8,128)S(1)}, f32[32,48,128]{2,1,0:T(8,128)S(1)}, f32[32,48,128]{2,1,0:T(8,128)S(1)...) custom-call(s32[4]{0:T(128)S(1)} %add_convert_fusion.edge, ...), custom_call_target="tpu_custom_call" | custom-call | tf_op jit(solution)/shard_map/coefficients/pallas_call | solution.py:226
  47.6 0.9 inner.1.kept
  48.5 0.0 collective-permute-done.2.low
  48.5 2.6 %collective-permute-done.3.high = f32[8,48,128]{2,1,0:T(8,128)S(1)} collective-permute-done((f32[8,48,128]{2,1,0:T(8,128)S(1)}, f32[8,48,128]{2,1,0:T(8,128)S(1)}, u32[]{:S(2)}, u32[]{:S(2)}) %collective-permute-start.3) | collective-permute-done | bytes 196640 | tf_op jit(solution)/shard_map/ppermute | solution.py:220
  51.1 2.4 %fine.1 = (f32[8,2,32,128]{3,2,1,0:T(8,128)}, f32[2,8,2,16,128]{4,3,2,1,0:T(8,128)S(1)}) custom-call(f32[8,48,128]{2,1,0:T(8,128)S(1)} %collective-permute-done.2.low, f32[8,48,128]{2,1,0:T(8,128)S(1)} %get-tuple-element.19.first, f32[8,48,128]{2,1,0:T(8,128)S(1)} %get-tuple-element.18.second, f32[8,48,128]{2,1,0:T(8,128)S(1)} %collective-permute-done.3.high, ...), custom_call_target="tpu_custom_call" | custom-call | tf_op jit(solution)/shard_map/fine/pallas_call | solution.py:232
  53.5 8.7 %all-to-all-start.1 = ((f32[8,2,32,128]{3,2,1,0:T(8,128)}), f32[8,2,32,128]{3,2,1,0:T(8,128)S(1)}, u32[]{:S(2)}, u32[]{:S(2)}) async-start(f32[8,2,32,128]{3,2,1,0:T(8,128)} %get-tuple-element.29), calls=%async_computation.1 | async-start | bytes 524288 | tf_op jit(solution)/shard_map/all_to_all | solution.py:174
  62.2 0.2 copy.8
  62.3 0.1 reshape.20.blocks
  62.5 0.6 copy-done.4
  63.0 0.1 reshape.21.counts
  63.1 8.5 %all-to-all-done.1.tiles = f32[8,2,32,128]{3,2,1,0:T(8,128)S(1)} async-done(((f32[8,2,32,128]{3,2,1,0:T(8,128)}), f32[8,2,32,128]{3,2,1,0:T(8,128)S(1)}, u32[]{:S(2)}, u32[]{:S(2)}) %all-to-all-start.1) | async-done | bytes 262176 | tf_op jit(solution)/shard_map/all_to_all | solution.py:174
  71.6 0.7 pick.1
  72.3 10.3 %all_to_all.20 = f32[16,2,8,128]{3,2,1,0:T(8,128)S(1)} all-to-all(f32[16,2,8,128]{3,2,1,0:T(8,128)S(1)} %pick.1), channel_id=1, replica_groups=mesh['y'=8,'zh'=2,'x'=4,'zl'=4,'c'=2] {'y'}, dimensions={0} | all-to-all | bytes 262144 | tf_op jit(solution)/shard_map/all_to_all | solution.py:174
  82.6 0.8 pack.1
  83.4 10.3 %all-to-all-start.3 = ((f32[16,2,24,128]{3,2,1,0:T(8,128)}), f32[16,2,24,128]{3,2,1,0:T(8,128)S(1)}, u32[]{:S(2)}, u32[]{:S(2)}) async-start(f32[16,2,24,128]{3,2,1,0:T(8,128)} %bitcast.9), calls=%async_computation.3 | async-start | bytes 786432 | tf_op jit(solution)/shard_map/all_to_all | solution.py:174
  93.7 14.5 %all-to-all-done.3.received = f32[16,2,24,128]{3,2,1,0:T(8,128)S(1)} async-done(((f32[16,2,24,128]{3,2,1,0:T(8,128)}), f32[16,2,24,128]{3,2,1,0:T(8,128)S(1)}, u32[]{:S(2)}, u32[]{:S(2)}) %all-to-all-start.3) | async-done | bytes 393248 | tf_op jit(solution)/shard_map/all_to_all | solution.py:174
  108.3 0.8 advance.1
  (13 shorter events, 0.1 us)
Async XLA Ops:
  0.6 93.1 %copy-start = (f32[2,256,128]{2,1,0:T(8,128)S(1)}, f32[2,256,128]{2,1,0:T(8,128)}, u32[]{:S(2)}) copy-start(f32[2,256,128]{2,1,0:T(8,128)} %param.7) | copy-start | bytes 786436
  0.6 12.0 %copy-start.2 = (f32[2,256,128]{2,1,0:T(8,128)S(1)}, f32[2,256,128]{2,1,0:T(8,128)}, u32[]{:S(2)}) copy-start(f32[2,256,128]{2,1,0:T(8,128)} %param.6) | copy-start | bytes 786436
  0.7 30.4 %all-to-all-start = ((f32[16,2,16,128]{3,2,1,0:T(8,128)}), f32[16,2,16,128]{3,2,1,0:T(8,128)S(1)}, u32[]{:S(2)}, u32[]{:S(2)}) async-start(f32[16,2,16,128]{3,2,1,0:T(8,128)} %states.1), calls=%async_computation | async-start | bytes 524288 | tf_op jit(solution)/shard_map/all_to_all | solution.py:174
  31.1 9.0 %collective-permute-start = (f32[8,2,8,128]{3,2,1,0:T(8,128)S(1)}, f32[8,2,8,128]{3,2,1,0:T(8,128)S(1)}, u32[]{:S(2)}, u32[]{:S(2)}) collective-permute-start(f32[8,2,8,128]{3,2,1,0:T(8,128)S(1)} %get-tuple-element.35), channel_id=1, source_target_pairs={{0,64},{64,128},{128,192},{192,256},{256,320},{320,384},{384,448},... | collective-permute-start | bytes 196616 | tf_op jit(solution)/shard_map/ppermute | solution.py:213
  34.3 5.8 %collective-permute-start.1 = (f32[8,2,8,128]{3,2,1,0:T(8,128)S(1)}, f32[8,2,8,128]{3,2,1,0:T(8,128)S(1)}, u32[]{:S(2)}, u32[]{:S(2)}) collective-permute-start(f32[8,2,8,128]{3,2,1,0:T(8,128)S(1)} %get-tuple-element.34), channel_id=1, source_target_pairs={{64,0},{128,64},{192,128},{256,192},{320,256},{384,320},{448,384},... | collective-permute-start | bytes 196616 | tf_op jit(solution)/shard_map/ppermute | solution.py:214
  35.6 9.9 %collective-permute-start.4 = (f32[8,48,128]{2,1,0:T(8,128)S(1)}, f32[8,48,128]{2,1,0:T(8,128)S(1)}, u32[]{:S(2)}, u32[]{:S(2)}) collective-permute-start(f32[8,48,128]{2,1,0:T(8,128)S(1)} %get-tuple-element.33), channel_id=1, source_target_pairs={{0,8},{8,16},{16,24},{1,9},{9,17},{17,25},{2,10},{10,18},{18,26},{... | collective-permute-start | bytes 589832 | tf_op jit(solution)/shard_map/ppermute | solution.py:215
  38.8 7.6 %collective-permute-start.5 = (f32[8,48,128]{2,1,0:T(8,128)S(1)}, f32[8,48,128]{2,1,0:T(8,128)S(1)}, u32[]{:S(2)}, u32[]{:S(2)}) collective-permute-start(f32[8,48,128]{2,1,0:T(8,128)S(1)} %get-tuple-element.32), channel_id=1, source_target_pairs={{8,0},{16,8},{24,16},{9,1},{17,9},{25,17},{10,2},{18,10},{26,18},{... | collective-permute-start | bytes 589832 | tf_op jit(solution)/shard_map/ppermute | solution.py:216
  40.1 8.4 %collective-permute-start.2 = (f32[8,48,128]{2,1,0:T(8,128)S(1)}, f32[8,48,128]{2,1,0:T(8,128)S(1)}, u32[]{:S(2)}, u32[]{:S(2)}) collective-permute-start(f32[8,48,128]{2,1,0:T(8,128)S(1)} %get-tuple-element.18.second), channel_id=1, source_target_pairs={{0,8},{8,16},{16,24},{1,9},{9,17},{17,25},{2,10},{10,18},{18,26},{... | collective-permute-start | bytes 589832 | tf_op jit(solution)/shard_map/ppermute | solution.py:219
  44.1 7.0 %collective-permute-start.3 = (f32[8,48,128]{2,1,0:T(8,128)S(1)}, f32[8,48,128]{2,1,0:T(8,128)S(1)}, u32[]{:S(2)}, u32[]{:S(2)}) collective-permute-start(f32[8,48,128]{2,1,0:T(8,128)S(1)} %get-tuple-element.19.first), channel_id=1, source_target_pairs={{8,0},{16,8},{24,16},{9,1},{17,9},{25,17},{10,2},{18,10},{26,18},{... | collective-permute-start | bytes 589832 | tf_op jit(solution)/shard_map/ppermute | solution.py:220
  53.5 8.7 %copy-start.3 = (s32[16,16,2]{1,2,0:T(2,128)S(1)}, s32[16,16,2]{1,2,0:T(2,128)}, u32[]{:S(2)}) copy-start(s32[16,16,2]{1,2,0:T(2,128)} %param.8) | copy-start | bytes 6148
  53.5 18.1 %all-to-all-start.1 = ((f32[8,2,32,128]{3,2,1,0:T(8,128)}), f32[8,2,32,128]{3,2,1,0:T(8,128)S(1)}, u32[]{:S(2)}, u32[]{:S(2)}) async-start(f32[8,2,32,128]{3,2,1,0:T(8,128)} %get-tuple-element.29), calls=%async_computation.1 | async-start | bytes 524288 | tf_op jit(solution)/shard_map/all_to_all | solution.py:174
  62.3 0.7 copy-start.4
  83.4 24.9 %copy-start.1 = (f32[16,2,16,128]{3,2,1,0:T(8,128)S(1)}, f32[16,2,16,128]{3,2,1,0:T(8,128)}, u32[]{:S(2)}) copy-start(f32[16,2,16,128]{3,2,1,0:T(8,128)} %states.1) | copy-start | bytes 786436
  83.4 24.9 %all-to-all-start.3 = ((f32[16,2,24,128]{3,2,1,0:T(8,128)}), f32[16,2,24,128]{3,2,1,0:T(8,128)S(1)}, u32[]{:S(2)}, u32[]{:S(2)}) async-start(f32[16,2,24,128]{3,2,1,0:T(8,128)} %bitcast.9), calls=%async_computation.3 | async-start | bytes 786432 | tf_op jit(solution)/shard_map/all_to_all | solution.py:174

commit v9 on v8

--- a/solution.py
+++ b/solution.py
@@ -13,11 +13,27 @@
 RING = ("zh", "zl", "c")
 SLAB = ("x", "zl", "c")
 CUTS = ("y", "zh")
-NEAR = ("zl", "c")
 
 VMEM = pl.BlockSpec(memory_space=pltpu.VMEM)
 SMEM = pl.BlockSpec(memory_space=pltpu.SMEM)
 PARAMS = pltpu.CompilerParams(vmem_limit_bytes=40 * 2**20)
+
+
+def load_kernel(states, kappa, out):
+    for d in range(out.shape[0]):
+        for k in range(2):
+            out[d, 16 * k : 16 * k + 16] = states[d, k]
+        out[d, 32:56] = kappa[d % 2]
+
+
+def gather_kernel(place, mine, other, own, first, second, kappa):
+    for part, source in ((place[0], mine), (1 - place[0], other)):
+        for j in range(8):
+            for h in range(2):
+                kappa[2 * j + part, 24 * h : 24 * h + 24] = source[h, j]
+    for z in range(FINE):
+        own[z] = first[z] = kappa[z]
+        own[FINE + z] = second[z] = kappa[FINE + z]
 
 
 def join_kernel(own, south, north, first, second):
@@ -26,8 +42,8 @@
             for k in range(2):
                 layer = 2 * j + k
                 out[layer, 0:8] = south[start + j, k]
-                out[layer, 8:24] = own[0, start + j, k]
-                out[layer, 24:40] = own[1, start + j, k]
+                out[layer, 8:24] = own[0, start + j, 16 * k : 16 * k + 16]
+                out[layer, 24:40] = own[1, start + j, 16 * k : 16 * k + 16]
                 out[layer, 40:48] = north[start + j, k]
 
 
@@ -205,16 +221,29 @@
     y_down = [(i + 1, i) for i in range(ny - 1)]
 
     padded = jnp.pad(diffusivity, ((0, 0), (FINE, FINE), (0, 0)))
-    kappa = lax.dynamic_slice_in_dim(padded, y * tile_rows, wide, 1)
-    kappas = lax.all_gather(kappa, NEAR, tiled=True)
-
-    own = exchange(states, RING).reshape(2, half, thick, own_rows, lanes)
-    own, kappas = lax.optimization_barrier((own, kappas))
-    south = lax.ppermute(own[1, :, :, own_rows - FINE :], "y", y_up)
-    north = lax.ppermute(own[0, :, :, :FINE], "y", y_down)
-    k_low = lax.ppermute(kappas[half:], "x", x_up)
-    k_high = lax.ppermute(kappas[:half], "x", x_down)
+    window = y * tile_rows + lax.axis_index("zh") * (wide // 2)
+    kappa = lax.dynamic_slice_in_dim(padded, window, wide // 2, 1)
+    layers = thick * own_rows
+    packed = layers + wide // 2
+    (load,) = call(
+        load_kernel, "load", [(slices, packed, lanes)], [VMEM] * 2
+    )(states, kappa)
+    own = exchange(load, RING).reshape(2, half, packed, lanes)
+    ends_of = own[:, :, :layers].reshape(2, half, thick, own_rows, lanes)
+    south = lax.ppermute(ends_of[1, :, :, own_rows - FINE :], "y", y_up)
+    north = lax.ppermute(ends_of[0, :, :, :FINE], "y", y_down)
     part = (FINE, wide, lanes)
+    mine = own[:, :, layers:]
+    other = lax.ppermute(mine, "c", [(0, 1), (1, 0)])
+    kappas, k_first, k_second = call(
+        gather_kernel,
+        "gather",
+        [(2 * FINE, wide, lanes), part, part],
+        [SMEM, VMEM, VMEM],
+        [(2 * FINE, wide, lanes)],
+    )(lax.axis_index("c")[None], mine, other)
+    k_low = lax.ppermute(k_second, "x", x_up)
+    k_high = lax.ppermute(k_first, "x", x_down)
     first, second = call(join_kernel, "join", [part] * 2, [VMEM] * 3)(own, south, north)
     low = lax.ppermute(second, "x", x_up)
     high = lax.ppermute(first, "x", x_down)

time: 110 us -> 109 us (level)
  starting transfers between devices: 45.2 us -> 33.9 us
  blocking collectives: 28.7 us -> 37.9 us
    all_to_all x1 -> x2, blocking collectives: 10.3 us -> 37.9 us  [exchange(): return lax.all_to_all(value, axes, 0, 0, tiled=True)]
    all_gather x1 -> x0, blocking collectives: 18.4 us -> none  [body(): kappas = lax.all_gather(kappa, NEAR, tiled=True)]
    all_to_all x3 -> x2, starting transfers between devices: 31 us -> 17.8 us  [exchange(): return lax.all_to_all(value, axes, 0, 0, tiled=True)]
    ppermute x4 -> x5, starting transfers between devices: 8.91 us -> 10.8 us  [the longest x1 3.2 us: body(): south = lax.ppermute(ends_of[1, :, :, own_rows - FINE:], 'y', y_up)]
    all_to_all x3 -> x2, waiting for transfers between devices: 23 us -> 23 us  [exchange(): return lax.all_to_all(value, axes, 0, 0, tiled=True)]
where the time goes in v9:
time: 109 us; the launch traced here: 108 us
  blocking collectives  37.9 us (35%)
  starting transfers between devices  33.9 us (31%)
  waiting for transfers between devices  25.7 us (24%)
  Pallas kernels  7.51 us (7%)
  local copies, waits for them, and re-layouts  2 us (2%)
    all_to_all x2, blocking collectives, exchange(): return lax.all_to_all(value, axes, 0, 0, tiled=True)  37.9 us
    all_to_all x2, waiting for transfers between devices, exchange(): return lax.all_to_all(value, axes, 0, 0, tiled=True)  23 us
    all_to_all x2, starting transfers between devices, exchange(): return lax.all_to_all(value, axes, 0, 0, tiled=True)  17.8 us
    ppermute x1, starting transfers between devices, body(): low = lax.ppermute(second, 'x', x_up)  4 us
    ppermute x1, starting transfers between devices, body(): south = lax.ppermute(ends_of[1, :, :, own_rows - FINE:], 'y', y_up)  3.2 us
    ppermute x1, starting transfers between devices, body(): k_low = lax.ppermute(k_second, 'x', x_up)  3.13 us
    pallas_call x1, Pallas kernels, body(): call(fine_kernel, 'fine', [(ny, deep // ny, tile_rows, lanes), (2, half,...  2.76 us
    ppermute x1, waiting for transfers between devices, body(): high = lax.ppermute(first, 'x', x_down)  2.2 us
  transfers between devices with their start and end apart: 9, of which 4 were waited for; matrix products, arithmetic and copies ran while one was open for 0% of the time, Pallas kernels for 2%

profile of v9, /device:TPU:1, one launch (start us, length us, event | category | flops | bytes accessed | tf_op | source)
XLA Modules:
  0.0 108.0 jit_solution(4727954094996026756)
XLA Ops:
  0.6 0.0 copy-start
  0.7 0.8 pad_dynamic-slice_fusion.kappa
  1.5 0.2 copy-done.1
  1.7 27.6 %all_to_all.20 = f32[16,56,128]{2,1,0:T(8,128)S(1)} all-to-all(f32[16,56,128]{2,1,0:T(8,128)S(1)} %load.1), channel_id=1, replica_groups=mesh['y'=8,'zh'=2,'x'=4,'zl'=4,'c'=2] {'zh','zl','c'}, dimensions={0} | all-to-all | bytes 917504 | tf_op jit(solution)/shard_map/all_to_all | solution.py:190
  29.3 1.9 %collective-permute-start.4 = (f32[2,8,24,128]{3,2,1,0:T(8,128)S(1)}, f32[2,8,24,128]{3,2,1,0:T(8,128)S(1)}, u32[]{:S(2)}, u32[]{:S(2)}) collective-permute-start(f32[2,8,24,128]{3,2,1,0:T(8,128)S(1)} %slice.19.mine), channel_id=1, source_target_pairs={{0,1},{1,0},{2,3},{3,2},{4,5},{5,4},{6,7},{7,6},{8,9},{9,8},{10,11... | collective-permute-start | bytes 589832 | tf_op jit(solution)/shard_map/ppermute | solution.py:237
  31.3 3.2 %collective-permute-start = (f32[8,2,8,128]{3,2,1,0:T(8,128)S(1)}, f32[8,2,8,128]{3,2,1,0:T(8,128)S(1)}, u32[]{:S(2)}, u32[]{:S(2)}) collective-permute-start(f32[8,2,8,128]{3,2,1,0:T(8,128)S(1)} %get-tuple-element.35), channel_id=1, source_target_pairs={{0,64},{64,128},{128,192},{192,256},{256,320},{320,384},{384,448},... | collective-permute-start | bytes 196616 | tf_op jit(solution)/shard_map/ppermute | solution.py:233
  34.5 1.3 %collective-permute-start.1 = (f32[8,2,8,128]{3,2,1,0:T(8,128)S(1)}, f32[8,2,8,128]{3,2,1,0:T(8,128)S(1)}, u32[]{:S(2)}, u32[]{:S(2)}) collective-permute-start(f32[8,2,8,128]{3,2,1,0:T(8,128)S(1)} %get-tuple-element.34), channel_id=1, source_target_pairs={{64,0},{128,64},{192,128},{256,192},{320,256},{384,320},{448,384},... | collective-permute-start | bytes 196616 | tf_op jit(solution)/shard_map/ppermute | solution.py:234
  35.8 0.0 collective-permute-done.4.other
  35.8 0.1 gather.1
  35.9 3.1 %collective-permute-start.5 = (f32[8,48,128]{2,1,0:T(8,128)S(1)}, f32[8,48,128]{2,1,0:T(8,128)S(1)}, u32[]{:S(2)}, u32[]{:S(2)}) collective-permute-start(f32[8,48,128]{2,1,0:T(8,128)S(1)} %get-tuple-element.20), channel_id=1, source_target_pairs={{0,8},{8,16},{16,24},{1,9},{9,17},{17,25},{2,10},{10,18},{18,26},{... | collective-permute-start | bytes 589832 | tf_op jit(solution)/shard_map/ppermute | solution.py:245
  39.0 1.3 %collective-permute-start.6 = (f32[8,48,128]{2,1,0:T(8,128)S(1)}, f32[8,48,128]{2,1,0:T(8,128)S(1)}, u32[]{:S(2)}, u32[]{:S(2)}) collective-permute-start(f32[8,48,128]{2,1,0:T(8,128)S(1)} %get-tuple-element.22), channel_id=1, source_target_pairs={{8,0},{16,8},{24,16},{9,1},{17,9},{25,17},{10,2},{18,10},{26,18},{... | collective-permute-start | bytes 589832 | tf_op jit(solution)/shard_map/ppermute | solution.py:246
  40.3 0.0 collective-permute-done.1.north
  40.4 4.0 %collective-permute-start.2 = (f32[8,48,128]{2,1,0:T(8,128)S(1)}, f32[8,48,128]{2,1,0:T(8,128)S(1)}, u32[]{:S(2)}, u32[]{:S(2)}) collective-permute-start(f32[8,48,128]{2,1,0:T(8,128)S(1)} %get-tuple-element.18.second), channel_id=1, source_target_pairs={{0,8},{8,16},{16,24},{1,9},{9,17},{17,25},{2,10},{10,18},{18,26},{... | collective-permute-start | bytes 589832 | tf_op jit(solution)/shard_map/ppermute | solution.py:248
  44.4 1.3 %collective-permute-start.3 = (f32[8,48,128]{2,1,0:T(8,128)S(1)}, f32[8,48,128]{2,1,0:T(8,128)S(1)}, u32[]{:S(2)}, u32[]{:S(2)}) collective-permute-start(f32[8,48,128]{2,1,0:T(8,128)S(1)} %get-tuple-element.19.first), channel_id=1, source_target_pairs={{8,0},{16,8},{24,16},{9,1},{17,9},{25,17},{10,2},{18,10},{26,18},{... | collective-permute-start | bytes 589832 | tf_op jit(solution)/shard_map/ppermute | solution.py:249
  45.7 0.1 add_convert_fusion.edge
  45.8 0.5 collective-permute-done.6.high
  46.3 1.2 %coefficients.1 = (f32[32,48,128]{2,1,0:T(8,128)S(1)}, f32[32,48,128]{2,1,0:T(8,128)S(1)}, f32[32,48,128]{2,1,0:T(8,128)S(1)}, f32[32,48,128]{2,1,0:T(8,128)S(1)...) custom-call(s32[4]{0:T(128)S(1)} %add_convert_fusion.edge, ...), custom_call_target="tpu_custom_call" | custom-call | tf_op jit(solution)/shard_map/coefficients/pallas_call | solution.py:255
  47.5 1.1 %inner.1.kept = f32[7,4,48,128]{3,2,1,0:T(8,128)S(1)} custom-call(f32[8,48,128]{2,1,0:T(8,128)S(1)} %get-tuple-element.19.first, f32[8,48,128]{2,1,0:T(8,128)S(1)} %get-tuple-element.18.second, f32[32,48,128]{2,1,0:T(8,128)S(1)} %get-tuple-element.23.refs_0_, f32[32,48,128]{2,1,0:T(8,128)S(1)} %get-tuple-element.24.refs_1_, ...), custom_call_target="tpu_custom_call" | custom-call | tf_op jit(solution)/shard_map/inner/pallas_call | solution.py:258
  48.6 2.2 %collective-permute-done.3.high = f32[8,48,128]{2,1,0:T(8,128)S(1)} collective-permute-done((f32[8,48,128]{2,1,0:T(8,128)S(1)}, f32[8,48,128]{2,1,0:T(8,128)S(1)}, u32[]{:S(2)}, u32[]{:S(2)}) %collective-permute-start.3) | collective-permute-done | bytes 196640 | tf_op jit(solution)/shard_map/ppermute | solution.py:249
  50.8 2.8 %fine.1 = (f32[8,2,32,128]{3,2,1,0:T(8,128)}, f32[2,8,2,16,128]{4,3,2,1,0:T(8,128)S(1)}) custom-call(f32[8,48,128]{2,1,0:T(8,128)S(1)} %collective-permute-done.2.low, f32[8,48,128]{2,1,0:T(8,128)S(1)} %get-tuple-element.19.first, f32[8,48,128]{2,1,0:T(8,128)S(1)} %get-tuple-element.18.second, f32[8,48,128]{2,1,0:T(8,128)S(1)} %collective-permute-done.3.high, ...), custom_call_target="tpu_custom_call" | custom-call | tf_op jit(solution)/shard_map/fine/pallas_call | solution.py:261
  53.6 8.9 %all-to-all-start.1 = ((f32[8,2,32,128]{3,2,1,0:T(8,128)}), f32[8,2,32,128]{3,2,1,0:T(8,128)S(1)}, u32[]{:S(2)}, u32[]{:S(2)}) async-start(f32[8,2,32,128]{3,2,1,0:T(8,128)} %get-tuple-element.31), calls=%async_computation.1 | async-start | bytes 524288 | tf_op jit(solution)/shard_map/all_to_all | solution.py:190
  62.5 0.2 copy.7
  62.7 0.1 reshape.24.blocks
  62.8 0.6 copy-done.3
  63.4 0.1 reshape.25.counts
  63.5 8.5 %all-to-all-done.1.tiles = f32[8,2,32,128]{3,2,1,0:T(8,128)S(1)} async-done(((f32[8,2,32,128]{3,2,1,0:T(8,128)}), f32[8,2,32,128]{3,2,1,0:T(8,128)S(1)}, u32[]{:S(2)}, u32[]{:S(2)}) %all-to-all-start.1) | async-done | bytes 262176 | tf_op jit(solution)/shard_map/all_to_all | solution.py:190
  72.0 0.7 pick.1
  72.7 10.3 %all_to_all.21 = f32[16,2,8,128]{3,2,1,0:T(8,128)S(1)} all-to-all(f32[16,2,8,128]{3,2,1,0:T(8,128)S(1)} %pick.1), channel_id=1, replica_groups=mesh['y'=8,'zh'=2,'x'=4,'zl'=4,'c'=2] {'y'}, dimensions={0} | all-to-all | bytes 262144 | tf_op jit(solution)/shard_map/all_to_all | solution.py:190
  83.0 0.8 pack.1
  83.8 8.9 %all-to-all-start.3 = ((f32[16,2,24,128]{3,2,1,0:T(8,128)}), f32[16,2,24,128]{3,2,1,0:T(8,128)S(1)}, u32[]{:S(2)}, u32[]{:S(2)}) async-start(f32[16,2,24,128]{3,2,1,0:T(8,128)} %bitcast.11), calls=%async_computation.3 | async-start | bytes 786432 | tf_op jit(solution)/shard_map/all_to_all | solution.py:190
  92.7 14.5 %all-to-all-done.3.received = f32[16,2,24,128]{3,2,1,0:T(8,128)S(1)} async-done(((f32[16,2,24,128]{3,2,1,0:T(8,128)}), f32[16,2,24,128]{3,2,1,0:T(8,128)S(1)}, u32[]{:S(2)}, u32[]{:S(2)}) %all-to-all-start.3) | async-done | bytes 393248 | tf_op jit(solution)/shard_map/all_to_all | solution.py:190
  107.2 0.8 advance.1
  (14 shorter events, 0.1 us)
Async XLA Ops:
  0.6 92.0 %copy-start = (f32[2,256,128]{2,1,0:T(8,128)S(1)}, f32[2,256,128]{2,1,0:T(8,128)}, u32[]{:S(2)}) copy-start(f32[2,256,128]{2,1,0:T(8,128)} %param.7) | copy-start | bytes 786436
  0.6 1.0 copy-start.1
  29.3 6.5 %collective-permute-start.4 = (f32[2,8,24,128]{3,2,1,0:T(8,128)S(1)}, f32[2,8,24,128]{3,2,1,0:T(8,128)S(1)}, u32[]{:S(2)}, u32[]{:S(2)}) collective-permute-start(f32[2,8,24,128]{3,2,1,0:T(8,128)S(1)} %slice.19.mine), channel_id=1, source_target_pairs={{0,1},{1,0},{2,3},{3,2},{4,5},{5,4},{6,7},{7,6},{8,9},{9,8},{10,11... | collective-permute-start | bytes 589832 | tf_op jit(solution)/shard_map/ppermute | solution.py:237
  31.3 9.0 %collective-permute-start = (f32[8,2,8,128]{3,2,1,0:T(8,128)S(1)}, f32[8,2,8,128]{3,2,1,0:T(8,128)S(1)}, u32[]{:S(2)}, u32[]{:S(2)}) collective-permute-start(f32[8,2,8,128]{3,2,1,0:T(8,128)S(1)} %get-tuple-element.35), channel_id=1, source_target_pairs={{0,64},{64,128},{128,192},{192,256},{256,320},{320,384},{384,448},... | collective-permute-start | bytes 196616 | tf_op jit(solution)/shard_map/ppermute | solution.py:233
  34.5 5.8 %collective-permute-start.1 = (f32[8,2,8,128]{3,2,1,0:T(8,128)S(1)}, f32[8,2,8,128]{3,2,1,0:T(8,128)S(1)}, u32[]{:S(2)}, u32[]{:S(2)}) collective-permute-start(f32[8,2,8,128]{3,2,1,0:T(8,128)S(1)} %get-tuple-element.34), channel_id=1, source_target_pairs={{64,0},{128,64},{192,128},{256,192},{320,256},{384,320},{448,384},... | collective-permute-start | bytes 196616 | tf_op jit(solution)/shard_map/ppermute | solution.py:234
  35.9 9.9 %collective-permute-start.5 = (f32[8,48,128]{2,1,0:T(8,128)S(1)}, f32[8,48,128]{2,1,0:T(8,128)S(1)}, u32[]{:S(2)}, u32[]{:S(2)}) collective-permute-start(f32[8,48,128]{2,1,0:T(8,128)S(1)} %get-tuple-element.20), channel_id=1, source_target_pairs={{0,8},{8,16},{16,24},{1,9},{9,17},{17,25},{2,10},{10,18},{18,26},{... | collective-permute-start | bytes 589832 | tf_op jit(solution)/shard_map/ppermute | solution.py:245
  39.0 7.2 %collective-permute-start.6 = (f32[8,48,128]{2,1,0:T(8,128)S(1)}, f32[8,48,128]{2,1,0:T(8,128)S(1)}, u32[]{:S(2)}, u32[]{:S(2)}) collective-permute-start(f32[8,48,128]{2,1,0:T(8,128)S(1)} %get-tuple-element.22), channel_id=1, source_target_pairs={{8,0},{16,8},{24,16},{9,1},{17,9},{25,17},{10,2},{18,10},{26,18},{... | collective-permute-start | bytes 589832 | tf_op jit(solution)/shard_map/ppermute | solution.py:246
  40.4 8.2 %collective-permute-start.2 = (f32[8,48,128]{2,1,0:T(8,128)S(1)}, f32[8,48,128]{2,1,0:T(8,128)S(1)}, u32[]{:S(2)}, u32[]{:S(2)}) collective-permute-start(f32[8,48,128]{2,1,0:T(8,128)S(1)} %get-tuple-element.18.second), channel_id=1, source_target_pairs={{0,8},{8,16},{16,24},{1,9},{9,17},{17,25},{2,10},{10,18},{18,26},{... | collective-permute-start | bytes 589832 | tf_op jit(solution)/shard_map/ppermute | solution.py:248
  44.4 6.4 %collective-permute-start.3 = (f32[8,48,128]{2,1,0:T(8,128)S(1)}, f32[8,48,128]{2,1,0:T(8,128)S(1)}, u32[]{:S(2)}, u32[]{:S(2)}) collective-permute-start(f32[8,48,128]{2,1,0:T(8,128)S(1)} %get-tuple-element.19.first), channel_id=1, source_target_pairs={{8,0},{16,8},{24,16},{9,1},{17,9},{25,17},{10,2},{18,10},{26,18},{... | collective-permute-start | bytes 589832 | tf_op jit(solution)/shard_map/ppermute | solution.py:249
  53.6 9.0 %copy-start.2 = (s32[16,16,2]{1,2,0:T(2,128)S(1)}, s32[16,16,2]{1,2,0:T(2,128)}, u32[]{:S(2)}) copy-start(s32[16,16,2]{1,2,0:T(2,128)} %param.8) | copy-start | bytes 6148
  53.6 18.4 %all-to-all-start.1 = ((f32[8,2,32,128]{3,2,1,0:T(8,128)}), f32[8,2,32,128]{3,2,1,0:T(8,128)S(1)}, u32[]{:S(2)}, u32[]{:S(2)}) async-start(f32[8,2,32,128]{3,2,1,0:T(8,128)} %get-tuple-element.31), calls=%async_computation.1 | async-start | bytes 524288 | tf_op jit(solution)/shard_map/all_to_all | solution.py:190
  62.7 0.7 copy-start.3
  83.8 23.4 %all-to-all-start.3 = ((f32[16,2,24,128]{3,2,1,0:T(8,128)}), f32[16,2,24,128]{3,2,1,0:T(8,128)S(1)}, u32[]{:S(2)}, u32[]{:S(2)}) async-start(f32[16,2,24,128]{3,2,1,0:T(8,128)} %bitcast.11), calls=%async_computation.3 | async-start | bytes 786432 | tf_op jit(solution)/shard_map/all_to_all | solution.py:190

commit v10 on v9

--- a/solution.py
+++ b/solution.py
@@ -19,11 +19,20 @@
 PARAMS = pltpu.CompilerParams(vmem_limit_bytes=40 * 2**20)
 
 
-def load_kernel(states, kappa, out):
+def load_kernel(skip, states, kappa, out):
+    rows, lanes = kappa.shape[1:]
+    for r in range(0, rows, 8):
+        row = skip[0] + r
+        fits = jnp.where(row >= 0, jnp.where(row < rows, 1, 0), 0)
+        start = pl.multiple_of(jnp.clip(row, 0, rows - 8), 8)
+        keep = jnp.full((8, lanes), fits) == 1
+        for k in range(2):
+            tile = jnp.where(keep, kappa[k, pl.ds(start, 8), :], 0.0)
+            for d in range(k, out.shape[0], 2):
+                out[d, 32 + r : 40 + r] = tile
     for d in range(out.shape[0]):
         for k in range(2):
             out[d, 16 * k : 16 * k + 16] = states[d, k]
-        out[d, 32:56] = kappa[d % 2]
 
 
 def gather_kernel(place, mine, other, own, first, second, kappa):
@@ -220,14 +229,14 @@
     y_up = [(i, i + 1) for i in range(ny - 1)]
     y_down = [(i + 1, i) for i in range(ny - 1)]
 
-    padded = jnp.pad(diffusivity, ((0, 0), (FINE, FINE), (0, 0)))
-    window = y * tile_rows + lax.axis_index("zh") * (wide // 2)
-    kappa = lax.dynamic_slice_in_dim(padded, window, wide // 2, 1)
+    window = y * tile_rows - FINE + lax.axis_index("zh") * (wide // 2)
+    inside = jnp.clip(window, 0, diffusivity.shape[1] - wide // 2)
+    kappa = lax.dynamic_slice_in_dim(diffusivity, inside, wide // 2, 1)
     layers = thick * own_rows
     packed = layers + wide // 2
     (load,) = call(
-        load_kernel, "load", [(slices, packed, lanes)], [VMEM] * 2
-    )(states, kappa)
+        load_kernel, "load", [(slices, packed, lanes)], [SMEM, VMEM, VMEM]
+    )((window - inside)[None], states, kappa)
     own = exchange(load, RING).reshape(2, half, packed, lanes)
     ends_of = own[:, :, :layers].reshape(2, half, thick, own_rows, lanes)
     south = lax.ppermute(ends_of[1, :, :, own_rows - FINE :], "y", y_up)

time: 109 us -> 110 us (level)
  local copies, waits for them, and re-layouts: 2 us -> 3.6 us
    unnamed x9 -> x11, local copies, waits for them, and re-layouts: 0.94 us -> 2.61 us
  transfers between devices with their start and end apart: 9 -> 9, of which waited for: 4 -> 4; matrix products, arithmetic and copies ran while one was open for 0% -> 1% of each run, Pallas kernels for 2% -> 2%
where the time goes in v10:
time: 110 us; the launch traced here: 109 us
  blocking collectives  37.9 us (34%)
  starting transfers between devices  34.1 us (31%)
  waiting for transfers between devices  25 us (23%)
  Pallas kernels  7.51 us (7%)
  local copies, waits for them, and re-layouts  3.6 us (3%)
    all_to_all x2, blocking collectives, exchange(): return lax.all_to_all(value, axes, 0, 0, tiled=True)  37.9 us
    all_to_all x2, waiting for transfers between devices, exchange(): return lax.all_to_all(value, axes, 0, 0, tiled=True)  22.3 us
    all_to_all x2, starting transfers between devices, exchange(): return lax.all_to_all(value, axes, 0, 0, tiled=True)  17.9 us
    ppermute x1, starting transfers between devices, body(): low = lax.ppermute(second, 'x', x_up)  4 us
    ppermute x1, starting transfers between devices, body(): south = lax.ppermute(ends_of[1, :, :, own_rows - FINE:], 'y', y_up)  3.2 us
    ppermute x1, starting transfers between devices, body(): k_low = lax.ppermute(k_second, 'x', x_up)  3.13 us
    pallas_call x1, Pallas kernels, body(): call(fine_kernel, 'fine', [(ny, deep // ny, tile_rows, lanes), (2, half,...  2.76 us
    unnamed x11, local copies, waits for them, and re-layouts  2.61 us
  transfers between devices with their start and end apart: 9, of which 4 were waited for; matrix products, arithmetic and copies ran while one was open for 1% of the time, Pallas kernels for 2%

profile of v10, /device:TPU:1, one launch (start us, length us, event | category | flops | bytes accessed | tf_op | source)
XLA Modules:
  0.0 109.0 jit_solution(6174594502899970066)
XLA Ops:
  0.6 0.0 copy-start
  0.7 0.9 copy-done
  1.6 0.9 copy-done.1
  2.6 27.6 %all_to_all.20 = f32[16,56,128]{2,1,0:T(8,128)S(1)} all-to-all(f32[16,56,128]{2,1,0:T(8,128)S(1)} %load.1), channel_id=1, replica_groups=mesh['y'=8,'zh'=2,'x'=4,'zl'=4,'c'=2] {'zh','zl','c'}, dimensions={0} | all-to-all | bytes 917504 | tf_op jit(solution)/shard_map/all_to_all | solution.py:199
  30.2 1.9 %collective-permute-start.4 = (f32[2,8,24,128]{3,2,1,0:T(8,128)S(1)}, f32[2,8,24,128]{3,2,1,0:T(8,128)S(1)}, u32[]{:S(2)}, u32[]{:S(2)}) collective-permute-start(f32[2,8,24,128]{3,2,1,0:T(8,128)S(1)} %slice.19.mine), channel_id=1, source_target_pairs={{0,1},{1,0},{2,3},{3,2},{4,5},{5,4},{6,7},{7,6},{8,9},{9,8},{10,11... | collective-permute-start | bytes 589832 | tf_op jit(solution)/shard_map/ppermute | solution.py:246
  32.2 3.2 %collective-permute-start = (f32[8,2,8,128]{3,2,1,0:T(8,128)S(1)}, f32[8,2,8,128]{3,2,1,0:T(8,128)S(1)}, u32[]{:S(2)}, u32[]{:S(2)}) collective-permute-start(f32[8,2,8,128]{3,2,1,0:T(8,128)S(1)} %get-tuple-element.35), channel_id=1, source_target_pairs={{0,64},{64,128},{128,192},{192,256},{256,320},{320,384},{384,448},... | collective-permute-start | bytes 196616 | tf_op jit(solution)/shard_map/ppermute | solution.py:242
  35.4 1.3 %collective-permute-start.1 = (f32[8,2,8,128]{3,2,1,0:T(8,128)S(1)}, f32[8,2,8,128]{3,2,1,0:T(8,128)S(1)}, u32[]{:S(2)}, u32[]{:S(2)}) collective-permute-start(f32[8,2,8,128]{3,2,1,0:T(8,128)S(1)} %get-tuple-element.34), channel_id=1, source_target_pairs={{64,0},{128,64},{192,128},{256,192},{320,256},{384,320},{448,384},... | collective-permute-start | bytes 196616 | tf_op jit(solution)/shard_map/ppermute | solution.py:243
  36.7 0.1 gather.1
  36.8 3.1 %collective-permute-start.5 = (f32[8,48,128]{2,1,0:T(8,128)S(1)}, f32[8,48,128]{2,1,0:T(8,128)S(1)}, u32[]{:S(2)}, u32[]{:S(2)}) collective-permute-start(f32[8,48,128]{2,1,0:T(8,128)S(1)} %get-tuple-element.20), channel_id=1, source_target_pairs={{0,8},{8,16},{16,24},{1,9},{9,17},{17,25},{2,10},{10,18},{18,26},{... | collective-permute-start | bytes 589832 | tf_op jit(solution)/shard_map/ppermute | solution.py:254
  39.9 1.3 %collective-permute-start.6 = (f32[8,48,128]{2,1,0:T(8,128)S(1)}, f32[8,48,128]{2,1,0:T(8,128)S(1)}, u32[]{:S(2)}, u32[]{:S(2)}) collective-permute-start(f32[8,48,128]{2,1,0:T(8,128)S(1)} %get-tuple-element.22), channel_id=1, source_target_pairs={{8,0},{16,8},{24,16},{9,1},{17,9},{25,17},{10,2},{18,10},{26,18},{... | collective-permute-start | bytes 589832 | tf_op jit(solution)/shard_map/ppermute | solution.py:255
  41.2 0.0 collective-permute-done.south
  41.3 4.0 %collective-permute-start.2 = (f32[8,48,128]{2,1,0:T(8,128)S(1)}, f32[8,48,128]{2,1,0:T(8,128)S(1)}, u32[]{:S(2)}, u32[]{:S(2)}) collective-permute-start(f32[8,48,128]{2,1,0:T(8,128)S(1)} %get-tuple-element.18.second), channel_id=1, source_target_pairs={{0,8},{8,16},{16,24},{1,9},{9,17},{17,25},{2,10},{10,18},{18,26},{... | collective-permute-start | bytes 589832 | tf_op jit(solution)/shard_map/ppermute | solution.py:257
  45.3 1.3 %collective-permute-start.3 = (f32[8,48,128]{2,1,0:T(8,128)S(1)}, f32[8,48,128]{2,1,0:T(8,128)S(1)}, u32[]{:S(2)}, u32[]{:S(2)}) collective-permute-start(f32[8,48,128]{2,1,0:T(8,128)S(1)} %get-tuple-element.19.first), channel_id=1, source_target_pairs={{8,0},{16,8},{24,16},{9,1},{17,9},{25,17},{10,2},{18,10},{26,18},{... | collective-permute-start | bytes 589832 | tf_op jit(solution)/shard_map/ppermute | solution.py:258
  46.6 0.1 add_convert_fusion.edge
  46.7 0.5 collective-permute-done.6.high
  47.1 1.2 %coefficients.1 = (f32[32,48,128]{2,1,0:T(8,128)S(1)}, f32[32,48,128]{2,1,0:T(8,128)S(1)}, f32[32,48,128]{2,1,0:T(8,128)S(1)}, f32[32,48,128]{2,1,0:T(8,128)S(1)...) custom-call(s32[4]{0:T(128)S(1)} %add_convert_fusion.edge, ...), custom_call_target="tpu_custom_call" | custom-call | tf_op jit(solution)/shard_map/coefficients/pallas_call | solution.py:264
  48.4 1.1 inner.1.kept
  49.5 2.2 %collective-permute-done.3.high = f32[8,48,128]{2,1,0:T(8,128)S(1)} collective-permute-done((f32[8,48,128]{2,1,0:T(8,128)S(1)}, f32[8,48,128]{2,1,0:T(8,128)S(1)}, u32[]{:S(2)}, u32[]{:S(2)}) %collective-permute-start.3) | collective-permute-done | bytes 196640 | tf_op jit(solution)/shard_map/ppermute | solution.py:258
  51.7 2.8 %fine.1 = (f32[8,2,32,128]{3,2,1,0:T(8,128)}, f32[2,8,2,16,128]{4,3,2,1,0:T(8,128)S(1)}) custom-call(f32[8,48,128]{2,1,0:T(8,128)S(1)} %collective-permute-done.2.low, f32[8,48,128]{2,1,0:T(8,128)S(1)} %get-tuple-element.19.first, f32[8,48,128]{2,1,0:T(8,128)S(1)} %get-tuple-element.18.second, f32[8,48,128]{2,1,0:T(8,128)S(1)} %collective-permute-done.3.high, ...), custom_call_target="tpu_custom_call" | custom-call | tf_op jit(solution)/shard_map/fine/pallas_call | solution.py:270
  54.5 8.9 %all-to-all-start.1 = ((f32[8,2,32,128]{3,2,1,0:T(8,128)}), f32[8,2,32,128]{3,2,1,0:T(8,128)S(1)}, u32[]{:S(2)}, u32[]{:S(2)}) async-start(f32[8,2,32,128]{3,2,1,0:T(8,128)} %get-tuple-element.31), calls=%async_computation.1 | async-start | bytes 524288 | tf_op jit(solution)/shard_map/all_to_all | solution.py:199
  63.4 0.2 copy.7
  63.6 0.1 reshape.24.blocks
  63.7 0.6 copy-done.4
  64.3 0.1 reshape.25.counts
  64.4 8.5 %all-to-all-done.1.tiles = f32[8,2,32,128]{3,2,1,0:T(8,128)S(1)} async-done(((f32[8,2,32,128]{3,2,1,0:T(8,128)}), f32[8,2,32,128]{3,2,1,0:T(8,128)S(1)}, u32[]{:S(2)}, u32[]{:S(2)}) %all-to-all-start.1) | async-done | bytes 262176 | tf_op jit(solution)/shard_map/all_to_all | solution.py:199
  72.8 0.7 pick.1
  73.6 10.3 %all_to_all.21 = f32[16,2,8,128]{3,2,1,0:T(8,128)S(1)} all-to-all(f32[16,2,8,128]{3,2,1,0:T(8,128)S(1)} %pick.1), channel_id=1, replica_groups=mesh['y'=8,'zh'=2,'x'=4,'zl'=4,'c'=2] {'y'}, dimensions={0} | all-to-all | bytes 262144 | tf_op jit(solution)/shard_map/all_to_all | solution.py:199
  83.9 0.8 pack.1
  84.7 9.0 %all-to-all-start.3 = ((f32[16,2,24,128]{3,2,1,0:T(8,128)}), f32[16,2,24,128]{3,2,1,0:T(8,128)S(1)}, u32[]{:S(2)}, u32[]{:S(2)}) async-start(f32[16,2,24,128]{3,2,1,0:T(8,128)} %bitcast.12), calls=%async_computation.3 | async-start | bytes 786432 | tf_op jit(solution)/shard_map/all_to_all | solution.py:199
  93.7 0.7 constant_dynamic-slice_fusion.gain
  94.4 13.8 %all-to-all-done.3.received = f32[16,2,24,128]{3,2,1,0:T(8,128)S(1)} async-done(((f32[16,2,24,128]{3,2,1,0:T(8,128)}), f32[16,2,24,128]{3,2,1,0:T(8,128)S(1)}, u32[]{:S(2)}, u32[]{:S(2)}) %all-to-all-start.3) | async-done | bytes 393248 | tf_op jit(solution)/shard_map/all_to_all | solution.py:199
  108.2 0.8 advance.1
  (16 shorter events, 0.1 us)
Async XLA Ops:
  0.6 1.0 copy-start
  1.6 0.9 copy-start.1
  30.2 6.5 %collective-permute-start.4 = (f32[2,8,24,128]{3,2,1,0:T(8,128)S(1)}, f32[2,8,24,128]{3,2,1,0:T(8,128)S(1)}, u32[]{:S(2)}, u32[]{:S(2)}) collective-permute-start(f32[2,8,24,128]{3,2,1,0:T(8,128)S(1)} %slice.19.mine), channel_id=1, source_target_pairs={{0,1},{1,0},{2,3},{3,2},{4,5},{5,4},{6,7},{7,6},{8,9},{9,8},{10,11... | collective-permute-start | bytes 589832 | tf_op jit(solution)/shard_map/ppermute | solution.py:246
  32.2 9.0 %collective-permute-start = (f32[8,2,8,128]{3,2,1,0:T(8,128)S(1)}, f32[8,2,8,128]{3,2,1,0:T(8,128)S(1)}, u32[]{:S(2)}, u32[]{:S(2)}) collective-permute-start(f32[8,2,8,128]{3,2,1,0:T(8,128)S(1)} %get-tuple-element.35), channel_id=1, source_target_pairs={{0,64},{64,128},{128,192},{192,256},{256,320},{320,384},{384,448},... | collective-permute-start | bytes 196616 | tf_op jit(solution)/shard_map/ppermute | solution.py:242
  35.4 5.8 %collective-permute-start.1 = (f32[8,2,8,128]{3,2,1,0:T(8,128)S(1)}, f32[8,2,8,128]{3,2,1,0:T(8,128)S(1)}, u32[]{:S(2)}, u32[]{:S(2)}) collective-permute-start(f32[8,2,8,128]{3,2,1,0:T(8,128)S(1)} %get-tuple-element.34), channel_id=1, source_target_pairs={{64,0},{128,64},{192,128},{256,192},{320,256},{384,320},{448,384},... | collective-permute-start | bytes 196616 | tf_op jit(solution)/shard_map/ppermute | solution.py:243
  36.8 9.9 %collective-permute-start.5 = (f32[8,48,128]{2,1,0:T(8,128)S(1)}, f32[8,48,128]{2,1,0:T(8,128)S(1)}, u32[]{:S(2)}, u32[]{:S(2)}) collective-permute-start(f32[8,48,128]{2,1,0:T(8,128)S(1)} %get-tuple-element.20), channel_id=1, source_target_pairs={{0,8},{8,16},{16,24},{1,9},{9,17},{17,25},{2,10},{10,18},{18,26},{... | collective-permute-start | bytes 589832 | tf_op jit(solution)/shard_map/ppermute | solution.py:254
  39.9 7.2 %collective-permute-start.6 = (f32[8,48,128]{2,1,0:T(8,128)S(1)}, f32[8,48,128]{2,1,0:T(8,128)S(1)}, u32[]{:S(2)}, u32[]{:S(2)}) collective-permute-start(f32[8,48,128]{2,1,0:T(8,128)S(1)} %get-tuple-element.22), channel_id=1, source_target_pairs={{8,0},{16,8},{24,16},{9,1},{17,9},{25,17},{10,2},{18,10},{26,18},{... | collective-permute-start | bytes 589832 | tf_op jit(solution)/shard_map/ppermute | solution.py:255
  41.3 8.2 %collective-permute-start.2 = (f32[8,48,128]{2,1,0:T(8,128)S(1)}, f32[8,48,128]{2,1,0:T(8,128)S(1)}, u32[]{:S(2)}, u32[]{:S(2)}) collective-permute-start(f32[8,48,128]{2,1,0:T(8,128)S(1)} %get-tuple-element.18.second), channel_id=1, source_target_pairs={{0,8},{8,16},{16,24},{1,9},{9,17},{17,25},{2,10},{10,18},{18,26},{... | collective-permute-start | bytes 589832 | tf_op jit(solution)/shard_map/ppermute | solution.py:257
  45.3 6.4 %collective-permute-start.3 = (f32[8,48,128]{2,1,0:T(8,128)S(1)}, f32[8,48,128]{2,1,0:T(8,128)S(1)}, u32[]{:S(2)}, u32[]{:S(2)}) collective-permute-start(f32[8,48,128]{2,1,0:T(8,128)S(1)} %get-tuple-element.19.first), channel_id=1, source_target_pairs={{8,0},{16,8},{24,16},{9,1},{17,9},{25,17},{10,2},{18,10},{26,18},{... | collective-permute-start | bytes 589832 | tf_op jit(solution)/shard_map/ppermute | solution.py:258
  54.5 9.0 %copy-start.3 = (s32[16,16,2]{1,2,0:T(2,128)S(1)}, s32[16,16,2]{1,2,0:T(2,128)}, u32[]{:S(2)}) copy-start(s32[16,16,2]{1,2,0:T(2,128)} %param.8) | copy-start | bytes 6148
  54.5 18.4 %all-to-all-start.1 = ((f32[8,2,32,128]{3,2,1,0:T(8,128)}), f32[8,2,32,128]{3,2,1,0:T(8,128)S(1)}, u32[]{:S(2)}, u32[]{:S(2)}) async-start(f32[8,2,32,128]{3,2,1,0:T(8,128)} %get-tuple-element.31), calls=%async_computation.1 | async-start | bytes 524288 | tf_op jit(solution)/shard_map/all_to_all | solution.py:199
  63.6 0.7 copy-start.4
  84.7 23.6 %copy-start.2 = (f32[16,2,16,128]{3,2,1,0:T(8,128)S(1)}, f32[16,2,16,128]{3,2,1,0:T(8,128)}, u32[]{:S(2)}) copy-start(f32[16,2,16,128]{3,2,1,0:T(8,128)} %states.3) | copy-start | bytes 786436
  84.7 23.5 %all-to-all-start.3 = ((f32[16,2,24,128]{3,2,1,0:T(8,128)}), f32[16,2,24,128]{3,2,1,0:T(8,128)S(1)}, u32[]{:S(2)}, u32[]{:S(2)}) async-start(f32[16,2,24,128]{3,2,1,0:T(8,128)} %bitcast.12), calls=%async_computation.3 | async-start | bytes 786432 | tf_op jit(solution)/shard_map/all_to_all | solution.py:199

commit v11 on v9

--- a/solution.py
+++ b/solution.py
@@ -229,9 +229,10 @@
         load_kernel, "load", [(slices, packed, lanes)], [VMEM] * 2
     )(states, kappa)
     own = exchange(load, RING).reshape(2, half, packed, lanes)
-    ends_of = own[:, :, :layers].reshape(2, half, thick, own_rows, lanes)
-    south = lax.ppermute(ends_of[1, :, :, own_rows - FINE :], "y", y_up)
-    north = lax.ppermute(ends_of[0, :, :, :FINE], "y", y_down)
+    upper = [own[1, :, r - FINE : r] for r in (own_rows, 2 * own_rows)]
+    lower = [own[0, :, r : r + FINE] for r in (0, own_rows)]
+    south = lax.ppermute(jnp.stack(upper, axis=1), "y", y_up)
+    north = lax.ppermute(jnp.stack(lower, axis=1), "y", y_down)
     part = (FINE, wide, lanes)
     mine = own[:, :, layers:]
     other = lax.ppermute(mine, "c", [(0, 1), (1, 0)])

time: 109 us -> 107 us (0.982)
  starting transfers between devices: 33.9 us -> 32.7 us
    all_to_all x2, starting transfers between devices: 17.8 us -> 15.8 us  [exchange(): return lax.all_to_all(value, axes, 0, 0, tiled=True)]
where the time goes in v11:
time: 107 us
  blocking collectives  37.9 us (35%)
  starting transfers between devices  32.7 us (31%)
  waiting for transfers between devices  25.7 us (24%)
  Pallas kernels  7.51 us (7%)
  local copies, waits for them, and re-layouts  1.99 us (2%)
    all_to_all x2, blocking collectives, exchange(): return lax.all_to_all(value, axes, 0, 0, tiled=True)  37.9 us
    all_to_all x2, waiting for transfers between devices, exchange(): return lax.all_to_all(value, axes, 0, 0, tiled=True)  23 us
    all_to_all x2, starting transfers between devices, exchange(): return lax.all_to_all(value, axes, 0, 0, tiled=True)  15.8 us
    ppermute x1, starting transfers between devices, body(): low = lax.ppermute(second, 'x', x_up)  4 us
    ppermute x1, starting transfers between devices, body(): south = lax.ppermute(jnp.stack(upper, axis=1), 'y', y_up)  3.99 us
    ppermute x1, starting transfers between devices, body(): k_low = lax.ppermute(k_second, 'x', x_up)  3.13 us
    pallas_call x1, Pallas kernels, body(): call(fine_kernel, 'fine', [(ny, deep // ny, tile_rows, lanes), (2, half,...  2.76 us
    ppermute x1, waiting for transfers between devices, body(): high = lax.ppermute(first, 'x', x_down)  2.5 us
  transfers between devices with their start and end apart: 9, of which 4 were waited for; matrix products, arithmetic and copies ran while one was open for 0% of the time, Pallas kernels for 2%

profile of v11, /device:TPU:1, one launch (start us, length us, event | category | flops | bytes accessed | tf_op | source)
XLA Modules:
  0.0 106.8 jit_solution(10708400268347298386)
XLA Ops:
  0.6 0.0 copy-start
  0.7 0.8 pad_dynamic-slice_fusion.kappa
  1.5 0.2 copy-done.1
  1.7 27.6 %all_to_all.20 = f32[16,56,128]{2,1,0:T(8,128)S(1)} all-to-all(f32[16,56,128]{2,1,0:T(8,128)S(1)} %load.1), channel_id=1, replica_groups=mesh['y'=8,'zh'=2,'x'=4,'zl'=4,'c'=2] {'zh','zl','c'}, dimensions={0} | all-to-all | bytes 917504 | tf_op jit(solution)/shard_map/all_to_all | solution.py:190
  29.3 1.9 %collective-permute-start.4 = (f32[2,8,24,128]{3,2,1,0:T(8,128)S(1)}, f32[2,8,24,128]{3,2,1,0:T(8,128)S(1)}, u32[]{:S(2)}, u32[]{:S(2)}) collective-permute-start(f32[2,8,24,128]{3,2,1,0:T(8,128)S(1)} %slice.24.mine), channel_id=1, source_target_pairs={{0,1},{1,0},{2,3},{3,2},{4,5},{5,4},{6,7},{7,6},{8,9},{9,8},{10,11... | collective-permute-start | bytes 589832 | tf_op jit(solution)/shard_map/ppermute | solution.py:238
  31.3 1.3 %collective-permute-start.1 = (f32[8,2,8,128]{3,2,0,1:T(8,128)S(1)}, f32[8,2,8,128]{3,2,0,1:T(8,128)S(1)}, u32[]{:S(2)}, u32[]{:S(2)}) collective-permute-start(f32[8,2,8,128]{3,2,0,1:T(8,128)S(1)} %pad_maximum_fusion.1), channel_id=1, source_target_pairs={{64,0},{128,64},{192,128},{256,192},{320,256},{384,320},{448,384},... | collective-permute-start | bytes 196616 | tf_op jit(solution)/shard_map/ppermute | solution.py:235
  32.6 4.0 %collective-permute-start = (f32[8,2,8,128]{3,2,0,1:T(8,128)S(1)}, f32[8,2,8,128]{3,2,0,1:T(8,128)S(1)}, u32[]{:S(2)}, u32[]{:S(2)}) collective-permute-start(f32[8,2,8,128]{3,2,0,1:T(8,128)S(1)} %pad_maximum_fusion), channel_id=1, source_target_pairs={{0,64},{64,128},{128,192},{192,256},{256,320},{320,384},{384,448},... | collective-permute-start | bytes 196616 | tf_op jit(solution)/shard_map/ppermute | solution.py:234
  36.6 0.1 gather.1
  36.7 3.1 %collective-permute-start.5 = (f32[8,48,128]{2,1,0:T(8,128)S(1)}, f32[8,48,128]{2,1,0:T(8,128)S(1)}, u32[]{:S(2)}, u32[]{:S(2)}) collective-permute-start(f32[8,48,128]{2,1,0:T(8,128)S(1)} %get-tuple-element.20), channel_id=1, source_target_pairs={{0,8},{8,16},{16,24},{1,9},{9,17},{17,25},{2,10},{10,18},{18,26},{... | collective-permute-start | bytes 589832 | tf_op jit(solution)/shard_map/ppermute | solution.py:246
  39.8 1.3 %collective-permute-start.6 = (f32[8,48,128]{2,1,0:T(8,128)S(1)}, f32[8,48,128]{2,1,0:T(8,128)S(1)}, u32[]{:S(2)}, u32[]{:S(2)}) collective-permute-start(f32[8,48,128]{2,1,0:T(8,128)S(1)} %get-tuple-element.22), channel_id=1, source_target_pairs={{8,0},{16,8},{24,16},{9,1},{17,9},{25,17},{10,2},{18,10},{26,18},{... | collective-permute-start | bytes 589832 | tf_op jit(solution)/shard_map/ppermute | solution.py:247
  41.1 0.0 collective-permute-done.1
  41.1 0.0 collective-permute-done
  41.2 4.0 %collective-permute-start.2 = (f32[8,48,128]{2,1,0:T(8,128)S(1)}, f32[8,48,128]{2,1,0:T(8,128)S(1)}, u32[]{:S(2)}, u32[]{:S(2)}) collective-permute-start(f32[8,48,128]{2,1,0:T(8,128)S(1)} %get-tuple-element.18.second), channel_id=1, source_target_pairs={{0,8},{8,16},{16,24},{1,9},{9,17},{17,25},{2,10},{10,18},{18,26},{... | collective-permute-start | bytes 589832 | tf_op jit(solution)/shard_map/ppermute | solution.py:249
  45.2 1.3 %collective-permute-start.3 = (f32[8,48,128]{2,1,0:T(8,128)S(1)}, f32[8,48,128]{2,1,0:T(8,128)S(1)}, u32[]{:S(2)}, u32[]{:S(2)}) collective-permute-start(f32[8,48,128]{2,1,0:T(8,128)S(1)} %get-tuple-element.19.first), channel_id=1, source_target_pairs={{8,0},{16,8},{24,16},{9,1},{17,9},{25,17},{10,2},{18,10},{26,18},{... | collective-permute-start | bytes 589832 | tf_op jit(solution)/shard_map/ppermute | solution.py:250
  46.5 0.1 add_convert_fusion.edge
  46.6 0.2 collective-permute-done.6.high
  46.8 1.2 %coefficients.1 = (f32[32,48,128]{2,1,0:T(8,128)S(1)}, f32[32,48,128]{2,1,0:T(8,128)S(1)}, f32[32,48,128]{2,1,0:T(8,128)S(1)}, f32[32,48,128]{2,1,0:T(8,128)S(1)...) custom-call(s32[4]{0:T(128)S(1)} %add_convert_fusion.edge, ...), custom_call_target="tpu_custom_call" | custom-call | tf_op jit(solution)/shard_map/coefficients/pallas_call | solution.py:256
  48.0 1.1 %inner.1.kept = f32[7,4,48,128]{3,2,1,0:T(8,128)S(1)} custom-call(f32[8,48,128]{2,1,0:T(8,128)S(1)} %get-tuple-element.19.first, f32[8,48,128]{2,1,0:T(8,128)S(1)} %get-tuple-element.18.second, f32[32,48,128]{2,1,0:T(8,128)S(1)} %get-tuple-element.23.refs_0_, f32[32,48,128]{2,1,0:T(8,128)S(1)} %get-tuple-element.24.refs_1_, ...), custom_call_target="tpu_custom_call" | custom-call | tf_op jit(solution)/shard_map/inner/pallas_call | solution.py:259
  49.1 2.5 %collective-permute-done.3.high = f32[8,48,128]{2,1,0:T(8,128)S(1)} collective-permute-done((f32[8,48,128]{2,1,0:T(8,128)S(1)}, f32[8,48,128]{2,1,0:T(8,128)S(1)}, u32[]{:S(2)}, u32[]{:S(2)}) %collective-permute-start.3) | collective-permute-done | bytes 196640 | tf_op jit(solution)/shard_map/ppermute | solution.py:250
  51.6 2.8 %fine.1 = (f32[8,2,32,128]{3,2,1,0:T(8,128)}, f32[2,8,2,16,128]{4,3,2,1,0:T(8,128)S(1)}) custom-call(f32[8,48,128]{2,1,0:T(8,128)S(1)} %collective-permute-done.2.low, f32[8,48,128]{2,1,0:T(8,128)S(1)} %get-tuple-element.19.first, f32[8,48,128]{2,1,0:T(8,128)S(1)} %get-tuple-element.18.second, f32[8,48,128]{2,1,0:T(8,128)S(1)} %collective-permute-done.3.high, ...), custom_call_target="tpu_custom_call" | custom-call | tf_op jit(solution)/shard_map/fine/pallas_call | solution.py:262
  54.4 7.0 %all-to-all-start.1 = ((f32[8,2,32,128]{3,2,1,0:T(8,128)}), f32[8,2,32,128]{3,2,1,0:T(8,128)S(1)}, u32[]{:S(2)}, u32[]{:S(2)}) async-start(f32[8,2,32,128]{3,2,1,0:T(8,128)} %get-tuple-element.31), calls=%async_computation.1 | async-start | bytes 524288 | tf_op jit(solution)/shard_map/all_to_all | solution.py:190
  61.3 0.2 copy.11
  61.5 0.1 reshape.20.blocks
  61.7 0.6 copy-done.3
  62.2 0.1 reshape.21.counts
  62.3 8.5 %all-to-all-done.1.tiles = f32[8,2,32,128]{3,2,1,0:T(8,128)S(1)} async-done(((f32[8,2,32,128]{3,2,1,0:T(8,128)}), f32[8,2,32,128]{3,2,1,0:T(8,128)S(1)}, u32[]{:S(2)}, u32[]{:S(2)}) %all-to-all-start.1) | async-done | bytes 262176 | tf_op jit(solution)/shard_map/all_to_all | solution.py:190
  70.8 0.7 pick.1
  71.5 10.3 %all_to_all.21 = f32[16,2,8,128]{3,2,1,0:T(8,128)S(1)} all-to-all(f32[16,2,8,128]{3,2,1,0:T(8,128)S(1)} %pick.1), channel_id=1, replica_groups=mesh['y'=8,'zh'=2,'x'=4,'zl'=4,'c'=2] {'y'}, dimensions={0} | all-to-all | bytes 262144 | tf_op jit(solution)/shard_map/all_to_all | solution.py:190
  81.8 0.8 pack.1
  82.6 8.9 %all-to-all-start.3 = ((f32[16,2,24,128]{3,2,1,0:T(8,128)}), f32[16,2,24,128]{3,2,1,0:T(8,128)S(1)}, u32[]{:S(2)}, u32[]{:S(2)}) async-start(f32[16,2,24,128]{3,2,1,0:T(8,128)} %bitcast.12), calls=%async_computation.3 | async-start | bytes 786432 | tf_op jit(solution)/shard_map/all_to_all | solution.py:190
  91.5 14.5 %all-to-all-done.3.received = f32[16,2,24,128]{3,2,1,0:T(8,128)S(1)} async-done(((f32[16,2,24,128]{3,2,1,0:T(8,128)}), f32[16,2,24,128]{3,2,1,0:T(8,128)S(1)}, u32[]{:S(2)}, u32[]{:S(2)}) %all-to-all-start.3) | async-done | bytes 393248 | tf_op jit(solution)/shard_map/all_to_all | solution.py:190
  106.0 0.8 advance.1
  (17 shorter events, 0.1 us)
Async XLA Ops:
  0.6 90.8 %copy-start = (f32[2,256,128]{2,1,0:T(8,128)S(1)}, f32[2,256,128]{2,1,0:T(8,128)}, u32[]{:S(2)}) copy-start(f32[2,256,128]{2,1,0:T(8,128)} %param.7) | copy-start | bytes 786436
  0.6 1.0 copy-start.1
  29.3 7.3 %collective-permute-start.4 = (f32[2,8,24,128]{3,2,1,0:T(8,128)S(1)}, f32[2,8,24,128]{3,2,1,0:T(8,128)S(1)}, u32[]{:S(2)}, u32[]{:S(2)}) collective-permute-start(f32[2,8,24,128]{3,2,1,0:T(8,128)S(1)} %slice.24.mine), channel_id=1, source_target_pairs={{0,1},{1,0},{2,3},{3,2},{4,5},{5,4},{6,7},{7,6},{8,9},{9,8},{10,11... | collective-permute-start | bytes 589832 | tf_op jit(solution)/shard_map/ppermute | solution.py:238
  31.3 9.8 %collective-permute-start.1 = (f32[8,2,8,128]{3,2,0,1:T(8,128)S(1)}, f32[8,2,8,128]{3,2,0,1:T(8,128)S(1)}, u32[]{:S(2)}, u32[]{:S(2)}) collective-permute-start(f32[8,2,8,128]{3,2,0,1:T(8,128)S(1)} %pad_maximum_fusion.1), channel_id=1, source_target_pairs={{64,0},{128,64},{192,128},{256,192},{320,256},{384,320},{448,384},... | collective-permute-start | bytes 196616 | tf_op jit(solution)/shard_map/ppermute | solution.py:235
  32.6 8.6 %collective-permute-start = (f32[8,2,8,128]{3,2,0,1:T(8,128)S(1)}, f32[8,2,8,128]{3,2,0,1:T(8,128)S(1)}, u32[]{:S(2)}, u32[]{:S(2)}) collective-permute-start(f32[8,2,8,128]{3,2,0,1:T(8,128)S(1)} %pad_maximum_fusion), channel_id=1, source_target_pairs={{0,64},{64,128},{128,192},{192,256},{256,320},{320,384},{384,448},... | collective-permute-start | bytes 196616 | tf_op jit(solution)/shard_map/ppermute | solution.py:234
  36.7 9.9 %collective-permute-start.5 = (f32[8,48,128]{2,1,0:T(8,128)S(1)}, f32[8,48,128]{2,1,0:T(8,128)S(1)}, u32[]{:S(2)}, u32[]{:S(2)}) collective-permute-start(f32[8,48,128]{2,1,0:T(8,128)S(1)} %get-tuple-element.20), channel_id=1, source_target_pairs={{0,8},{8,16},{16,24},{1,9},{9,17},{17,25},{2,10},{10,18},{18,26},{... | collective-permute-start | bytes 589832 | tf_op jit(solution)/shard_map/ppermute | solution.py:246
  39.8 7.0 %collective-permute-start.6 = (f32[8,48,128]{2,1,0:T(8,128)S(1)}, f32[8,48,128]{2,1,0:T(8,128)S(1)}, u32[]{:S(2)}, u32[]{:S(2)}) collective-permute-start(f32[8,48,128]{2,1,0:T(8,128)S(1)} %get-tuple-element.22), channel_id=1, source_target_pairs={{8,0},{16,8},{24,16},{9,1},{17,9},{25,17},{10,2},{18,10},{26,18},{... | collective-permute-start | bytes 589832 | tf_op jit(solution)/shard_map/ppermute | solution.py:247
  41.2 7.9 %collective-permute-start.2 = (f32[8,48,128]{2,1,0:T(8,128)S(1)}, f32[8,48,128]{2,1,0:T(8,128)S(1)}, u32[]{:S(2)}, u32[]{:S(2)}) collective-permute-start(f32[8,48,128]{2,1,0:T(8,128)S(1)} %get-tuple-element.18.second), channel_id=1, source_target_pairs={{0,8},{8,16},{16,24},{1,9},{9,17},{17,25},{2,10},{10,18},{18,26},{... | collective-permute-start | bytes 589832 | tf_op jit(solution)/shard_map/ppermute | solution.py:249
  45.2 6.4 %collective-permute-start.3 = (f32[8,48,128]{2,1,0:T(8,128)S(1)}, f32[8,48,128]{2,1,0:T(8,128)S(1)}, u32[]{:S(2)}, u32[]{:S(2)}) collective-permute-start(f32[8,48,128]{2,1,0:T(8,128)S(1)} %get-tuple-element.19.first), channel_id=1, source_target_pairs={{8,0},{16,8},{24,16},{9,1},{17,9},{25,17},{10,2},{18,10},{26,18},{... | collective-permute-start | bytes 589832 | tf_op jit(solution)/shard_map/ppermute | solution.py:250
  54.4 7.0 %copy-start.2 = (s32[16,16,2]{1,2,0:T(2,128)S(1)}, s32[16,16,2]{1,2,0:T(2,128)}, u32[]{:S(2)}) copy-start(s32[16,16,2]{1,2,0:T(2,128)} %param.8) | copy-start | bytes 6148
  54.4 16.4 %all-to-all-start.1 = ((f32[8,2,32,128]{3,2,1,0:T(8,128)}), f32[8,2,32,128]{3,2,1,0:T(8,128)S(1)}, u32[]{:S(2)}, u32[]{:S(2)}) async-start(f32[8,2,32,128]{3,2,1,0:T(8,128)} %get-tuple-element.31), calls=%async_computation.1 | async-start | bytes 524288 | tf_op jit(solution)/shard_map/all_to_all | solution.py:190
  61.5 0.7 copy-start.3
  82.6 23.4 %all-to-all-start.3 = ((f32[16,2,24,128]{3,2,1,0:T(8,128)}), f32[16,2,24,128]{3,2,1,0:T(8,128)S(1)}, u32[]{:S(2)}, u32[]{:S(2)}) async-start(f32[16,2,24,128]{3,2,1,0:T(8,128)} %bitcast.12), calls=%async_computation.3 | async-start | bytes 786432 | tf_op jit(solution)/shard_map/all_to_all | solution.py:190
